TPU v7x, 128 devices: a whole 4x4x4 slice. The times are simulated.
128 devices in a mesh: shot: 2 (over core), gx: 8 (over y_lo, x), gy: 8 (over z, y_hi).
Axes of the slice: x: 4, y: 4 (y_hi: 2, y_lo: 2; y = y_hi * 2 + y_lo), z: 4, core: 2. Of those that a mesh axis runs over, the one named last changes fastest.
Arguments:
- adjoint_prev: float32 [2, 256, 256, 512], P('shot', 'gx', 'gy'), may hold values from -6 to 6
- adjoint_now: float32 [2, 256, 256, 512], P('shot', 'gx', 'gy'), may hold values from -6 to 6
- speed_term: float32 [2, 256, 256, 512], P('shot', 'gx', 'gy'), may hold values from 0.05 to 0.25
- adjoint_source: float32 [2, 2, 256, 256, 512], P('shot', None, 'gx', 'gy'), may hold values from -6 to 6
- forward_accel: float32 [2, 2, 256, 256, 512], P('shot', None, 'gx', 'gy'), may hold values from -6 to 6
- footprint: int32 [2, 8, 8, 512], P('shot', 'gx', 'gy'), may hold values from 0 to 16383, as said below
- live_counts: int32 [2, 8, 8], P('shot', 'gx', 'gy'), may hold values from 256 to 512, as said below
Outputs:
- level_one: float32 [2, 256, 256, 512], P('shot', 'gx', 'gy')
- level_two: float32 [2, 256, 256, 512], P('shot', 'gx', 'gy')
- model_gradient: float32 [16384, 1024], P(('shot', 'gx', 'gy'))
Inputs may be any that keep to these rules, and one draw needn't show every extreme that they name: `footprint`: among the 512 entries of one device's list, each owner device o (entries with id // 128 == o, owners numbered over shot, gx, gy in that order) appears exactly 4 times; live and dead entries alike. Entries at positions from live_counts on are dead and contribute nothing.
All inputs are finite; a program needn't handle non-finite values.
Results may differ from a plain program's by a relative error of at most 0.0029.
Values may be sent and summed in bfloat16 or wider, within the bound.
No kernel may reach another device: no remote copies, remote signals or barrier semaphores. Data moves between devices by JAX's collectives and lax.ppermute only.
A program may use at most 128 MiB of HBM per device.

v0:
```python
import jax
import jax.numpy as jnp
from jax import lax
from jax.sharding import PartitionSpec as P

TX = 8
TY = 8
TZ = 16
TILES_DEV = 128


CENTER = -205.0 / 72.0
COEFFS = (8.0 / 5.0, -1.0 / 5.0, 8.0 / 315.0, -1.0 / 560.0)


def padded_2(block, sides, width):
    for axis, dim in sides:
        count = lax.axis_size(axis)
        forward = [(i, i + 1) for i in range(count - 1)]
        backward = [(target, source) for source, target in forward]
        low = lax.ppermute(
            lax.slice_in_dim(block, block.shape[dim] - width, None, axis=dim), axis, forward
        )
        high = lax.ppermute(lax.slice_in_dim(block, 0, width, axis=dim), axis, backward)
        block = jnp.concatenate([low, block, high], axis=dim)
    return block


def stencil(extended):
    cells_wide = extended.shape[0] - 8
    cells_long = extended.shape[1] - 8
    cells_deep = extended.shape[2]
    padded = jnp.pad(extended, ((0, 0), (0, 0), (4, 4)))

    def window(first_shift, second_shift, third_shift):
        return padded[
            4 + first_shift : 4 + first_shift + cells_wide,
            4 + second_shift : 4 + second_shift + cells_long,
            4 + third_shift : 4 + third_shift + cells_deep,
        ]

    middle = window(0, 0, 0)
    summed = 3.0 * CENTER * middle
    for offset, weight in enumerate(COEFFS, 1):
        nearby = window(offset, 0, 0) + window(-offset, 0, 0)
        nearby = nearby + window(0, offset, 0) + window(0, -offset, 0)
        nearby = nearby + window(0, 0, offset) + window(0, 0, -offset)
        summed = summed + weight * nearby
    return (summed, middle)


def advance(earlier, current, velocity, source):
    extended = padded_2(current, (("gx", 0), ("gy", 1)), 4)
    laplace_term, middle = stencil(extended)
    return 2.0 * current - earlier + velocity * laplace_term + source


def per_device(
    adjoint_prev, adjoint_now, speed_term, adjoint_source, forward_accel, footprint, live_counts
):
    earlier = adjoint_prev[0]
    current = adjoint_now[0]
    velocity = speed_term[0]
    sources = adjoint_source[0]
    forward = forward_accel[0]
    stepped_one = advance(earlier, current, velocity, sources[0])
    stepped_two = advance(current, stepped_one, velocity, sources[1])
    imaging = forward[0] * stepped_one + forward[1] * stepped_two
    cells_wide, cells_long, cells_deep = imaging.shape
    blocks = imaging.reshape(cells_wide // TX, TX, cells_long // TY, TY, cells_deep // TZ, TZ)
    blocks = blocks.transpose(0, 2, 4, 1, 3, 5).reshape(-1, TX * TY * TZ)
    slot_count = blocks.shape[0]
    listed = footprint.reshape(slot_count)
    active = jnp.arange(slot_count, dtype=jnp.int32) < live_counts.reshape(())
    blocks = jnp.where(active[:, None], blocks, 0.0).astype(jnp.bfloat16)
    owners = lax.axis_size("shot") * lax.axis_size("gx") * lax.axis_size("gy")
    capacity = slot_count // owners
    target = listed // TILES_DEV
    local_ids = jnp.where(active, listed % TILES_DEV, -1)
    ordering = jnp.argsort(target, stable=True)
    outgoing = blocks[ordering].reshape(owners, capacity, -1)
    sent_ids = local_ids[ordering].reshape(owners, capacity)
    incoming, arrived_ids = (
        lax.all_to_all(outgoing, ("shot", "gx", "gy"), split_axis=0, concat_axis=0, tiled=True),
        lax.all_to_all(sent_ids, ("shot", "gx", "gy"), split_axis=0, concat_axis=0, tiled=True),
    )
    flat_ids = arrived_ids.reshape(-1)
    arrived = incoming.reshape(flat_ids.shape[0], -1)
    onehot = (jnp.arange(TILES_DEV, dtype=jnp.int32)[:, None] == flat_ids[None, :]).astype(
        jnp.bfloat16
    )
    gradient = jnp.dot(onehot, arrived, preferred_element_type=jnp.float32)
    return (stepped_one[None], stepped_two[None], gradient)


def solution(mesh):
    return jax.shard_map(
        per_device,
        mesh=mesh,
        in_specs=(
            P("shot", "gx", "gy", None),
            P("shot", "gx", "gy", None),
            P("shot", "gx", "gy", None),
            P("shot", None, "gx", "gy", None),
            P("shot", None, "gx", "gy", None),
            P("shot", "gx", "gy", None),
            P("shot", "gx", "gy"),
        ),
        out_specs=(
            P("shot", "gx", "gy", None),
            P("shot", "gx", "gy", None),
            P(("shot", "gx", "gy"), None),
        ),
        check_vma=False,
    )
```

profile of v0, /device:TPU:1, one launch (start us, length us, event | category | flops | bytes accessed | tf_op | source)
XLA Modules:
  0.0 185.8 jit_solution(17350390518750344897)
XLA Ops:
  0.6 1.2 slice_bitcast_fusion.1
  1.9 4.0 %collective-permute-start.1 = (f32[4,32,512]{2,1,0:T(8,128)S(1)}, f32[4,32,512]{2,1,0:T(8,128)S(1)}, u32[]{:S(2)}, u32[]{:S(2)}) collective-permute-start(f32[4,32,512]{2,1,0:T(8,128)S(1)} %get-tuple-element.18), channel_id=1, source_target_pairs={{0,8},{8,16},{16,24},{24,32},{32,40},{40,48},{48,56},{1,9},{9,17},... | collective-permute-start | bytes 786440 | tf_op jit(solution)/shard_map/ppermute | solution.py:21
  5.8 1.3 collective-permute-start
  7.1 3.6 %collective-permute-done.1 = f32[4,32,512]{2,1,0:T(8,128)S(1)} collective-permute-done((f32[4,32,512]{2,1,0:T(8,128)S(1)}, f32[4,32,512]{2,1,0:T(8,128)S(1)}, u32[]{:S(2)}, u32[]{:S(2)}) %collective-permute-start.1) | collective-permute-done | bytes 262176 | tf_op jit(solution)/shard_map/ppermute | solution.py:21
  10.8 3.8 %collective-permute-done = f32[4,32,512]{2,1,0:T(8,128)S(1)} collective-permute-done((f32[4,32,512]{2,1,0:T(8,128)S(1)}, f32[4,32,512]{2,1,0:T(8,128)S(1)}, u32[]{:S(2)}, u32[]{:S(2)}) %collective-permute-start) | collective-permute-done | bytes 262176 | tf_op jit(solution)/shard_map/ppermute | solution.py:24
  14.6 1.3 pad_maximum_fusion.9
  15.9 1.3 collective-permute-start.2
  17.2 5.5 %collective-permute-start.3 = (f32[40,4,512]{2,1,0:T(4,128)S(1)}, f32[40,4,512]{2,1,0:T(4,128)S(1)}, u32[]{:S(2)}, u32[]{:S(2)}) collective-permute-start(f32[40,4,512]{2,1,0:T(4,128)S(1)} %get-tuple-element.13), channel_id=1, source_target_pairs={{0,1},{1,2},{2,3},{3,4},{4,5},{5,6},{6,7},{8,9},{9,10},{10,11},{11... | collective-permute-start | bytes 983048 | tf_op jit(solution)/shard_map/ppermute | solution.py:21
  22.8 3.9 %collective-permute-done.2 = f32[40,4,512]{2,1,0:T(4,128)S(1)} collective-permute-done((f32[40,4,512]{2,1,0:T(4,128)S(1)}, f32[40,4,512]{2,1,0:T(4,128)S(1)}, u32[]{:S(2)}, u32[]{:S(2)}) %collective-permute-start.2) | collective-permute-done | bytes 327712 | tf_op jit(solution)/shard_map/ppermute | solution.py:24
  26.7 0.9 collective-permute-done.3
  27.6 4.2 %select_maximum_fusion.4 = f32[40,40,520]{2,1,0:T(8,128)S(1)} fusion(f32[40,4,512]{2,1,0:T(4,128)S(1)} %collective-permute-done.2, f32[40,4,512]{2,1,0:T(4,128)S(1)} %collective-permute-done.3, f32[4,32,512]{2,1,0:T(8,128)S(1)} %collective-permute-done, f32[32,32,512]{2,1,0:T(8,128)S(1)} %bitcast.40, f32[4,32,512]{2,1,0:T(8,128)S(1)} %collective-permute-done.1), kind=kLoop, calls=%fused_computation.20 | loop fusion | flops 9984000 | bytes 6604800 | tf_op jit(solution)/shard_map/concatenate | solution.py:25
  31.8 2.3 %pad_maximum_fusion = (f32[40,36,512]{2,1,0:T(8,128)S(1)}, f32[40,36,512]{2,1,0:T(8,128)}) fusion(f32[40,4,512]{2,1,0:T(4,128)S(1)} %collective-permute-done.2, f32[4,32,512]{2,1,0:T(8,128)S(1)} %collective-permute-done, f32[32,32,512]{2,1,0:T(8,128)S(1)} %bitcast.41, f32[4,32,512]{2,1,0:T(8,128)S(1)} %collective-permute-done.1, ...), kind=kLoop, calls=%fused_computation.25 | loop fusion | flops 4423680 | bytes 9175040 | tf_op jit(solution)/shard_map/concatenate | solution.py:25
  34.1 11.0 %fusion.43 = f32[32,32,512]{2,1,0:T(8,128)S(1)} fusion(f32[32,32,512]{2,1,0:T(8,128)S(1)} %bitcast.42, f32[4,32,512]{2,1,0:T(8,128)S(1)} %collective-permute-done.1, f32[4,32,512]{2,1,0:T(8,128)S(1)} %collective-permute-done, f32[40,40,520]{2,1,0:T(8,128)S(1)} %select_maximum_fusion.4, f32[40,36,512]{2,1,0:T(8,128)} %get-tuple-element.12, ...), kind=kLoop, calls=%fused_computation.83 | loop fusion | flops 22020096 | bytes 44564480 | tf_op jit(solution)/shard_map/add | solution.py:55
  45.1 1.3 collective-permute-start.4
  46.4 4.0 %collective-permute-start.5 = (f32[4,32,512]{2,1,0:T(8,128)S(1)}, f32[4,32,512]{2,1,0:T(8,128)S(1)}, u32[]{:S(2)}, u32[]{:S(2)}) collective-permute-start(f32[4,32,512]{2,1,0:T(8,128)S(1)} %get-tuple-element.15), channel_id=1, source_target_pairs={{0,8},{8,16},{16,24},{24,32},{32,40},{40,48},{48,56},{1,9},{9,17},... | collective-permute-start | bytes 786440 | tf_op jit(solution)/shard_map/ppermute | solution.py:21
  51.1 3.8 %sort.17 = (s32[512]{0:T(512)}, s32[512]{0:T(512)S(1)}) sort(s32[512]{0:T(512)S(1)} %get-tuple-element.20, s32[512]{0:T(512)S(1)} %iota.14), dimensions={0}, to_apply=%region_0.1 | sort | flops 4608 | bytes 8192 | tf_op jit(solution)/shard_map/jit(argsort)/sort | solution.py:80
  54.9 2.2 %pad_maximum_fusion.6 = (f32[40,4,512]{2,1,0:T(4,128)}, f32[40,4,512]{2,1,0:T(4,128)}) fusion(f32[4,32,512]{2,1,0:T(8,128)S(1)} %collective-permute-done.4, f32[32,32,512]{2,1,0:T(8,128)} %copy-done.1, f32[4,32,512]{2,1,0:T(8,128)S(1)} %collective-permute-done.5), kind=kLoop, calls=%fused_computation.124 | loop fusion | flops 327680 | bytes 3276800 | tf_op jit(solution)/shard_map/concatenate | solution.py:25
  57.1 1.3 collective-permute-start.6
  58.4 8.9 %collective-permute-start.7 = (f32[40,4,512]{2,1,0:T(4,128)}, f32[40,4,512]{2,1,0:T(4,128)S(1)}, u32[]{:S(2)}, u32[]{:S(2)}) collective-permute-start(f32[40,4,512]{2,1,0:T(4,128)} %get-tuple-element.9), channel_id=1, source_target_pairs={{0,1},{1,2},{2,3},{3,4},{4,5},{5,6},{6,7},{8,9},{9,10},{10,11},{11... | collective-permute-start | bytes 983048 | tf_op jit(solution)/shard_map/ppermute | solution.py:21
  67.4 3.5 %gather_fusion = s32[512]{0:T(512)S(1)} fusion(s32[512]{0:T(512)S(1)} %get-tuple-element.19, s32[1024]{0:T(1024)S(1)} %pad_clamp_fusion), kind=kCustom, calls=%fused_computation | custom fusion | bytes 6144 | tf_op jit(solution)/shard_map/gather | solution.py:82
  71.6 21.0 %all-to-all-start = ((s32[128,1,4]{2,1,0:T(1,128)}), s32[128,1,4]{2,1,0:T(1,128)S(1)}, u32[]{:S(2)}, u32[]{:S(2)}) async-start(s32[128,1,4]{2,1,0:T(1,128)} %bitcast.11), calls=%async_computation | async-start | bytes 131072 | tf_op jit(solution)/shard_map/all_to_all | solution.py:85
  93.4 5.5 %select_maximum_fusion = f32[40,40,520]{2,1,0:T(8,128)S(1)} fusion(f32[40,4,512]{2,1,0:T(4,128)S(1)} %collective-permute-done.6, f32[40,4,512]{2,1,0:T(4,128)S(1)} %collective-permute-done.7, f32[4,32,512]{2,1,0:T(8,128)S(1)} %collective-permute-done.4, f32[32,32,512]{2,1,0:T(8,128)} %copy-done.1, f32[4,32,512]{2,1,0:T(8,128)S(1)} %collective-permute-done.5), kind=kLoop, calls=%fused_computation.16 | loop fusion | flops 9984000 | bytes 6604800 | tf_op jit(solution)/shard_map/concatenate | solution.py:25
  98.9 4.3 %pad_maximum_fusion.1 = (f32[40,36,512]{2,1,0:T(8,128)}, f32[40,36,512]{2,1,0:T(8,128)}) fusion(f32[40,4,512]{2,1,0:T(4,128)S(1)} %collective-permute-done.6, f32[4,32,512]{2,1,0:T(8,128)S(1)} %collective-permute-done.4, f32[32,32,512]{2,1,0:T(8,128)S(1)} %copy-done.2, f32[4,32,512]{2,1,0:T(8,128)S(1)} %collective-permute-done.5, f32[40,4,512]{2,1,0:T(4,128)} %copy-done.5), kind=kLoop, calls=%fused_computation.27 | loop fusion | flops 4423680 | bytes 9175040 | tf_op jit(solution)/shard_map/concatenate | solution.py:25
  103.2 19.3 %fusion.67 = (bf16[32,32,512]{2,1,0:T(8,128)(2,1)}, f32[32,32,512]{2,1,0:T(8,128)}) fusion(f32[32,32,512]{2,1,0:T(8,128)S(1)} %copy-done.2, f32[1,2,32,32,512]{4,3,2,1,0:T(8,128)} %param.11, f32[1,2,32,32,512]{4,3,2,1,0:T(8,128)} %param.10, f32[40,40,520]{2,1,0:T(8,128)S(1)} %select_maximum_fusion, f32[40,36,512]{2,1,0:T(8,128)} %get-tuple-element.8, ...), kind=kLoop, calls=%fused_computation.120 | loop fusion | flops 24117248 | bytes 49807360 | tf_op jit(solution)/shard_map/add | solution.py:68
  122.5 9.6 %reshape.46 = bf16[4,8,4,8,32,16]{5,4,3,2,1,0:T(8,128)(2,1)} reshape(bf16[32,32,512]{2,1,0:T(8,128)(2,1)} %get-tuple-element.5) | data formatting | bytes 2097152 | tf_op jit(solution)/shard_map/reshape | solution.py:70
  132.0 11.0 %copy.14 = bf16[4,4,32,8,8,16]{2,1,0,5,4,3:T(4,128)(2,1)} copy(bf16[4,4,32,8,8,16]{5,2,4,1,3,0:T(8,128)(2,1)} %bitcast.44) | data formatting | bytes 2097152 | tf_op jit(solution)/shard_map/transpose | solution.py:71
  143.0 8.5 %reshape.47 = bf16[512,1024]{0,1:T(8,128)(2,1)S(1)} reshape(bf16[4,4,32,8,8,16]{2,1,0,5,4,3:T(4,128)(2,1)} %copy.14) | data formatting | bytes 2097152 | tf_op jit(solution)/shard_map/reshape | solution.py:71
  152.3 2.1 %gather_fusion.1 = bf16[512,1024]{1,0:T(8,128)(2,1)S(1)} fusion(bf16[512,1024]{1,0:T(8,128)(2,1)S(1)} %select_convert_fusion, s32[1024]{0:T(1024)S(1)} %pad_clamp_fusion), kind=kCustom, calls=%fused_computation.1 | custom fusion | bytes 2099200 | tf_op jit(solution)/shard_map/gather | solution.py:81
  154.4 1.2 reshape.48
  155.6 9.8 %all-to-all-start.1 = ((bf16[128,4,1024]{2,1,0:T(4,128)(2,1)}), bf16[128,4,1024]{2,1,0:T(4,128)(2,1)S(1)}, u32[]{:S(2)}, u32[]{:S(2)}) async-start(bf16[128,4,1024]{2,1,0:T(4,128)(2,1)} %reshape.48), calls=%async_computation.1 | async-start | bytes 2097152 | tf_op jit(solution)/shard_map/all_to_all | solution.py:84
  166.8 17.6 %all-to-all-done.1 = bf16[128,4,1024]{2,1,0:T(4,128)(2,1)S(1)} async-done(((bf16[128,4,1024]{2,1,0:T(4,128)(2,1)}), bf16[128,4,1024]{2,1,0:T(4,128)(2,1)S(1)}, u32[]{:S(2)}, u32[]{:S(2)}) %all-to-all-start.1) | async-done | bytes 1048608 | tf_op jit(solution)/shard_map/all_to_all | solution.py:84
  184.7 1.1 fusion.68
  (32 shorter events, 4.0 us)
Async XLA Ops:
  0.6 27.0 %copy-start = (f32[1,32,32,512]{3,2,1,0:T(8,128)S(1)}, f32[1,32,32,512]{3,2,1,0:T(8,128)}, u32[]{:S(2)}) copy-start(f32[1,32,32,512]{3,2,1,0:T(8,128)} %param.8) | copy-start | bytes 6291460
  1.9 8.9 %collective-permute-start.1 = (f32[4,32,512]{2,1,0:T(8,128)S(1)}, f32[4,32,512]{2,1,0:T(8,128)S(1)}, u32[]{:S(2)}, u32[]{:S(2)}) collective-permute-start(f32[4,32,512]{2,1,0:T(8,128)S(1)} %get-tuple-element.18), channel_id=1, source_target_pairs={{0,8},{8,16},{16,24},{24,32},{32,40},{40,48},{48,56},{1,9},{9,17},... | collective-permute-start | bytes 786440 | tf_op jit(solution)/shard_map/ppermute | solution.py:21
  5.8 8.8 %collective-permute-start = (f32[4,32,512]{2,1,0:T(8,128)S(1)}, f32[4,32,512]{2,1,0:T(8,128)S(1)}, u32[]{:S(2)}, u32[]{:S(2)}) collective-permute-start(f32[4,32,512]{2,1,0:T(8,128)S(1)} %get-tuple-element.17), channel_id=1, source_target_pairs={{8,0},{16,8},{24,16},{32,24},{40,32},{48,40},{56,48},{9,1},{17,9},... | collective-permute-start | bytes 786440 | tf_op jit(solution)/shard_map/ppermute | solution.py:24
  15.9 10.7 %collective-permute-start.2 = (f32[40,4,512]{2,1,0:T(4,128)S(1)}, f32[40,4,512]{2,1,0:T(4,128)S(1)}, u32[]{:S(2)}, u32[]{:S(2)}) collective-permute-start(f32[40,4,512]{2,1,0:T(4,128)S(1)} %get-tuple-element.14), channel_id=1, source_target_pairs={{1,0},{2,1},{3,2},{4,3},{5,4},{6,5},{7,6},{9,8},{10,9},{11,10},{12... | collective-permute-start | bytes 983048 | tf_op jit(solution)/shard_map/ppermute | solution.py:24
  17.2 10.3 %collective-permute-start.3 = (f32[40,4,512]{2,1,0:T(4,128)S(1)}, f32[40,4,512]{2,1,0:T(4,128)S(1)}, u32[]{:S(2)}, u32[]{:S(2)}) collective-permute-start(f32[40,4,512]{2,1,0:T(4,128)S(1)} %get-tuple-element.13), channel_id=1, source_target_pairs={{0,1},{1,2},{2,3},{3,4},{4,5},{5,6},{6,7},{8,9},{9,10},{10,11},{11... | collective-permute-start | bytes 983048 | tf_op jit(solution)/shard_map/ppermute | solution.py:21
  31.8 2.3 %copy-start.3 = (f32[1,32,32,512]{3,2,1,0:T(8,128)S(1)}, f32[1,32,32,512]{3,2,1,0:T(8,128)}, u32[]{:S(2)}) copy-start(f32[1,32,32,512]{3,2,1,0:T(8,128)} %param.9) | copy-start | bytes 6291460
  34.1 17.0 %copy-start.6 = (s32[1,1,1,512]{3,2,1,0:T(1,128)S(1)}, s32[1,1,1,512]{3,2,1,0:T(1,128)}, u32[]{:S(2)}) copy-start(s32[1,1,1,512]{3,2,1,0:T(1,128)} %param.12) | copy-start | bytes 6148
  45.1 6.0 %copy-start.1 = (f32[32,32,512]{2,1,0:T(8,128)}, f32[32,32,512]{2,1,0:T(8,128)S(1)}, u32[]{:S(2)}) copy-start(f32[32,32,512]{2,1,0:T(8,128)S(1)} %fusion.43) | copy-start | bytes 6291460
  45.1 9.8 %collective-permute-start.4 = (f32[4,32,512]{2,1,0:T(8,128)S(1)}, f32[4,32,512]{2,1,0:T(8,128)S(1)}, u32[]{:S(2)}, u32[]{:S(2)}) collective-permute-start(f32[4,32,512]{2,1,0:T(8,128)S(1)} %get-tuple-element.16), channel_id=1, source_target_pairs={{8,0},{16,8},{24,16},{32,24},{40,32},{48,40},{56,48},{9,1},{17,9},... | collective-permute-start | bytes 786440 | tf_op jit(solution)/shard_map/ppermute | solution.py:24
  46.4 8.5 %collective-permute-start.5 = (f32[4,32,512]{2,1,0:T(8,128)S(1)}, f32[4,32,512]{2,1,0:T(8,128)S(1)}, u32[]{:S(2)}, u32[]{:S(2)}) collective-permute-start(f32[4,32,512]{2,1,0:T(8,128)S(1)} %get-tuple-element.15), channel_id=1, source_target_pairs={{0,8},{8,16},{16,24},{24,32},{32,40},{40,48},{48,56},{1,9},{9,17},... | collective-permute-start | bytes 786440 | tf_op jit(solution)/shard_map/ppermute | solution.py:21
  57.1 35.5 %collective-permute-start.6 = (f32[40,4,512]{2,1,0:T(4,128)}, f32[40,4,512]{2,1,0:T(4,128)S(1)}, u32[]{:S(2)}, u32[]{:S(2)}) collective-permute-start(f32[40,4,512]{2,1,0:T(4,128)} %get-tuple-element.10), channel_id=1, source_target_pairs={{1,0},{2,1},{3,2},{4,3},{5,4},{6,5},{7,6},{9,8},{10,9},{11,10},{12... | collective-permute-start | bytes 983048 | tf_op jit(solution)/shard_map/ppermute | solution.py:24
  58.4 34.3 %collective-permute-start.7 = (f32[40,4,512]{2,1,0:T(4,128)}, f32[40,4,512]{2,1,0:T(4,128)S(1)}, u32[]{:S(2)}, u32[]{:S(2)}) collective-permute-start(f32[40,4,512]{2,1,0:T(4,128)} %get-tuple-element.9), channel_id=1, source_target_pairs={{0,1},{1,2},{2,3},{3,4},{4,5},{5,6},{6,7},{8,9},{9,10},{10,11},{11... | collective-permute-start | bytes 983048 | tf_op jit(solution)/shard_map/ppermute | solution.py:21
  71.6 84.0 %all-to-all-start = ((s32[128,1,4]{2,1,0:T(1,128)}), s32[128,1,4]{2,1,0:T(1,128)S(1)}, u32[]{:S(2)}, u32[]{:S(2)}) async-start(s32[128,1,4]{2,1,0:T(1,128)} %bitcast.11), calls=%async_computation | async-start | bytes 131072 | tf_op jit(solution)/shard_map/all_to_all | solution.py:85
  92.6 6.3 %copy-start.2 = (f32[32,32,512]{2,1,0:T(8,128)S(1)}, f32[32,32,512]{2,1,0:T(8,128)}, u32[]{:S(2)}) copy-start(f32[32,32,512]{2,1,0:T(8,128)} %copy-done.1) | copy-start | bytes 6291460
  92.7 0.7 copy-start.5
  98.9 4.3 %copy-start.4 = (f32[1,32,32,512]{3,2,1,0:T(8,128)S(1)}, f32[1,32,32,512]{3,2,1,0:T(8,128)}, u32[]{:S(2)}) copy-start(f32[1,32,32,512]{3,2,1,0:T(8,128)} %param.9) | copy-start | bytes 6291460
  155.6 28.8 %all-to-all-start.1 = ((bf16[128,4,1024]{2,1,0:T(4,128)(2,1)}), bf16[128,4,1024]{2,1,0:T(4,128)(2,1)S(1)}, u32[]{:S(2)}, u32[]{:S(2)}) async-start(bf16[128,4,1024]{2,1,0:T(4,128)(2,1)} %reshape.48), calls=%async_computation.1 | async-start | bytes 2097152 | tf_op jit(solution)/shard_map/all_to_all | solution.py:84
where the time goes:
time: 187 us; the launch traced here: 186 us
  starting transfers between devices  58.3 us (31%)
  other arithmetic  54.9 us (29%)
  local copies, waits for them, and re-layouts  40 us (21%)
  waiting for transfers between devices  29.9 us (16%)
    ppermute x4, starting transfers between devices, padded_2(): lax.ppermute(lax.slice_in_dim(block, block.shape[dim] - width, None, axis...  22.4 us
    all_to_all x1, starting transfers between devices, per_device(): lax.all_to_all(sent_ids, ('shot', 'gx', 'gy'), split_axis=0, concat_axis=...  21 us
    concatenate x6, other arithmetic, padded_2(): block = jnp.concatenate([low, block, high], axis=dim)  19.8 us
    add x1, other arithmetic, per_device(): imaging = forward[0] * stepped_one + forward[1] * stepped_two  19.3 us
    all_to_all x1, waiting for transfers between devices, per_device(): lax.all_to_all(outgoing, ('shot', 'gx', 'gy'), split_axis=0, concat_axis=...  17.6 us
    add x1, other arithmetic, advance(): return 2.0 * current - earlier + velocity * laplace_term + source  11 us
    transpose x1, local copies, waits for them, and re-layouts, per_device(): blocks = blocks.transpose(0, 2, 4, 1, 3, 5).reshape(-1, TX * TY * TZ)  11 us
    all_to_all x1, starting transfers between devices, per_device(): lax.all_to_all(outgoing, ('shot', 'gx', 'gy'), split_axis=0, concat_axis=...  9.76 us
  transfers between devices with their start and end apart: 10, of which 5 were waited for; matrix products, arithmetic and copies ran while one was open for 38% of the time, Pallas kernels for 0%

commit v1 on v0

v1 whole, which is shorter than its diff:
```python
import jax
import jax.numpy as jnp
from jax import lax
from jax.experimental import pallas as pl
from jax.experimental.pallas import tpu as pltpu
from jax.sharding import PartitionSpec as P

CENTER = -205.0 / 72.0
COEFFS = (8.0 / 5.0, -1.0 / 5.0, 8.0 / 315.0, -1.0 / 560.0)

CX = 32
CY = 32
CZ = 512
XB = 8
OWNERS = 128
CAP = 4
SLABS = 9
NDEV = 8

F32 = jnp.float32
BF16 = jnp.bfloat16
VMEM_LIMIT = 60 * 1024 * 1024

SWAP_A = [(i, i ^ 1) for i in range(NDEV)]
SWAP_B = [(i, (i + 1) % NDEV if i % 2 else (i - 1) % NDEV) for i in range(NDEV)]


def swap_faces(x0, x1, y0, y1):
    return (
        lax.ppermute(x0, "gx", SWAP_A),
        lax.ppermute(x1, "gx", SWAP_B),
        lax.ppermute(y0, "gy", SWAP_A),
        lax.ppermute(y1, "gy", SWAP_B),
    )


def place_halos(ext, rx0, rx1, ry0, ry1, gx, gy):
    def put_x(low, high):
        ext[0:4, 8:40, :] = low[...].astype(F32)
        ext[36:40, 8:40, :] = high[...].astype(F32)

    def put_y(low, high):
        ext[4:36, 4:8, :] = low[...].astype(F32)
        ext[4:36, 40:44, :] = high[...].astype(F32)

    @pl.when(gx % 2 == 1)
    def _():
        put_x(rx0, rx1)

    @pl.when(gx % 2 == 0)
    def _():
        put_x(rx1, rx0)

    @pl.when(gy % 2 == 1)
    def _():
        put_y(ry0, ry1)

    @pl.when(gy % 2 == 0)
    def _():
        put_y(ry1, ry0)

    @pl.when(gx == 0)
    def _():
        ext[0:4, 8:40, :] = jnp.zeros((4, CY, CZ), F32)

    @pl.when(gx == NDEV - 1)
    def _():
        ext[36:40, 8:40, :] = jnp.zeros((4, CY, CZ), F32)

    @pl.when(gy == 0)
    def _():
        ext[4:36, 4:8, :] = jnp.zeros((CX, 4, CZ), F32)

    @pl.when(gy == NDEV - 1)
    def _():
        ext[4:36, 40:44, :] = jnp.zeros((CX, 4, CZ), F32)


def laplace_rows(ext, x, ty):
    rows = ext[x + 4, 8 * ty : 8 * ty + 24, :]
    middle = rows[8:16]
    lane = lax.broadcasted_iota(jnp.int32, (8, CZ), 1)
    summed = (3.0 * CENTER) * middle
    for k, weight in enumerate(COEFFS, 1):
        nearby = ext[x + 4 + k, 8 * ty + 8 : 8 * ty + 16, :] + ext[x + 4 - k, 8 * ty + 8 : 8 * ty + 16, :]
        nearby = nearby + rows[8 + k : 16 + k] + rows[8 - k : 16 - k]
        nearby = nearby + jnp.where(lane >= k, pltpu.roll(middle, k, 1), 0.0)
        nearby = nearby + jnp.where(lane < CZ - k, pltpu.roll(middle, CZ - k, 1), 0.0)
        summed = summed + weight * nearby
    return summed, middle


def first_kernel(
    where_ref, now_hbm, rx0, rx1, ry0, ry1, prev_ref, speed_ref, source_ref,
    one_ref, sx0, sx1, sy0, sy1, ext, sem,
):
    step = pl.program_id(0)
    gx = where_ref[0]
    gy = where_ref[1]

    @pl.when(step == 0)
    def _():
        copy = pltpu.make_async_copy(now_hbm.at[0], ext.at[4:36, 8:40, :], sem)
        copy.start()
        place_halos(ext, rx0, rx1, ry0, ry1, gx, gy)
        copy.wait()

    def plane(xl, carry):
        x = step * XB + xl
        for ty in range(4):
            rows = slice(8 * ty, 8 * ty + 8)
            summed, middle = laplace_rows(ext, x, ty)
            one_ref[0, xl, rows, :] = (
                2.0 * middle - prev_ref[0, xl, rows, :] + speed_ref[0, xl, rows, :] * summed
                + source_ref[0, 0, xl, rows, :]
            )
        return carry

    lax.fori_loop(0, XB, plane, 0)

    @pl.when((step == 0) & (gx % 2 == 1))
    def _():
        sx0[...] = one_ref[0, 0:4].astype(BF16)

    @pl.when((step == 0) & (gx % 2 == 0))
    def _():
        sx1[...] = one_ref[0, 0:4].astype(BF16)

    @pl.when((step == 3) & (gx % 2 == 1))
    def _():
        sx1[...] = one_ref[0, 4:8].astype(BF16)

    @pl.when((step == 3) & (gx % 2 == 0))
    def _():
        sx0[...] = one_ref[0, 4:8].astype(BF16)

    @pl.when(gy % 2 == 1)
    def _():
        sy0[...] = one_ref[0, :, 0:4, :].astype(BF16)
        sy1[...] = one_ref[0, :, 28:32, :].astype(BF16)

    @pl.when(gy % 2 == 0)
    def _():
        sy1[...] = one_ref[0, :, 0:4, :].astype(BF16)
        sy0[...] = one_ref[0, :, 28:32, :].astype(BF16)


def swap_granules(vals):
    granule = lax.broadcasted_iota(jnp.int32, (8, 128), 1) // 16
    vals = list(vals)
    for bit in (1, 2, 4):
        mask = (granule & bit) != 0
        for i in range(8):
            if i & bit:
                continue
            low, high = vals[i], vals[i + bit]
            vals[i] = jnp.where(mask, pltpu.roll(high, 16 * bit, 1), low)
            vals[i + bit] = jnp.where(mask, high, pltpu.roll(low, 128 - 16 * bit, 1))
    return vals


def second_kernel(
    where_ref, foot_ref, live_ref, one_hbm, rx0, rx1, ry0, ry1, now_ref, speed_ref, source_ref, forward_ref,
    two_ref, out_ref, ext, image, slots, count, sem,
):
    step = pl.program_id(0)
    gx = where_ref[0]
    gy = where_ref[1]

    @pl.when(step == 0)
    def _():
        copy = pltpu.make_async_copy(one_hbm.at[0], ext.at[4:36, 8:40, :], sem)
        copy.start()
        for o in range(OWNERS):
            count[o] = 0
        place_halos(ext, rx0, rx1, ry0, ry1, gx, gy)
        copy.wait()

    for ty in range(4):
        rows = slice(8 * ty, 8 * ty + 8)

        def plane(xl, carry):
            x = step * XB + xl
            summed, middle = laplace_rows(ext, x, ty)
            two = (
                2.0 * middle - now_ref[0, xl, rows, :] + speed_ref[0, xl, rows, :] * summed
                + source_ref[0, 0, xl, rows, :]
            )
            two_ref[0, xl, rows, :] = two
            image[xl] = forward_ref[0, 0, xl, rows, :] * middle + forward_ref[0, 1, xl, rows, :] * two
            return carry

        lax.fori_loop(0, XB, plane, 0)

        for zv in range(4):
            pieces = swap_granules([image[x, :, 128 * zv : 128 * zv + 128] for x in range(XB)])
            for p in range(8):
                s = step * 128 + ty * 32 + zv * 8 + p
                listed = foot_ref[s]
                owner = listed // OWNERS
                rank = count[owner]
                count[owner] = rank + 1
                at = owner * SLABS + 2 * rank
                piece = pieces[p].astype(BF16)
                out_ref[at] = piece[0:4]
                out_ref[at + 1] = piece[4:8]
                slot = jnp.where(s < live_ref[0], listed % OWNERS, -1).astype(F32)
                slots[owner, pl.ds(rank, 1), :] = jnp.full((1, 128), slot, F32)

    @pl.when(step == 3)
    def _():
        def put(o, carry):
            out_ref[o * SLABS + 8] = slots[o].astype(BF16)
            return carry

        lax.fori_loop(0, OWNERS, put, 0)


def owner_kernel(in_ref, grad_ref, rows, ids, spread):
    def unpack(j, carry):
        halves = []
        for b in range(2):
            source = 2 * j + b
            for k in range(CAP):
                rows[source * CAP + k, 0:4, :] = in_ref[source * SLABS + 2 * k].astype(F32)
                rows[source * CAP + k, 4:8, :] = in_ref[source * SLABS + 2 * k + 1].astype(F32)
            halves.append(in_ref[source * SLABS + 8].astype(F32))
        ids[pl.ds(8 * j, 8), :] = jnp.concatenate(halves, axis=0)
        return carry

    lax.fori_loop(0, OWNERS // 2, unpack, 0)
    slot = lax.broadcasted_iota(jnp.int32, (OWNERS * CAP, 128), 1).astype(F32)
    onehot = jnp.where(ids[...] == slot, 1.0, 0.0).astype(BF16)
    for y in range(8):
        spread[:, 128 * y : 128 * y + 128] = lax.dot_general(
            onehot, rows[:, y, :].astype(BF16), (((0,), (0,)), ((), ())), preferred_element_type=F32
        )
    for t in range(16):
        at = slice(8 * t, 8 * t + 8)
        vals = swap_granules([spread[at, 128 * y : 128 * y + 128] for y in range(8)])
        for x in range(8):
            grad_ref[at, 128 * x : 128 * x + 128] = vals[x]


def whole(shape):
    return pl.BlockSpec(shape, lambda i: (0,) * len(shape))


SMEM = pl.BlockSpec(memory_space=pltpu.SMEM)
HBM = pl.BlockSpec(memory_space=pl.ANY)
PLANES = pl.BlockSpec((1, XB, CY, CZ), lambda i: (0, i, 0, 0))
FACE_X = whole((4, CY, CZ))
FACE_Y = whole((CX, 4, CZ))
PARAMS = pltpu.CompilerParams(dimension_semantics=("arbitrary",), vmem_limit_bytes=VMEM_LIMIT)


def picked(half):
    return pl.BlockSpec((1, 1, XB, CY, CZ), lambda i: (0, half, i, 0, 0))


def per_device(
    adjoint_prev, adjoint_now, speed_term, adjoint_source, forward_accel, footprint, live_counts
):
    gx = lax.axis_index("gx").astype(jnp.int32)
    gy = lax.axis_index("gy").astype(jnp.int32)
    place = jnp.stack([gx, gy])
    current = adjoint_now[0]
    odd_x = gx % 2 == 1
    odd_y = gy % 2 == 1
    x_low, x_high = current[0:4].astype(BF16), current[28:32].astype(BF16)
    y_low, y_high = current[:, 0:4].astype(BF16), current[:, 28:32].astype(BF16)
    faces = swap_faces(
        jnp.where(odd_x, x_low, x_high),
        jnp.where(odd_x, x_high, x_low),
        jnp.where(odd_y, y_low, y_high),
        jnp.where(odd_y, y_high, y_low),
    )
    face_x = jax.ShapeDtypeStruct((4, CY, CZ), BF16)
    face_y = jax.ShapeDtypeStruct((CX, 4, CZ), BF16)
    face_y_planes = pl.BlockSpec((XB, 4, CZ), lambda i: (i, 0, 0))
    level = jax.ShapeDtypeStruct((1, CX, CY, CZ), F32)
    level_one, *send = pl.pallas_call(
        first_kernel,
        grid=(CX // XB,),
        in_specs=[SMEM, HBM, FACE_X, FACE_X, FACE_Y, FACE_Y, PLANES, PLANES, picked(0)],
        out_specs=[PLANES, FACE_X, FACE_X, face_y_planes, face_y_planes],
        out_shape=[level, face_x, face_x, face_y, face_y],
        scratch_shapes=[pltpu.VMEM((CX + 8, CY + 16, CZ), F32), pltpu.SemaphoreType.DMA],
        compiler_params=PARAMS,
        name="level_one",
    )(place, adjoint_now, *faces, adjoint_prev, speed_term, adjoint_source)
    faces = swap_faces(*send)
    level_two, outgoing = pl.pallas_call(
        second_kernel,
        grid=(CX // XB,),
        in_specs=[
            SMEM, SMEM, SMEM, HBM, FACE_X, FACE_X, FACE_Y, FACE_Y, PLANES, PLANES, picked(1),
            pl.BlockSpec((1, 2, XB, CY, CZ), lambda i: (0, 0, i, 0, 0)),
        ],
        out_specs=[PLANES, whole((OWNERS * SLABS, 4, 128))],
        out_shape=[level, jax.ShapeDtypeStruct((OWNERS * SLABS, 4, 128), BF16)],
        scratch_shapes=[
            pltpu.VMEM((CX + 8, CY + 16, CZ), F32),
            pltpu.VMEM((XB, 8, CZ), F32),
            pltpu.VMEM((OWNERS, CAP, 128), F32),
            pltpu.SMEM((OWNERS,), jnp.int32),
            pltpu.SemaphoreType.DMA,
        ],
        compiler_params=PARAMS,
        name="level_two",
    )(
        place, footprint.reshape(-1), live_counts.reshape(-1), level_one, *faces,
        adjoint_now, speed_term, adjoint_source, forward_accel,
    )
    incoming = lax.all_to_all(outgoing, ("shot", "gx", "gy"), split_axis=0, concat_axis=0, tiled=True)
    gradient = pl.pallas_call(
        owner_kernel,
        out_shape=jax.ShapeDtypeStruct((OWNERS, 1024), F32),
        scratch_shapes=[
            pltpu.VMEM((OWNERS * CAP, 8, 128), F32),
            pltpu.VMEM((OWNERS * CAP, 128), F32),
            pltpu.VMEM((OWNERS, 1024), F32),
        ],
        compiler_params=pltpu.CompilerParams(vmem_limit_bytes=VMEM_LIMIT),
        name="owner_sum",
    )(incoming)
    return (level_one, level_two, gradient)


def solution(mesh):
    return jax.shard_map(
        per_device,
        mesh=mesh,
        in_specs=(
            P("shot", "gx", "gy", None),
            P("shot", "gx", "gy", None),
            P("shot", "gx", "gy", None),
            P("shot", None, "gx", "gy", None),
            P("shot", None, "gx", "gy", None),
            P("shot", "gx", "gy", None),
            P("shot", "gx", "gy"),
        ),
        out_specs=(
            P("shot", "gx", "gy", None),
            P("shot", "gx", "gy", None),
            P(("shot", "gx", "gy"), None),
        ),
        check_vma=False,
    )
```

time: 187 us -> 107 us (0.57)
  other arithmetic: 54.9 us -> 3.41 us
  Pallas kernels: 0 us -> 43.7 us
  starting transfers between devices: 58.3 us -> 17 us
  local copies, waits for them, and re-layouts: 40 us -> 1.99 us
  blocking collectives: 0 us -> 27.8 us
  waiting for transfers between devices: 29.9 us -> 11.8 us
    pallas_call x0 -> x3, Pallas kernels: none -> 43.7 us  [the longest x1 26.9 us: per_device(): pl.pallas_call(second_kernel, grid=(CX // XB,), in_specs=[SMEM, SMEM, SME...]
    all_to_all x2 -> x0, starting transfers between devices: 30.8 us -> none  [the longest x1 21 us: per_device(): lax.all_to_all(sent_ids, ('shot', 'gx', 'gy'), split_axis=0, concat_axis=...]
    add x2 -> x0, other arithmetic: 30.3 us -> none  [the longest x1 19.3 us: per_device(): imaging = forward[0] * stepped_one + forward[1] * stepped_two]
    all_to_all x0 -> x1, blocking collectives: none -> 27.8 us  [per_device(): lax.all_to_all(outgoing, ('shot', 'gx', 'gy'), split_axis=0, concat_axis=...]
    reshape x5 -> x0, local copies, waits for them, and re-layouts: 20.1 us -> none  [the longest x1 9.59 us: per_device(): imaging.reshape(cells_wide // TX, TX, cells_long // TY, TY, cells_deep //...]
    concatenate x6 -> x0, other arithmetic: 19.8 us -> none  [padded_2(): block = jnp.concatenate([low, block, high], axis=dim)]
    all_to_all x2 -> x0, waiting for transfers between devices: 17.6 us -> none  [the longest x1 17.6 us: per_device(): lax.all_to_all(outgoing, ('shot', 'gx', 'gy'), split_axis=0, concat_axis=...]
    transpose x1 -> x0, local copies, waits for them, and re-layouts: 11 us -> none  [per_device(): blocks = blocks.transpose(0, 2, 4, 1, 3, 5).reshape(-1, TX * TY * TZ)]
  transfers between devices with their start and end apart: 10 -> 8, of which waited for: 5 -> 3; matrix products, arithmetic and copies ran while one was open for 38% -> 1% of each run, Pallas kernels for 0% -> 0%
where the time goes in v1:
time: 107 us
  Pallas kernels  43.7 us (41%)
  blocking collectives  27.8 us (26%)
  starting transfers between devices  17 us (16%)
  waiting for transfers between devices  11.8 us (11%)
  other arithmetic  3.41 us (3%)
  local copies, waits for them, and re-layouts  1.99 us (2%)
  between operations  1.42 us (1%)
    all_to_all x1, blocking collectives, per_device(): lax.all_to_all(outgoing, ('shot', 'gx', 'gy'), split_axis=0, concat_axis=...  27.8 us
    pallas_call x1, Pallas kernels, per_device(): pl.pallas_call(second_kernel, grid=(CX // XB,), in_specs=[SMEM, SMEM, SME...  26.9 us
    pallas_call x1, Pallas kernels, per_device(): pl.pallas_call(first_kernel, grid=(CX // XB,), in_specs=[SMEM, HBM, FACE_...  11.5 us
    ppermute x2, waiting for transfers between devices, swap_faces(): lax.ppermute(y0, 'gy', SWAP_A)  10.1 us
    ppermute x2, starting transfers between devices, swap_faces(): lax.ppermute(y1, 'gy', SWAP_B)  7.22 us
    ppermute x2, starting transfers between devices, swap_faces(): lax.ppermute(x1, 'gx', SWAP_B)  5.34 us
    pallas_call x1, Pallas kernels, per_device(): pl.pallas_call(owner_kernel, out_shape=jax.ShapeDtypeStruct((OWNERS, 1024...  5.32 us
    ppermute x2, starting transfers between devices, swap_faces(): lax.ppermute(y0, 'gy', SWAP_A)  4.31 us
  transfers between devices with their start and end apart: 8, of which 3 were waited for; matrix products, arithmetic and copies ran while one was open for 1% of the time, Pallas kernels for 0%

profile of v1, /device:TPU:1, one launch (start us, length us, event | category | flops | bytes accessed | tf_op | source)
XLA Modules:
  0.0 107.1 jit_solution(10164456632272893748)
XLA Ops:
  0.6 0.0 copy-start
  0.7 1.9 %convert_bitcast_fusion = bf16[32,32,512]{2,1,0:T(8,128)(2,1)S(1)} fusion(f32[1,32,32,512]{3,2,1,0:T(8,128)} %now_ref.1), kind=kLoop, calls=%fused_computation.5 | loop fusion | flops 524288 | bytes 3145728 | tf_op jit(solution)/shard_map/convert.1
  2.5 0.8 broadcast_select_fusion
  3.3 7.2 %collective-permute-start.3 = (bf16[32,4,512]{2,1,0:T(4,128)(2,1)}, bf16[32,4,512]{2,1,0:T(4,128)(2,1)S(1)}, u32[]{:S(2)}, u32[]{:S(2)}) collective-permute-start(bf16[32,4,512]{2,1,0:T(4,128)(2,1)} %get-tuple-element.17), channel_id=1, source_target_pairs={{0,7},{1,2},{2,1},{3,4},{4,3},{5,6},{6,5},{7,0},{8,15},{9,10},{10,... | collective-permute-start | bytes 393224 | tf_op jit(solution)/shard_map/ppermute | solution.py:33
  10.6 0.0 collective-permute-start.2
  10.6 0.1 convert.8
  10.8 2.7 %collective-permute-start.1 = (bf16[4,32,512]{2,1,0:T(8,128)(2,1)S(1)}, bf16[4,32,512]{2,1,0:T(8,128)(2,1)S(1)}, u32[]{:S(2)}, u32[]{:S(2)}) collective-permute-start(bf16[4,32,512]{2,1,0:T(8,128)(2,1)S(1)} %get-tuple-element.19), channel_id=1, source_target_pairs={{0,56},{8,16},{16,8},{24,32},{32,24},{40,48},{48,40},{56,0},{1,57}... | collective-permute-start | bytes 393224 | tf_op jit(solution)/shard_map/ppermute | solution.py:31
  13.4 0.0 collective-permute-start
  13.4 0.6 pad_add_fusion.where_ref
  14.0 0.0 collective-permute-done.3.ry1
  14.0 4.6 %collective-permute-done.2.ry0 = bf16[32,4,512]{2,1,0:T(4,128)(2,1)S(1)} collective-permute-done((bf16[32,4,512]{2,1,0:T(4,128)(2,1)S(1)}, bf16[32,4,512]{2,1,0:T(4,128)(2,1)S(1)}, u32[]{:S(2)}, u32[]{:S(2)}) %collective-permute-start.2) | collective-permute-done | bytes 131104 | tf_op jit(solution)/shard_map/ppermute | solution.py:32
  18.6 0.0 collective-permute-done.1.rx1
  18.6 0.0 collective-permute-done.rx0
  18.6 0.6 copy-done.2
  19.2 0.0 copy-done.4
  19.3 0.7 copy-done.6
  19.9 11.5 %level_one.1 = (f32[1,32,32,512]{3,2,1,0:T(8,128)}, bf16[4,32,512]{2,1,0:T(8,128)(2,1)}, bf16[4,32,512]{2,1,0:T(8,128)(2,1)}, bf16[32,4,512]{2,1,0:T(4,128)(2,1)}, bf16[32,4,512]{2,1,0:T(4,128)(2,1)}) custom-call(s32[2]{0:T(128)} %pad_add_fusion.where_ref, f32[1,32,32,512]{3,2,1,0:T(8,128)} %now_ref.1, bf16[4,32,512]{2,1,0:T(8,128)(2,1)} %copy-done.6, ...), custom_call_target="tpu_custom_call" | custom-call | tf_op jit(solution)/shard_map/level_one/pallas_call | solution.py:282
  31.5 0.1 collective-permute-start.4
  31.5 2.7 %collective-permute-start.5 = (bf16[4,32,512]{2,1,0:T(8,128)(2,1)}, bf16[4,32,512]{2,1,0:T(8,128)(2,1)S(1)}, u32[]{:S(2)}, u32[]{:S(2)}) collective-permute-start(bf16[4,32,512]{2,1,0:T(8,128)(2,1)} %get-tuple-element.12), channel_id=1, source_target_pairs={{0,56},{8,16},{16,8},{24,32},{32,24},{40,48},{48,40},{56,0},{1,57}... | collective-permute-start | bytes 393224 | tf_op jit(solution)/shard_map/ppermute | solution.py:31
  34.2 4.3 %collective-permute-start.6 = (bf16[32,4,512]{2,1,0:T(4,128)(2,1)}, bf16[32,4,512]{2,1,0:T(4,128)(2,1)S(1)}, u32[]{:S(2)}, u32[]{:S(2)}) collective-permute-start(bf16[32,4,512]{2,1,0:T(4,128)(2,1)} %get-tuple-element.13), channel_id=1, source_target_pairs={{0,1},{1,0},{2,3},{3,2},{4,5},{5,4},{6,7},{7,6},{8,9},{9,8},{10,11... | collective-permute-start | bytes 393224 | tf_op jit(solution)/shard_map/ppermute | solution.py:32
  38.5 0.0 collective-permute-start.7
  39.2 0.0 collective-permute-done.4.rx0
  39.2 0.0 copy-start.3
  39.2 0.0 collective-permute-done.5.rx1
  39.2 0.0 copy-start.5
  39.2 5.5 %collective-permute-done.6.ry0 = bf16[32,4,512]{2,1,0:T(4,128)(2,1)S(1)} collective-permute-done((bf16[32,4,512]{2,1,0:T(4,128)(2,1)}, bf16[32,4,512]{2,1,0:T(4,128)(2,1)S(1)}, u32[]{:S(2)}, u32[]{:S(2)}) %collective-permute-start.6) | collective-permute-done | bytes 131104 | tf_op jit(solution)/shard_map/ppermute | solution.py:32
  44.8 1.7 %collective-permute-done.7.ry1 = bf16[32,4,512]{2,1,0:T(4,128)(2,1)S(1)} collective-permute-done((bf16[32,4,512]{2,1,0:T(4,128)(2,1)}, bf16[32,4,512]{2,1,0:T(4,128)(2,1)S(1)}, u32[]{:S(2)}, u32[]{:S(2)}) %collective-permute-start.7) | collective-permute-done | bytes 131104 | tf_op jit(solution)/shard_map/ppermute | solution.py:33
  46.5 0.0 copy-done.7
  46.5 0.6 copy-done.8
  47.1 26.9 %level_two.1 = (f32[1,32,32,512]{3,2,1,0:T(8,128)}, bf16[1152,4,128]{2,1,0:T(4,128)(2,1)}) custom-call(s32[2]{0:T(128)} %pad_add_fusion.where_ref, s32[512]{0:T(512)} %bitcast.11, s32[1]{0:T(128)} %bitcast.10.live_ref, f32[1,32,32,512]{3,2,1,0:T(8,128)} %get-tuple-element.7.one_hbm, bf16[4,32,512]{2,1,0:T(8,128)(2,1)} %copy-done.3, ...), custom_call_target="tpu_custom_call" | custom-call | tf_op jit(solution)/shard_map/level_two/pallas_call | solution.py:293
  74.0 27.8 %all_to_all.5.in_ref = bf16[1152,4,128]{2,1,0:T(4,128)(2,1)} all-to-all(bf16[1152,4,128]{2,1,0:T(4,128)(2,1)} %get-tuple-element.16), channel_id=1, replica_groups=mesh['shot'=2,'gx'=8,'gy'=8] {'shot','gx','gy'}, dimensions={0} | all-to-all | bytes 2359296 | tf_op jit(solution)/shard_map/all_to_all | solution.py:315
  101.7 5.3 %owner_sum.1 = f32[128,1024]{1,0:T(8,128)} custom-call(bf16[1152,4,128]{2,1,0:T(4,128)(2,1)} %all_to_all.5.in_ref), custom_call_target="tpu_custom_call" | custom-call | tf_op jit(solution)/shard_map/owner_sum/pallas_call | solution.py:316
  (11 shorter events, 0.0 us)
Async XLA Ops:
  0.6 9.9 %copy-start = (f32[1,32,32,512]{3,2,1,0:T(8,128)S(1)}, f32[1,32,32,512]{3,2,1,0:T(8,128)}, u32[]{:S(2)}) copy-start(f32[1,32,32,512]{3,2,1,0:T(8,128)} %now_ref.1) | copy-start | bytes 6291460
  3.3 10.6 %collective-permute-start.3 = (bf16[32,4,512]{2,1,0:T(4,128)(2,1)}, bf16[32,4,512]{2,1,0:T(4,128)(2,1)S(1)}, u32[]{:S(2)}, u32[]{:S(2)}) collective-permute-start(bf16[32,4,512]{2,1,0:T(4,128)(2,1)} %get-tuple-element.17), channel_id=1, source_target_pairs={{0,7},{1,2},{2,1},{3,4},{4,3},{5,6},{6,5},{7,0},{8,15},{9,10},{10,... | collective-permute-start | bytes 393224 | tf_op jit(solution)/shard_map/ppermute | solution.py:33
  10.6 8.0 %collective-permute-start.2 = (bf16[32,4,512]{2,1,0:T(4,128)(2,1)S(1)}, bf16[32,4,512]{2,1,0:T(4,128)(2,1)S(1)}, u32[]{:S(2)}, u32[]{:S(2)}) collective-permute-start(bf16[32,4,512]{2,1,0:T(4,128)(2,1)S(1)} %get-tuple-element.18), channel_id=1, source_target_pairs={{0,1},{1,0},{2,3},{3,2},{4,5},{5,4},{6,7},{7,6},{8,9},{9,8},{10,11... | collective-permute-start | bytes 393224 | tf_op jit(solution)/shard_map/ppermute | solution.py:32
  10.8 7.8 %collective-permute-start.1 = (bf16[4,32,512]{2,1,0:T(8,128)(2,1)S(1)}, bf16[4,32,512]{2,1,0:T(8,128)(2,1)S(1)}, u32[]{:S(2)}, u32[]{:S(2)}) collective-permute-start(bf16[4,32,512]{2,1,0:T(8,128)(2,1)S(1)} %get-tuple-element.19), channel_id=1, source_target_pairs={{0,56},{8,16},{16,8},{24,32},{32,24},{40,48},{48,40},{56,0},{1,57}... | collective-permute-start | bytes 393224 | tf_op jit(solution)/shard_map/ppermute | solution.py:31
  13.4 5.1 %collective-permute-start = (bf16[4,32,512]{2,1,0:T(8,128)(2,1)S(1)}, bf16[4,32,512]{2,1,0:T(8,128)(2,1)S(1)}, u32[]{:S(2)}, u32[]{:S(2)}) collective-permute-start(bf16[4,32,512]{2,1,0:T(8,128)(2,1)S(1)} %get-tuple-element.20), channel_id=1, source_target_pairs={{0,8},{8,0},{16,24},{24,16},{32,40},{40,32},{48,56},{56,48},{1,9},... | collective-permute-start | bytes 393224 | tf_op jit(solution)/shard_map/ppermute | solution.py:30
  14.0 4.6 %copy-start.1 = (bf16[32,4,512]{2,1,0:T(4,128)(2,1)}, bf16[32,4,512]{2,1,0:T(4,128)(2,1)S(1)}, u32[]{:S(2)}) copy-start(bf16[32,4,512]{2,1,0:T(4,128)(2,1)S(1)} %collective-permute-done.3.ry1) | copy-start | bytes 393220
  18.6 0.6 copy-start.2
  18.6 0.7 copy-start.4
  19.3 0.7 copy-start.6
  31.5 7.7 %collective-permute-start.4 = (bf16[4,32,512]{2,1,0:T(8,128)(2,1)}, bf16[4,32,512]{2,1,0:T(8,128)(2,1)S(1)}, u32[]{:S(2)}, u32[]{:S(2)}) collective-permute-start(bf16[4,32,512]{2,1,0:T(8,128)(2,1)} %get-tuple-element.11), channel_id=1, source_target_pairs={{0,8},{8,0},{16,24},{24,16},{32,40},{40,32},{48,56},{56,48},{1,9},... | collective-permute-start | bytes 393224 | tf_op jit(solution)/shard_map/ppermute | solution.py:30
  31.5 7.7 %collective-permute-start.5 = (bf16[4,32,512]{2,1,0:T(8,128)(2,1)}, bf16[4,32,512]{2,1,0:T(8,128)(2,1)S(1)}, u32[]{:S(2)}, u32[]{:S(2)}) collective-permute-start(bf16[4,32,512]{2,1,0:T(8,128)(2,1)} %get-tuple-element.12), channel_id=1, source_target_pairs={{0,56},{8,16},{16,8},{24,32},{32,24},{40,48},{48,40},{56,0},{1,57}... | collective-permute-start | bytes 393224 | tf_op jit(solution)/shard_map/ppermute | solution.py:31
  34.2 10.5 %collective-permute-start.6 = (bf16[32,4,512]{2,1,0:T(4,128)(2,1)}, bf16[32,4,512]{2,1,0:T(4,128)(2,1)S(1)}, u32[]{:S(2)}, u32[]{:S(2)}) collective-permute-start(bf16[32,4,512]{2,1,0:T(4,128)(2,1)} %get-tuple-element.13), channel_id=1, source_target_pairs={{0,1},{1,0},{2,3},{3,2},{4,5},{5,4},{6,7},{7,6},{8,9},{9,8},{10,11... | collective-permute-start | bytes 393224 | tf_op jit(solution)/shard_map/ppermute | solution.py:32
  38.5 7.9 %collective-permute-start.7 = (bf16[32,4,512]{2,1,0:T(4,128)(2,1)}, bf16[32,4,512]{2,1,0:T(4,128)(2,1)S(1)}, u32[]{:S(2)}, u32[]{:S(2)}) collective-permute-start(bf16[32,4,512]{2,1,0:T(4,128)(2,1)} %get-tuple-element.14), channel_id=1, source_target_pairs={{0,7},{1,2},{2,1},{3,4},{4,3},{5,6},{6,5},{7,0},{8,15},{9,10},{10,... | collective-permute-start | bytes 393224 | tf_op jit(solution)/shard_map/ppermute | solution.py:33
  39.2 7.3 %copy-start.3 = (bf16[4,32,512]{2,1,0:T(8,128)(2,1)}, bf16[4,32,512]{2,1,0:T(8,128)(2,1)S(1)}, u32[]{:S(2)}) copy-start(bf16[4,32,512]{2,1,0:T(8,128)(2,1)S(1)} %collective-permute-done.4.rx0) | copy-start | bytes 393220
  39.2 7.3 %copy-start.5 = (bf16[4,32,512]{2,1,0:T(8,128)(2,1)}, bf16[4,32,512]{2,1,0:T(8,128)(2,1)S(1)}, u32[]{:S(2)}) copy-start(bf16[4,32,512]{2,1,0:T(8,128)(2,1)S(1)} %collective-permute-done.5.rx1) | copy-start | bytes 393220
  44.8 1.7 %copy-start.7 = (bf16[32,4,512]{2,1,0:T(4,128)(2,1)}, bf16[32,4,512]{2,1,0:T(4,128)(2,1)S(1)}, u32[]{:S(2)}) copy-start(bf16[32,4,512]{2,1,0:T(4,128)(2,1)S(1)} %collective-permute-done.6.ry0) | copy-start | bytes 393220
  46.5 0.6 copy-start.8

commit v2 on v0

v2 whole, which is shorter than its diff:
```python
import jax
import jax.numpy as jnp
import numpy as np
from jax import lax
from jax.experimental import pallas as pl
from jax.experimental.pallas import tpu as pltpu
from jax.sharding import PartitionSpec as P

CENTER = -205.0 / 72.0
COEFFS = (8.0 / 5.0, -1.0 / 5.0, 8.0 / 315.0, -1.0 / 560.0)

CX = 32
CY = 32
CZ = 512
OWNERS = 128
CAP = 4
SUB = 512
SLABS = 9
NDEV = 8

F32 = jnp.float32
BF16 = jnp.bfloat16
MIB = 1024 * 1024

SWAP_A = [(i, i ^ 1) for i in range(NDEV)]
SWAP_B = [(i, (i + 1) % NDEV if i % 2 else (i - 1) % NDEV) for i in range(NDEV)]


def depth_band():
    band = np.zeros((CZ, CZ), np.float64)
    for k, weight in enumerate(COEFFS, 1):
        band += weight * (np.eye(CZ, k=k) + np.eye(CZ, k=-k))
    high = band.astype(jnp.bfloat16)
    low = (band - high.astype(np.float64)).astype(jnp.bfloat16)
    return high, low


def swap_faces(x0, x1, y0, y1):
    return (
        lax.ppermute(x0, "gx", SWAP_A),
        lax.ppermute(x1, "gx", SWAP_B),
        lax.ppermute(y0, "gy", SWAP_A),
        lax.ppermute(y1, "gy", SWAP_B),
    )


def emit_faces(get_x, get_y, gx, gy, sx0, sx1, sy0, sy1):
    @pl.when(gx % 2 == 1)
    def _():
        sx0[...] = get_x(0).astype(BF16)
        sx1[...] = get_x(1).astype(BF16)

    @pl.when(gx % 2 == 0)
    def _():
        sx0[...] = get_x(1).astype(BF16)
        sx1[...] = get_x(0).astype(BF16)

    @pl.when(gy % 2 == 1)
    def _():
        sy0[...] = get_y(0).astype(BF16)
        sy1[...] = get_y(1).astype(BF16)

    @pl.when(gy % 2 == 0)
    def _():
        sy0[...] = get_y(1).astype(BF16)
        sy1[...] = get_y(0).astype(BF16)


def face_kernel(where_ref, now_hbm, sx0, sx1, sy0, sy1, xs, ys, sems):
    gx = where_ref[0]
    gy = where_ref[1]
    copies = [
        pltpu.make_async_copy(now_hbm.at[0, 0:4], xs.at[0], sems.at[0]),
        pltpu.make_async_copy(now_hbm.at[0, 28:32], xs.at[1], sems.at[1]),
        pltpu.make_async_copy(now_hbm.at[0, :, 0:8, :], ys.at[0], sems.at[2]),
        pltpu.make_async_copy(now_hbm.at[0, :, 24:32, :], ys.at[1], sems.at[3]),
    ]
    for copy in copies:
        copy.start()
    for copy in copies:
        copy.wait()
    emit_faces(
        lambda side: xs[side], lambda side: ys[side, :, 4 * side : 4 * side + 4, :], gx, gy, sx0, sx1, sy0, sy1
    )


def depth_terms(values, high_ref, low_ref, zs):
    for i in range(4):
        block = values[0, 8 * i : 8 * i + 8].reshape(8 * CY, CZ)
        big = block.astype(BF16)
        small = (block - big.astype(F32)).astype(BF16)
        term = jnp.dot(big, high_ref[...], preferred_element_type=F32)
        term = term + jnp.dot(big, low_ref[...], preferred_element_type=F32)
        term = term + jnp.dot(small, high_ref[...], preferred_element_type=F32)
        zs[8 * i : 8 * i + 8] = term.reshape(8, CY, CZ)


def extend(values, ext):
    ext[0:4, 8:40, :] = jnp.zeros((4, CY, CZ), F32)
    ext[36:40, 8:40, :] = jnp.zeros((4, CY, CZ), F32)

    def fill(x, carry):
        ext[x + 4, 0:8, :] = jnp.zeros((8, CZ), F32)
        ext[x + 4, 8:40, :] = values[0, x]
        ext[x + 4, 40:48, :] = jnp.zeros((8, CZ), F32)
        return carry

    lax.fori_loop(0, CX, fill, 0)


def laplace_rows(ext, zs, x, ty):
    rows = ext[x + 4, 8 * ty : 8 * ty + 24, :]
    middle = rows[8:16]
    summed = (3.0 * CENTER) * middle + zs[x, 8 * ty : 8 * ty + 8, :]
    for k, weight in enumerate(COEFFS, 1):
        nearby = ext[x + 4 + k, 8 * ty + 8 : 8 * ty + 16, :] + ext[x + 4 - k, 8 * ty + 8 : 8 * ty + 16, :]
        nearby = nearby + rows[8 + k : 16 + k] + rows[8 - k : 16 - k]
        summed = summed + weight * nearby
    return summed, middle


def first_kernel(
    foot_ref, live_ref, now_ref, prev_ref, speed_ref, source_ref, high_ref, low_ref,
    one_ref, out_ref, at_ref, ext, zs, slots, count,
):
    for o in range(OWNERS):
        count[o] = 0
    depth_terms(now_ref, high_ref, low_ref, zs)
    extend(now_ref, ext)
    live = live_ref[0]

    def plane(x, carry):
        for j in range(SUB // CX):
            s = x * (SUB // CX) + j
            listed = foot_ref[s]
            owner = listed // OWNERS
            rank = count[owner]
            count[owner] = rank + 1
            at_ref[s] = owner * SLABS + 2 * rank
            slot = jnp.where(s < live, listed % OWNERS, -1).astype(F32)
            slots[owner, pl.ds(rank, 1), :] = jnp.full((1, 128), slot, F32)
        for ty in range(4):
            rows = slice(8 * ty, 8 * ty + 8)
            summed, middle = laplace_rows(ext, zs, x, ty)
            one_ref[0, x, rows, :] = (
                2.0 * middle - prev_ref[0, x, rows, :] + speed_ref[0, x, rows, :] * summed
                + source_ref[0, 0, x, rows, :]
            )
        return carry

    lax.fori_loop(0, CX, plane, 0)

    def put(o, carry):
        out_ref[o * SLABS + 8] = slots[o].astype(BF16)
        return carry

    lax.fori_loop(0, OWNERS, put, 0)


def second_kernel(
    one_ref, now_ref, speed_ref, source_ref, forward_ref, high_ref, low_ref,
    done_hbm, two_ref, image_ref, ext, zs, sem,
):
    copy = pltpu.make_async_copy(one_ref, done_hbm, sem)
    copy.start()
    depth_terms(one_ref, high_ref, low_ref, zs)
    extend(one_ref, ext)

    def plane(x, carry):
        for ty in range(4):
            rows = slice(8 * ty, 8 * ty + 8)
            summed, middle = laplace_rows(ext, zs, x, ty)
            two = (
                2.0 * middle - now_ref[0, x, rows, :] + speed_ref[0, x, rows, :] * summed
                + source_ref[0, 1, x, rows, :]
            )
            two_ref[0, x, rows, :] = two
            image_ref[0, x, rows, :] = forward_ref[0, 0, x, rows, :] * middle + forward_ref[0, 1, x, rows, :] * two
        return carry

    lax.fori_loop(0, CX, plane, 0)
    copy.wait()


def add_halos(rx0, rx1, ry0, ry1, gx, gy, add):
    row = lax.broadcasted_iota(jnp.int32, (8, CZ), 0)

    def x_side(face, side):
        def rows_of(ty):
            at = pl.ds(pl.multiple_of(8 * ty, 8), 8)
            layers = [face[h, at, :].astype(F32) for h in range(4)]
            for j in range(4):
                if side == 0:
                    term = sum(COEFFS[k - 1] * layers[4 + j - k] for k in range(j + 1, 5))
                    add(j, at, term)
                else:
                    term = sum(COEFFS[k - 1] * layers[k - 1 - j] for k in range(j + 1, 5))
                    add(CX - 1 - j, at, term)

        for ty in range(4):
            rows_of(ty)

    def y_side(face, side):
        def weights(h):
            total = jnp.zeros((8, CZ), F32)
            for j in range(4):
                k = 4 + j - h if side == 0 else h + 1 + j
                if 1 <= k <= 4:
                    at = j if side == 0 else 7 - j
                    total = jnp.where(row == at, COEFFS[k - 1], total)
            return total

        columns = [weights(h) for h in range(4)]

        def plane(x, carry):
            layers = face[x].astype(F32)
            term = sum(columns[h] * jnp.broadcast_to(layers[h : h + 1], (8, CZ)) for h in range(4))
            add(x, slice(0, 8) if side == 0 else slice(24, 32), term)
            return carry

        lax.fori_loop(0, CX, plane, 0)

    @pl.when((gx > 0) & (gx % 2 == 1))
    def _():
        x_side(rx0, 0)

    @pl.when((gx > 0) & (gx % 2 == 0))
    def _():
        x_side(rx1, 0)

    @pl.when((gx < NDEV - 1) & (gx % 2 == 1))
    def _():
        x_side(rx1, 1)

    @pl.when((gx < NDEV - 1) & (gx % 2 == 0))
    def _():
        x_side(rx0, 1)

    @pl.when((gy > 0) & (gy % 2 == 1))
    def _():
        y_side(ry0, 0)

    @pl.when((gy > 0) & (gy % 2 == 0))
    def _():
        y_side(ry1, 0)

    @pl.when((gy < NDEV - 1) & (gy % 2 == 1))
    def _():
        y_side(ry1, 1)

    @pl.when((gy < NDEV - 1) & (gy % 2 == 0))
    def _():
        y_side(ry0, 1)


def first_edge_kernel(where_ref, part_ref, speed_ref, rx0, rx1, ry0, ry1, one_ref, sx0, sx1, sy0, sy1):
    del part_ref
    gx = where_ref[0]
    gy = where_ref[1]

    def add(x, rows, term):
        one_ref[0, x, rows, :] = one_ref[0, x, rows, :] + speed_ref[0, x, rows, :] * term

    add_halos(rx0, rx1, ry0, ry1, gx, gy, add)
    emit_faces(
        lambda side: one_ref[0, 28 * side : 28 * side + 4],
        lambda side: one_ref[0, :, 28 * side : 28 * side + 4, :],
        gx, gy, sx0, sx1, sy0, sy1,
    )


def swap_granules(vals):
    granule = lax.broadcasted_iota(jnp.int32, vals[0].shape, 1) // 16
    vals = list(vals)
    for bit in (1, 2, 4):
        mask = (granule & bit) != 0
        for i in range(8):
            if i & bit:
                continue
            low, high = vals[i], vals[i + bit]
            vals[i] = jnp.where(mask, pltpu.roll(high, 16 * bit, 1), low)
            vals[i + bit] = jnp.where(mask, high, pltpu.roll(low, 128 - 16 * bit, 1))
    return vals


def second_edge_kernel(
    where_ref, at_ref, part_ref, image_in, begun_ref, speed_ref, forward_ref, rx0, rx1, ry0, ry1,
    two_ref, image_ref, out_ref, done_hbm, sem,
):
    del part_ref, image_in, begun_ref
    gx = where_ref[0]
    gy = where_ref[1]

    def add(x, rows, term):
        change = speed_ref[0, x, rows, :] * term
        two_ref[0, x, rows, :] = two_ref[0, x, rows, :] + change
        image_ref[0, x, rows, :] = image_ref[0, x, rows, :] + forward_ref[0, 1, x, rows, :] * change

    add_halos(rx0, rx1, ry0, ry1, gx, gy, add)
    copy = pltpu.make_async_copy(two_ref, done_hbm, sem)
    copy.start()

    def column(tx, carry):
        for pair in range(2):
            for zv in range(4):
                pieces = swap_granules(
                    [
                        image_ref[0, 8 * tx + x, 16 * pair : 16 * pair + 16, 128 * zv : 128 * zv + 128].astype(BF16)
                        for x in range(8)
                    ]
                )
                for p in range(8):
                    for half in range(2):
                        at = at_ref[tx * 128 + (2 * pair + half) * 32 + zv * 8 + p]
                        out_ref[at] = pieces[p][8 * half : 8 * half + 4]
                        out_ref[at + 1] = pieces[p][8 * half + 4 : 8 * half + 8]
        return carry

    lax.fori_loop(0, 4, column, 0)
    copy.wait()


def owner_kernel(in_ref, grad_ref, rows, ids, spread):
    def unpack(j, carry):
        halves = []
        for b in range(2):
            source = 2 * j + b
            for k in range(CAP):
                rows[source * CAP + k, 0:4, :] = in_ref[source * SLABS + 2 * k].astype(F32)
                rows[source * CAP + k, 4:8, :] = in_ref[source * SLABS + 2 * k + 1].astype(F32)
            halves.append(in_ref[source * SLABS + 8].astype(F32))
        ids[pl.ds(8 * j, 8), :] = jnp.concatenate(halves, axis=0)
        return carry

    lax.fori_loop(0, OWNERS // 2, unpack, 0)
    slot = lax.broadcasted_iota(jnp.int32, (OWNERS * CAP, 128), 1).astype(F32)
    onehot = jnp.where(ids[...] == slot, 1.0, 0.0).astype(BF16)
    for y in range(8):
        spread[:, 128 * y : 128 * y + 128] = lax.dot_general(
            onehot, rows[:, y, :].astype(BF16), (((0,), (0,)), ((), ())), preferred_element_type=F32
        )
    for t in range(16):
        at = slice(8 * t, 8 * t + 8)
        vals = swap_granules([spread[at, 128 * y : 128 * y + 128] for y in range(8)])
        for x in range(8):
            grad_ref[at, 128 * x : 128 * x + 128] = vals[x]


SMEM = pl.BlockSpec(memory_space=pltpu.SMEM)
HBM = pl.BlockSpec(memory_space=pl.ANY)
VMEM = pl.BlockSpec(memory_space=pltpu.VMEM)


def params(mib):
    return pltpu.CompilerParams(vmem_limit_bytes=mib * MIB)


def near(array):
    return pltpu.with_memory_space_constraint(array, pltpu.VMEM)


def per_device(
    adjoint_prev, adjoint_now, speed_term, adjoint_source, forward_accel, footprint, live_counts
):
    place = jnp.stack([lax.axis_index("gx"), lax.axis_index("gy")]).astype(jnp.int32)
    faces_out = [pltpu.VMEM((4, CY, CZ), BF16)] * 2 + [pltpu.VMEM((CX, 4, CZ), BF16)] * 2
    level = pltpu.VMEM((1, CX, CY, CZ), F32)
    final = jax.ShapeDtypeStruct((1, CX, CY, CZ), F32)
    begun = pltpu.VMEM((OWNERS * SLABS, 4, 128), BF16)
    ext = pltpu.VMEM((CX + 8, CY + 16, CZ), F32)
    depth = pltpu.VMEM((CX, CY, CZ), F32)

    send = pl.pallas_call(
        face_kernel,
        in_specs=[SMEM, HBM],
        out_specs=[VMEM] * 4,
        out_shape=faces_out,
        scratch_shapes=[
            pltpu.VMEM((2, 4, CY, CZ), F32), pltpu.VMEM((2, CX, 8, CZ), F32), pltpu.SemaphoreType.DMA((4,)),
        ],
        compiler_params=params(8),
        name="faces",
    )(place, adjoint_now)
    faces = swap_faces(*send)
    now = near(adjoint_now)
    prev = near(adjoint_prev)
    speed = near(speed_term)
    source = near(adjoint_source)
    forward = near(forward_accel)
    high, low = [near(jnp.asarray(term)) for term in depth_band()]
    part_one, outgoing, at = pl.pallas_call(
        first_kernel,
        in_specs=[SMEM, SMEM] + [VMEM] * 6,
        out_specs=[VMEM, VMEM, SMEM],
        out_shape=[level, begun, jax.ShapeDtypeStruct((SUB,), jnp.int32)],
        scratch_shapes=[ext, depth, pltpu.VMEM((OWNERS, CAP, 128), F32), pltpu.SMEM((OWNERS,), jnp.int32)],
        compiler_params=params(12),
        name="level_one",
    )(footprint.reshape(-1), live_counts.reshape(-1), now, prev, speed, source, high, low)
    whole_one, *send = pl.pallas_call(
        first_edge_kernel,
        in_specs=[SMEM] + [VMEM] * 6,
        out_specs=[VMEM] * 5,
        out_shape=[level] + faces_out,
        input_output_aliases={1: 0},
        compiler_params=params(4),
        name="level_one_edge",
    )(place, part_one, speed, *[near(face) for face in faces])
    faces = swap_faces(*send)
    level_one, part_two, image = pl.pallas_call(
        second_kernel,
        in_specs=[VMEM] * 7,
        out_specs=[HBM, VMEM, VMEM],
        out_shape=[final, level, level],
        scratch_shapes=[ext, depth, pltpu.SemaphoreType.DMA],
        compiler_params=params(12),
        name="level_two",
    )(whole_one, now, speed, source, forward, high, low)
    _, _, outgoing, level_two = pl.pallas_call(
        second_edge_kernel,
        in_specs=[SMEM, SMEM] + [VMEM] * 9,
        out_specs=[VMEM, VMEM, VMEM, HBM],
        out_shape=[level, level, begun, final],
        scratch_shapes=[pltpu.SemaphoreType.DMA],
        input_output_aliases={2: 0, 3: 1, 4: 2},
        compiler_params=params(4),
        name="level_two_edge",
    )(place, at, part_two, image, outgoing, speed, forward, *[near(face) for face in faces])
    incoming = lax.all_to_all(outgoing, ("shot", "gx", "gy"), split_axis=0, concat_axis=0, tiled=True)
    gradient = pl.pallas_call(
        owner_kernel,
        in_specs=[VMEM],
        out_specs=VMEM,
        out_shape=jax.ShapeDtypeStruct((OWNERS, 1024), F32),
        scratch_shapes=[
            pltpu.VMEM((OWNERS * CAP, 8, 128), F32),
            pltpu.VMEM((OWNERS * CAP, 128), F32),
            pltpu.VMEM((OWNERS, 1024), F32),
        ],
        compiler_params=params(8),
        name="owner_sum",
    )(near(incoming))
    return (level_one, level_two, gradient)


def solution(mesh):
    return jax.shard_map(
        per_device,
        mesh=mesh,
        in_specs=(
            P("shot", "gx", "gy", None),
            P("shot", "gx", "gy", None),
            P("shot", "gx", "gy", None),
            P("shot", None, "gx", "gy", None),
            P("shot", None, "gx", "gy", None),
            P("shot", "gx", "gy", None),
            P("shot", "gx", "gy"),
        ),
        out_specs=(
            P("shot", "gx", "gy", None),
            P("shot", "gx", "gy", None),
            P(("shot", "gx", "gy"), None),
        ),
        check_vma=False,
    )
```

time: 187 us -> 82.1 us (0.44)
  other arithmetic: 54.9 us -> 0.08 us
  starting transfers between devices: 58.3 us -> 15.8 us
  local copies, waits for them, and re-layouts: 40 us -> 9.2 us
  blocking collectives: 0 us -> 27.9 us
  waiting for transfers between devices: 29.9 us -> 2 us
  Pallas kernels: 0 us -> 25.3 us
    all_to_all x2 -> x0, starting transfers between devices: 30.8 us -> none  [the longest x1 21 us: per_device(): lax.all_to_all(sent_ids, ('shot', 'gx', 'gy'), split_axis=0, concat_axis=...]
    add x2 -> x0, other arithmetic: 30.3 us -> none  [the longest x1 19.3 us: per_device(): imaging = forward[0] * stepped_one + forward[1] * stepped_two]
    all_to_all x0 -> x1, blocking collectives: none -> 27.9 us  [per_device(): lax.all_to_all(outgoing, ('shot', 'gx', 'gy'), split_axis=0, concat_axis=...]
    pallas_call x0 -> x6, Pallas kernels: none -> 25.3 us  [the longest x1 10.5 us: per_device(): pl.pallas_call(first_kernel, in_specs=[SMEM, SMEM] + [VMEM] * 6, out_spec...]
    reshape x5 -> x0, local copies, waits for them, and re-layouts: 20.1 us -> none  [the longest x1 9.59 us: per_device(): imaging.reshape(cells_wide // TX, TX, cells_long // TY, TY, cells_deep //...]
    concatenate x6 -> x0, other arithmetic: 19.8 us -> none  [padded_2(): block = jnp.concatenate([low, block, high], axis=dim)]
    all_to_all x2 -> x0, waiting for transfers between devices: 17.6 us -> none  [the longest x1 17.6 us: per_device(): lax.all_to_all(outgoing, ('shot', 'gx', 'gy'), split_axis=0, concat_axis=...]
    ppermute x8, starting transfers between devices: 27.6 us -> 15.8 us  [the longest x2 5.98 us: swap_faces(): lax.ppermute(y1, 'gy', SWAP_B)]
  transfers between devices with their start and end apart: 10 -> 8, of which waited for: 5 -> 1; matrix products, arithmetic and copies ran while one was open for 38% -> 0% of each run, Pallas kernels for 0% -> 20%
where the time goes in v2:
time: 82.1 us; the launch traced here: 81.8 us
  blocking collectives  27.9 us (34%)
  Pallas kernels  25.3 us (31%)
  starting transfers between devices  15.8 us (19%)
  local copies, waits for them, and re-layouts  9.2 us (11%)
  waiting for transfers between devices  2 us (2%)
  between operations  1.45 us (2%)
    all_to_all x1, blocking collectives, per_device(): lax.all_to_all(outgoing, ('shot', 'gx', 'gy'), split_axis=0, concat_axis=...  27.9 us
    pallas_call x1, Pallas kernels, per_device(): pl.pallas_call(first_kernel, in_specs=[SMEM, SMEM] + [VMEM] * 6, out_spec...  10.5 us
    unnamed x24, local copies, waits for them, and re-layouts  9.2 us
    pallas_call x1, Pallas kernels, per_device(): pl.pallas_call(second_kernel, in_specs=[VMEM] * 7, out_specs=[HBM, VMEM,...  6.02 us
    ppermute x2, starting transfers between devices, swap_faces(): lax.ppermute(y1, 'gy', SWAP_B)  5.98 us
    pallas_call x1, Pallas kernels, per_device(): pl.pallas_call(owner_kernel, in_specs=[VMEM], out_specs=VMEM, out_shape=j...  4.04 us
    ppermute x2, starting transfers between devices, swap_faces(): lax.ppermute(y0, 'gy', SWAP_A)  3.83 us
    ppermute x2, starting transfers between devices, swap_faces(): lax.ppermute(x1, 'gx', SWAP_B)  3.79 us
  transfers between devices with their start and end apart: 8, of which 1 were waited for; matrix products, arithmetic and copies ran while one was open for 0% of the time, Pallas kernels for 20%

profile of v2, /device:TPU:1, one launch (start us, length us, event | category | flops | bytes accessed | tf_op | source)
XLA Modules:
  0.0 81.8 jit_solution(12836590738264449340)
XLA Ops:
  0.6 0.1 pad_add_fusion.where_ref
  0.7 1.7 %copy-done.1 = f32[1,32,32,512]{3,2,1,0:T(8,128)S(1)} copy-done((f32[1,32,32,512]{3,2,1,0:T(8,128)S(1)}, f32[1,32,32,512]{3,2,1,0:T(8,128)}, u32[]{:S(2)}) %copy-start.1) | copy-done | bytes 2097176
  2.4 0.8 faces.1
  3.3 2.1 %collective-permute-start = (bf16[4,32,512]{2,1,0:T(8,128)(2,1)S(1)}, bf16[4,32,512]{2,1,0:T(8,128)(2,1)S(1)}, u32[]{:S(2)}, u32[]{:S(2)}) collective-permute-start(bf16[4,32,512]{2,1,0:T(8,128)(2,1)S(1)} %get-tuple-element.21), channel_id=1, source_target_pairs={{0,8},{8,0},{16,24},{24,16},{32,40},{40,32},{48,56},{56,48},{1,9},... | collective-permute-start | bytes 393224 | tf_op jit(solution)/shard_map/ppermute | solution.py:40
  5.4 2.8 %collective-permute-start.1 = (bf16[4,32,512]{2,1,0:T(8,128)(2,1)S(1)}, bf16[4,32,512]{2,1,0:T(8,128)(2,1)S(1)}, u32[]{:S(2)}, u32[]{:S(2)}) collective-permute-start(bf16[4,32,512]{2,1,0:T(8,128)(2,1)S(1)} %get-tuple-element.22), channel_id=1, source_target_pairs={{0,56},{8,16},{16,8},{24,32},{32,24},{40,48},{48,40},{56,0},{1,57}... | collective-permute-start | bytes 393224 | tf_op jit(solution)/shard_map/ppermute | solution.py:41
  8.2 2.6 %collective-permute-start.2 = (bf16[32,4,512]{2,1,0:T(4,128)(2,1)S(1)}, bf16[32,4,512]{2,1,0:T(4,128)(2,1)S(1)}, u32[]{:S(2)}, u32[]{:S(2)}) collective-permute-start(bf16[32,4,512]{2,1,0:T(4,128)(2,1)S(1)} %get-tuple-element.23), channel_id=1, source_target_pairs={{0,1},{1,0},{2,3},{3,2},{4,5},{5,4},{6,7},{7,6},{8,9},{9,8},{10,11... | collective-permute-start | bytes 393224 | tf_op jit(solution)/shard_map/ppermute | solution.py:42
  10.8 3.8 %collective-permute-start.3 = (bf16[32,4,512]{2,1,0:T(4,128)(2,1)S(1)}, bf16[32,4,512]{2,1,0:T(4,128)(2,1)S(1)}, u32[]{:S(2)}, u32[]{:S(2)}) collective-permute-start(bf16[32,4,512]{2,1,0:T(4,128)(2,1)S(1)} %get-tuple-element.24), channel_id=1, source_target_pairs={{0,7},{1,2},{2,1},{3,4},{4,3},{5,6},{6,5},{7,0},{8,15},{9,10},{10,... | collective-permute-start | bytes 393224 | tf_op jit(solution)/shard_map/ppermute | solution.py:43
  15.3 0.0 copy-start.2
  15.3 1.6 %copy-done.2 = f32[1,32,32,512]{3,2,1,0:T(8,128)S(1)} copy-done((f32[1,32,32,512]{3,2,1,0:T(8,128)S(1)}, f32[1,32,32,512]{3,2,1,0:T(8,128)}, u32[]{:S(2)}) %copy-start.2) | copy-done | bytes 2097176
  16.9 2.2 %copy-done.3 = f32[1,2,32,32,512]{4,3,2,1,0:T(8,128)S(1)} copy-done((f32[1,2,32,32,512]{4,3,2,1,0:T(8,128)S(1)}, f32[1,2,32,32,512]{4,3,2,1,0:T(8,128)}, u32[]{:S(2)}) %copy-start.3) | copy-done | bytes 4194328
  19.1 1.6 %copy-done.6 = f32[1,32,32,512]{3,2,1,0:T(8,128)S(1)} copy-done((f32[1,32,32,512]{3,2,1,0:T(8,128)S(1)}, f32[1,32,32,512]{3,2,1,0:T(8,128)}, u32[]{:S(2)}) %copy-start.6) | copy-done | bytes 2097176
  20.7 1.0 %copy-done.7 = bf16[512,512]{1,0:T(8,128)(2,1)S(1)} copy-done((bf16[512,512]{1,0:T(8,128)(2,1)S(1)}, bf16[512,512]{1,0:T(8,128)(2,1)}, u32[]{:S(2)}) %copy-start.7) | copy-done | bytes 524312
  21.7 1.0 %copy-done.9 = bf16[512,512]{1,0:T(8,128)(2,1)S(1)} copy-done((bf16[512,512]{1,0:T(8,128)(2,1)S(1)}, bf16[512,512]{1,0:T(8,128)(2,1)}, u32[]{:S(2)}) %copy-start.9) | copy-done | bytes 524312
  22.8 10.5 %level_one.1 = (f32[1,32,32,512]{3,2,1,0:T(8,128)S(1)}, bf16[1152,4,128]{2,1,0:T(4,128)(2,1)S(1)}, s32[512]{0:T(512)S(1)}) custom-call(s32[512]{0:T(512)S(1)} %bitcast.5, s32[1]{0:T(128)} %bitcast.4.live_ref, f32[1,32,32,512]{3,2,1,0:T(8,128)S(1)} %copy-done.2, f32[1,32,32,512]{3,2,1,0:T(8,128)S(1)} %copy-done.6, f32[1,32,32,512]{3,2,1,0:T(8,128)S(1)} %copy-done, ...), custom_call_target="tpu_custom_call" | custom-call | tf_op jit(solution)/shard_map/level_one/pallas_call | solution.py:391
  33.3 0.0 collective-permute-done.rx0
  33.3 0.0 collective-permute-done.1.rx1
  33.3 0.0 collective-permute-done.2.ry0
  33.3 0.0 collective-permute-done.3.ry1
  33.3 0.0 copy-start.4
  33.3 0.0 copy-start.8
  33.3 1.3 %level_one_edge.1 = (f32[1,32,32,512]{3,2,1,0:T(8,128)S(1)}, bf16[4,32,512]{2,1,0:T(8,128)(2,1)S(1)}, bf16[4,32,512]{2,1,0:T(8,128)(2,1)S(1)}, bf16[32,4,512]{2,1,0:T(4,128)(2,1)S(1)}, bf16[32,4,512]{2,1,0:T(4,128)(2,1)S(1)}) custom-call(s32[2]{0:T(128)S(1)} %pad_add_fusion.where_ref, ...), custom_call_target="tpu_custom_call", output_to_operand_aliasing={{0}: (1, {})} | custom-call | tf_op jit(solution)/shard_map/level_one_edge/pallas_call | solution.py:400
  34.7 0.1 collective-permute-start.4
  34.7 1.0 %collective-permute-start.5 = (bf16[4,32,512]{2,1,0:T(8,128)(2,1)S(1)}, bf16[4,32,512]{2,1,0:T(8,128)(2,1)S(1)}, u32[]{:S(2)}, u32[]{:S(2)}) collective-permute-start(bf16[4,32,512]{2,1,0:T(8,128)(2,1)S(1)} %get-tuple-element.32), channel_id=1, source_target_pairs={{0,56},{8,16},{16,8},{24,32},{32,24},{40,48},{48,40},{56,0},{1,57}... | collective-permute-start | bytes 393224 | tf_op jit(solution)/shard_map/ppermute | solution.py:41
  35.7 1.2 %collective-permute-start.6 = (bf16[32,4,512]{2,1,0:T(4,128)(2,1)S(1)}, bf16[32,4,512]{2,1,0:T(4,128)(2,1)S(1)}, u32[]{:S(2)}, u32[]{:S(2)}) collective-permute-start(bf16[32,4,512]{2,1,0:T(4,128)(2,1)S(1)} %get-tuple-element.33), channel_id=1, source_target_pairs={{0,1},{1,0},{2,3},{3,2},{4,5},{5,4},{6,7},{7,6},{8,9},{9,8},{10,11... | collective-permute-start | bytes 393224 | tf_op jit(solution)/shard_map/ppermute | solution.py:42
  36.9 2.2 %collective-permute-start.7 = (bf16[32,4,512]{2,1,0:T(4,128)(2,1)S(1)}, bf16[32,4,512]{2,1,0:T(4,128)(2,1)S(1)}, u32[]{:S(2)}, u32[]{:S(2)}) collective-permute-start(bf16[32,4,512]{2,1,0:T(4,128)(2,1)S(1)} %get-tuple-element.34), channel_id=1, source_target_pairs={{0,7},{1,2},{2,1},{3,4},{4,3},{5,6},{6,5},{7,0},{8,15},{9,10},{10,... | collective-permute-start | bytes 393224 | tf_op jit(solution)/shard_map/ppermute | solution.py:43
  39.1 6.0 %level_two.1 = (f32[1,32,32,512]{3,2,1,0:T(8,128)}, f32[1,32,32,512]{3,2,1,0:T(8,128)S(1)}, f32[1,32,32,512]{3,2,1,0:T(8,128)S(1)}) custom-call(f32[1,32,32,512]{3,2,1,0:T(8,128)S(1)} %get-tuple-element.25.one_ref, f32[1,32,32,512]{3,2,1,0:T(8,128)S(1)} %copy-done.2, f32[1,32,32,512]{3,2,1,0:T(8,128)S(1)} %copy-done, f32[1,2,32,32,512]{4,3,2,1,0:T(8,128)S(1)} %copy-done.4, ...), custom_call_target="tpu_custom_call" | custom-call | tf_op jit(solution)/shard_map/level_two/pallas_call | solution.py:410
  45.1 0.0 collective-permute-done.4.rx0
  45.1 0.0 collective-permute-done.5.rx1
  45.2 2.0 %collective-permute-done.7.ry1 = bf16[32,4,512]{2,1,0:T(4,128)(2,1)S(1)} collective-permute-done((bf16[32,4,512]{2,1,0:T(4,128)(2,1)S(1)}, bf16[32,4,512]{2,1,0:T(4,128)(2,1)S(1)}, u32[]{:S(2)}, u32[]{:S(2)}) %collective-permute-start.7) | collective-permute-done | bytes 131104 | tf_op jit(solution)/shard_map/ppermute | solution.py:43
  47.1 2.7 %level_two_edge.1 = (f32[1,32,32,512]{3,2,1,0:T(8,128)S(1)}, f32[1,32,32,512]{3,2,1,0:T(8,128)S(1)}, bf16[1152,4,128]{2,1,0:T(4,128)(2,1)S(1)}, f32[1,32,32,512]{3,2,1,0:T(8,128)}) custom-call(s32[2]{0:T(128)S(1)} %pad_add_fusion.where_ref, s32[512]{0:T(512)S(1)} %get-tuple-element.27.at_ref, ...), custom_call_target="tpu_custom_call", output_to_operand_aliasing={{0}: (2, {}), {1}: (3, {}), {2}: (4, {})} | custom-call | tf_op jit(solution)/shard_map/level_two_edge/pallas_call | solution.py:419
  49.8 27.9 %all_to_all.5.in_ref = bf16[1152,4,128]{2,1,0:T(4,128)(2,1)S(1)} all-to-all(bf16[1152,4,128]{2,1,0:T(4,128)(2,1)S(1)} %get-tuple-element.36), channel_id=1, replica_groups=mesh['shot'=2,'gx'=8,'gy'=8] {'shot','gx','gy'}, dimensions={0} | all-to-all | bytes 2359296 | tf_op jit(solution)/shard_map/all_to_all | solution.py:429
  77.8 4.0 %owner_sum.1 = f32[128,1024]{1,0:T(8,128)} custom-call(bf16[1152,4,128]{2,1,0:T(4,128)(2,1)S(1)} %all_to_all.5.in_ref), custom_call_target="tpu_custom_call" | custom-call | tf_op jit(solution)/shard_map/owner_sum/pallas_call | solution.py:430
  (16 shorter events, 0.0 us)
Async XLA Ops:
  0.6 14.7 %copy-start = (f32[1,32,32,512]{3,2,1,0:T(8,128)S(1)}, f32[1,32,32,512]{3,2,1,0:T(8,128)}, u32[]{:S(2)}) copy-start(f32[1,32,32,512]{3,2,1,0:T(8,128)} %speed_ref.7) | copy-start | bytes 6291460
  0.7 1.7 %copy-start.1 = (f32[1,32,32,512]{3,2,1,0:T(8,128)S(1)}, f32[1,32,32,512]{3,2,1,0:T(8,128)}, u32[]{:S(2)}) copy-start(f32[1,32,32,512]{3,2,1,0:T(8,128)} %now_ref.3) | copy-start | bytes 6291460
  2.4 12.9 %copy-start.11 = (s32[1,1,1,512]{3,2,1,0:T(1,128)S(1)}, s32[1,1,1,512]{3,2,1,0:T(1,128)}, u32[]{:S(2)}) copy-start(s32[1,1,1,512]{3,2,1,0:T(1,128)} %param.14) | copy-start | bytes 6148
  3.3 30.0 %collective-permute-start = (bf16[4,32,512]{2,1,0:T(8,128)(2,1)S(1)}, bf16[4,32,512]{2,1,0:T(8,128)(2,1)S(1)}, u32[]{:S(2)}, u32[]{:S(2)}) collective-permute-start(bf16[4,32,512]{2,1,0:T(8,128)(2,1)S(1)} %get-tuple-element.21), channel_id=1, source_target_pairs={{0,8},{8,0},{16,24},{24,16},{32,40},{40,32},{48,56},{56,48},{1,9},... | collective-permute-start | bytes 393224 | tf_op jit(solution)/shard_map/ppermute | solution.py:40
  5.4 27.9 %collective-permute-start.1 = (bf16[4,32,512]{2,1,0:T(8,128)(2,1)S(1)}, bf16[4,32,512]{2,1,0:T(8,128)(2,1)S(1)}, u32[]{:S(2)}, u32[]{:S(2)}) collective-permute-start(bf16[4,32,512]{2,1,0:T(8,128)(2,1)S(1)} %get-tuple-element.22), channel_id=1, source_target_pairs={{0,56},{8,16},{16,8},{24,32},{32,24},{40,48},{48,40},{56,0},{1,57}... | collective-permute-start | bytes 393224 | tf_op jit(solution)/shard_map/ppermute | solution.py:41
  8.2 25.1 %collective-permute-start.2 = (bf16[32,4,512]{2,1,0:T(4,128)(2,1)S(1)}, bf16[32,4,512]{2,1,0:T(4,128)(2,1)S(1)}, u32[]{:S(2)}, u32[]{:S(2)}) collective-permute-start(bf16[32,4,512]{2,1,0:T(4,128)(2,1)S(1)} %get-tuple-element.23), channel_id=1, source_target_pairs={{0,1},{1,0},{2,3},{3,2},{4,5},{5,4},{6,7},{7,6},{8,9},{9,8},{10,11... | collective-permute-start | bytes 393224 | tf_op jit(solution)/shard_map/ppermute | solution.py:42
  10.8 22.5 %collective-permute-start.3 = (bf16[32,4,512]{2,1,0:T(4,128)(2,1)S(1)}, bf16[32,4,512]{2,1,0:T(4,128)(2,1)S(1)}, u32[]{:S(2)}, u32[]{:S(2)}) collective-permute-start(bf16[32,4,512]{2,1,0:T(4,128)(2,1)S(1)} %get-tuple-element.24), channel_id=1, source_target_pairs={{0,7},{1,2},{2,1},{3,4},{4,3},{5,6},{6,5},{7,0},{8,15},{9,10},{10,... | collective-permute-start | bytes 393224 | tf_op jit(solution)/shard_map/ppermute | solution.py:43
  15.3 1.6 %copy-start.2 = (f32[1,32,32,512]{3,2,1,0:T(8,128)S(1)}, f32[1,32,32,512]{3,2,1,0:T(8,128)}, u32[]{:S(2)}) copy-start(f32[1,32,32,512]{3,2,1,0:T(8,128)} %now_ref.3) | copy-start | bytes 6291460
  16.9 2.2 %copy-start.3 = (f32[1,2,32,32,512]{4,3,2,1,0:T(8,128)S(1)}, f32[1,2,32,32,512]{4,3,2,1,0:T(8,128)}, u32[]{:S(2)}) copy-start(f32[1,2,32,32,512]{4,3,2,1,0:T(8,128)} %source_ref.3) | copy-start | bytes 12582916
  19.1 1.6 %copy-start.6 = (f32[1,32,32,512]{3,2,1,0:T(8,128)S(1)}, f32[1,32,32,512]{3,2,1,0:T(8,128)}, u32[]{:S(2)}) copy-start(f32[1,32,32,512]{3,2,1,0:T(8,128)} %prev_ref.1) | copy-start | bytes 6291460
  20.7 1.0 %copy-start.7 = (bf16[512,512]{1,0:T(8,128)(2,1)S(1)}, bf16[512,512]{1,0:T(8,128)(2,1)}, u32[]{:S(2)}) copy-start(bf16[512,512]{1,0:T(8,128)(2,1)} %constant.12.clone.low_ref) | copy-start | bytes 1572868
  21.7 1.0 %copy-start.9 = (bf16[512,512]{1,0:T(8,128)(2,1)S(1)}, bf16[512,512]{1,0:T(8,128)(2,1)}, u32[]{:S(2)}) copy-start(bf16[512,512]{1,0:T(8,128)(2,1)} %constant.11.clone.high_ref) | copy-start | bytes 1572868
  22.8 16.3 %copy-start.5 = (f32[1,2,32,32,512]{4,3,2,1,0:T(8,128)S(1)}, f32[1,2,32,32,512]{4,3,2,1,0:T(8,128)}, u32[]{:S(2)}) copy-start(f32[1,2,32,32,512]{4,3,2,1,0:T(8,128)} %forward_ref.3) | copy-start | bytes 12582916
  22.8 16.3 %copy-start.10 = (bf16[512,512]{1,0:T(8,128)(2,1)S(1)}, bf16[512,512]{1,0:T(8,128)(2,1)}, u32[]{:S(2)}) copy-start(bf16[512,512]{1,0:T(8,128)(2,1)} %constant.11.clone.high_ref) | copy-start | bytes 1572868
  33.3 5.8 %copy-start.4 = (f32[1,2,32,32,512]{4,3,2,1,0:T(8,128)S(1)}, f32[1,2,32,32,512]{4,3,2,1,0:T(8,128)}, u32[]{:S(2)}) copy-start(f32[1,2,32,32,512]{4,3,2,1,0:T(8,128)} %source_ref.3) | copy-start | bytes 12582916
  33.3 5.8 %copy-start.8 = (bf16[512,512]{1,0:T(8,128)(2,1)S(1)}, bf16[512,512]{1,0:T(8,128)(2,1)}, u32[]{:S(2)}) copy-start(bf16[512,512]{1,0:T(8,128)(2,1)} %constant.12.clone.low_ref) | copy-start | bytes 1572868
  34.7 10.5 %collective-permute-start.4 = (bf16[4,32,512]{2,1,0:T(8,128)(2,1)S(1)}, bf16[4,32,512]{2,1,0:T(8,128)(2,1)S(1)}, u32[]{:S(2)}, u32[]{:S(2)}) collective-permute-start(bf16[4,32,512]{2,1,0:T(8,128)(2,1)S(1)} %get-tuple-element.31), channel_id=1, source_target_pairs={{0,8},{8,0},{16,24},{24,16},{32,40},{40,32},{48,56},{56,48},{1,9},... | collective-permute-start | bytes 393224 | tf_op jit(solution)/shard_map/ppermute | solution.py:40
  34.7 10.4 %collective-permute-start.5 = (bf16[4,32,512]{2,1,0:T(8,128)(2,1)S(1)}, bf16[4,32,512]{2,1,0:T(8,128)(2,1)S(1)}, u32[]{:S(2)}, u32[]{:S(2)}) collective-permute-start(bf16[4,32,512]{2,1,0:T(8,128)(2,1)S(1)} %get-tuple-element.32), channel_id=1, source_target_pairs={{0,56},{8,16},{16,8},{24,32},{32,24},{40,48},{48,40},{56,0},{1,57}... | collective-permute-start | bytes 393224 | tf_op jit(solution)/shard_map/ppermute | solution.py:41
  35.7 9.4 %collective-permute-start.6 = (bf16[32,4,512]{2,1,0:T(4,128)(2,1)S(1)}, bf16[32,4,512]{2,1,0:T(4,128)(2,1)S(1)}, u32[]{:S(2)}, u32[]{:S(2)}) collective-permute-start(bf16[32,4,512]{2,1,0:T(4,128)(2,1)S(1)} %get-tuple-element.33), channel_id=1, source_target_pairs={{0,1},{1,0},{2,3},{3,2},{4,5},{5,4},{6,7},{7,6},{8,9},{9,8},{10,11... | collective-permute-start | bytes 393224 | tf_op jit(solution)/shard_map/ppermute | solution.py:42
  36.9 10.2 %collective-permute-start.7 = (bf16[32,4,512]{2,1,0:T(4,128)(2,1)S(1)}, bf16[32,4,512]{2,1,0:T(4,128)(2,1)S(1)}, u32[]{:S(2)}, u32[]{:S(2)}) collective-permute-start(bf16[32,4,512]{2,1,0:T(4,128)(2,1)S(1)} %get-tuple-element.34), channel_id=1, source_target_pairs={{0,7},{1,2},{2,1},{3,4},{4,3},{5,6},{6,5},{7,0},{8,15},{9,10},{10,... | collective-permute-start | bytes 393224 | tf_op jit(solution)/shard_map/ppermute | solution.py:43

commit v3 on v2

--- a/solution.py
+++ b/solution.py
@@ -20,6 +20,7 @@
 
 F32 = jnp.float32
 BF16 = jnp.bfloat16
+FACES_FLOPS = 10_000_000_000
 MIB = 1024 * 1024
 
 SWAP_A = [(i, i ^ 1) for i in range(NDEV)]
@@ -72,40 +73,38 @@
     copies = [
         pltpu.make_async_copy(now_hbm.at[0, 0:4], xs.at[0], sems.at[0]),
         pltpu.make_async_copy(now_hbm.at[0, 28:32], xs.at[1], sems.at[1]),
-        pltpu.make_async_copy(now_hbm.at[0, :, 0:8, :], ys.at[0], sems.at[2]),
-        pltpu.make_async_copy(now_hbm.at[0, :, 24:32, :], ys.at[1], sems.at[3]),
+        pltpu.make_async_copy(now_hbm.at[0, :, 0:4, :], ys.at[0], sems.at[2]),
+        pltpu.make_async_copy(now_hbm.at[0, :, 28:32, :], ys.at[1], sems.at[3]),
     ]
     for copy in copies:
         copy.start()
     for copy in copies:
         copy.wait()
     emit_faces(
-        lambda side: xs[side], lambda side: ys[side, :, 4 * side : 4 * side + 4, :], gx, gy, sx0, sx1, sy0, sy1
-    )
-
-
-def depth_terms(values, high_ref, low_ref, zs):
-    for i in range(4):
-        block = values[0, 8 * i : 8 * i + 8].reshape(8 * CY, CZ)
-        big = block.astype(BF16)
-        small = (block - big.astype(F32)).astype(BF16)
-        term = jnp.dot(big, high_ref[...], preferred_element_type=F32)
-        term = term + jnp.dot(big, low_ref[...], preferred_element_type=F32)
-        term = term + jnp.dot(small, high_ref[...], preferred_element_type=F32)
-        zs[8 * i : 8 * i + 8] = term.reshape(8, CY, CZ)
-
-
-def extend(values, ext):
+        lambda side: xs[side], lambda side: ys[side], gx, gy, sx0, sx1, sy0, sy1
+    )
+
+
+def depth_term(block, high_ref, low_ref):
+    block = block.reshape(8 * CY, CZ)
+    big = block.astype(BF16)
+    small = (block - big.astype(F32)).astype(BF16)
+    term = jnp.dot(big, high_ref[...], preferred_element_type=F32)
+    term = term + jnp.dot(big, low_ref[...], preferred_element_type=F32)
+    term = term + jnp.dot(small, high_ref[...], preferred_element_type=F32)
+    return term.reshape(8, CY, CZ)
+
+
+def clear_edges(ext):
     ext[0:4, 8:40, :] = jnp.zeros((4, CY, CZ), F32)
     ext[36:40, 8:40, :] = jnp.zeros((4, CY, CZ), F32)
 
-    def fill(x, carry):
+    def clear(x, carry):
         ext[x + 4, 0:8, :] = jnp.zeros((8, CZ), F32)
-        ext[x + 4, 8:40, :] = values[0, x]
         ext[x + 4, 40:48, :] = jnp.zeros((8, CZ), F32)
         return carry
 
-    lax.fori_loop(0, CX, fill, 0)
+    lax.fori_loop(0, CX, clear, 0)
 
 
 def laplace_rows(ext, zs, x, ty):
@@ -119,26 +118,40 @@
     return summed, middle
 
 
+def place_pieces(foot_ref, live, odd, at_ref, out_ref):
+    listed = foot_ref[...]
+    owner = listed // OWNERS
+    piece = lax.broadcasted_iota(jnp.int32, (1, SUB), 1)
+    slot = jnp.where(piece < live, listed % OWNERS, -1)
+    match = owner == lax.broadcasted_iota(jnp.int32, (OWNERS, SUB), 0)
+    earlier = lax.broadcasted_iota(jnp.int32, (SUB, SUB), 0) < lax.broadcasted_iota(jnp.int32, (SUB, SUB), 1)
+    ahead = jnp.dot(
+        jnp.where(match, 1.0, 0.0).astype(BF16), jnp.where(earlier, 1.0, 0.0).astype(BF16), preferred_element_type=F32
+    )
+    rank = jnp.sum(jnp.where(match, ahead, 0.0), axis=0, keepdims=True).astype(jnp.int32)
+    at_ref[...] = owner * SLABS + 2 * rank + odd
+    order = owner * CAP + rank
+    chosen = jnp.where(lax.broadcasted_iota(jnp.int32, (SUB, SUB), 0) == order, 1.0, 0.0).astype(BF16)
+    slots = lax.dot_general(
+        chosen, jnp.broadcast_to(slot.astype(F32), (OWNERS, SUB)).astype(BF16), (((1,), (1,)), ((), ())),
+        preferred_element_type=F32,
+    ).astype(BF16)
+    for o in range(OWNERS):
+        out_ref[o * SLABS + jnp.where(odd == 1, 0, SLABS - 1)] = slots[CAP * o : CAP * o + CAP]
+
+
 def first_kernel(
-    foot_ref, live_ref, now_ref, prev_ref, speed_ref, source_ref, high_ref, low_ref,
-    one_ref, out_ref, at_ref, ext, zs, slots, count,
+    where_ref, live_ref, foot_ref, now_ref, prev_ref, source_ref, speed_ref, high_ref, low_ref,
+    one_ref, out_ref, at_ref, ext, zs,
 ):
-    for o in range(OWNERS):
-        count[o] = 0
-    depth_terms(now_ref, high_ref, low_ref, zs)
-    extend(now_ref, ext)
-    live = live_ref[0]
+    place_pieces(foot_ref, live_ref[0], where_ref[1] % 2, at_ref, out_ref)
+    clear_edges(ext)
+    for i in range(4):
+        block = now_ref[0, 8 * i : 8 * i + 8]
+        ext[8 * i + 4 : 8 * i + 12, 8:40, :] = block
+        zs[8 * i : 8 * i + 8] = depth_term(block, high_ref, low_ref)
 
     def plane(x, carry):
-        for j in range(SUB // CX):
-            s = x * (SUB // CX) + j
-            listed = foot_ref[s]
-            owner = listed // OWNERS
-            rank = count[owner]
-            count[owner] = rank + 1
-            at_ref[s] = owner * SLABS + 2 * rank
-            slot = jnp.where(s < live, listed % OWNERS, -1).astype(F32)
-            slots[owner, pl.ds(rank, 1), :] = jnp.full((1, 128), slot, F32)
         for ty in range(4):
             rows = slice(8 * ty, 8 * ty + 8)
             summed, middle = laplace_rows(ext, zs, x, ty)
@@ -150,12 +163,6 @@
 
     lax.fori_loop(0, CX, plane, 0)
 
-    def put(o, carry):
-        out_ref[o * SLABS + 8] = slots[o].astype(BF16)
-        return carry
-
-    lax.fori_loop(0, OWNERS, put, 0)
-
 
 def second_kernel(
     one_ref, now_ref, speed_ref, source_ref, forward_ref, high_ref, low_ref,
@@ -163,8 +170,11 @@
 ):
     copy = pltpu.make_async_copy(one_ref, done_hbm, sem)
     copy.start()
-    depth_terms(one_ref, high_ref, low_ref, zs)
-    extend(one_ref, ext)
+    clear_edges(ext)
+    for i in range(4):
+        block = one_ref[0, 8 * i : 8 * i + 8]
+        ext[8 * i + 4 : 8 * i + 12, 8:40, :] = block
+        zs[8 * i : 8 * i + 8] = depth_term(block, high_ref, low_ref)
 
     def plane(x, carry):
         for ty in range(4):
@@ -311,7 +321,7 @@
                 )
                 for p in range(8):
                     for half in range(2):
-                        at = at_ref[tx * 128 + (2 * pair + half) * 32 + zv * 8 + p]
+                        at = at_ref[0, tx * 128 + (2 * pair + half) * 32 + zv * 8 + p]
                         out_ref[at] = pieces[p][8 * half : 8 * half + 4]
                         out_ref[at + 1] = pieces[p][8 * half + 4 : 8 * half + 8]
         return carry
@@ -320,25 +330,19 @@
     copy.wait()
 
 
-def owner_kernel(in_ref, grad_ref, rows, ids, spread):
+def owner_kernel(in_ref, grad_ref, rows, ids, flat, spread):
     def unpack(j, carry):
-        halves = []
-        for b in range(2):
-            source = 2 * j + b
-            for k in range(CAP):
-                rows[source * CAP + k, 0:4, :] = in_ref[source * SLABS + 2 * k].astype(F32)
-                rows[source * CAP + k, 4:8, :] = in_ref[source * SLABS + 2 * k + 1].astype(F32)
-            halves.append(in_ref[source * SLABS + 8].astype(F32))
-        ids[pl.ds(8 * j, 8), :] = jnp.concatenate(halves, axis=0)
+        for k in range(2 * CAP):
+            rows[8 * j + k] = in_ref[SLABS * j + k + k // CAP].astype(F32)
+        ids[pl.ds(pl.multiple_of(8 * j, 8), 8), :] = in_ref[SLABS * j + CAP].astype(F32)
         return carry
 
-    lax.fori_loop(0, OWNERS // 2, unpack, 0)
+    lax.fori_loop(0, OWNERS // 2, unpack, 0, unroll=4)
     slot = lax.broadcasted_iota(jnp.int32, (OWNERS * CAP, 128), 1).astype(F32)
     onehot = jnp.where(ids[...] == slot, 1.0, 0.0).astype(BF16)
     for y in range(8):
-        spread[:, 128 * y : 128 * y + 128] = lax.dot_general(
-            onehot, rows[:, y, :].astype(BF16), (((0,), (0,)), ((), ())), preferred_element_type=F32
-        )
+        flat[:, 128 * y : 128 * y + 128] = rows[:, y, :].astype(BF16)
+    spread[...] = lax.dot_general(onehot, flat[...], (((0,), (0,)), ((), ())), preferred_element_type=F32)
     for t in range(16):
         at = slice(8 * t, 8 * t + 8)
         vals = swap_granules([spread[at, 128 * y : 128 * y + 128] for y in range(8)])
@@ -347,12 +351,16 @@
 
 
 SMEM = pl.BlockSpec(memory_space=pltpu.SMEM)
-HBM = pl.BlockSpec(memory_space=pl.ANY)
+HBM = pl.BlockSpec(memory_space=pltpu.HBM)
 VMEM = pl.BlockSpec(memory_space=pltpu.VMEM)
 
 
 def params(mib):
     return pltpu.CompilerParams(vmem_limit_bytes=mib * MIB)
+
+
+def far(array):
+    return pltpu.with_memory_space_constraint(array, pltpu.HBM)
 
 
 def near(array):
@@ -376,27 +384,30 @@
         out_specs=[VMEM] * 4,
         out_shape=faces_out,
         scratch_shapes=[
-            pltpu.VMEM((2, 4, CY, CZ), F32), pltpu.VMEM((2, CX, 8, CZ), F32), pltpu.SemaphoreType.DMA((4,)),
+            pltpu.VMEM((2, 4, CY, CZ), F32), pltpu.VMEM((2, CX, 4, CZ), F32), pltpu.SemaphoreType.DMA((4,)),
         ],
         compiler_params=params(8),
+        cost_estimate=pl.CostEstimate(flops=FACES_FLOPS, bytes_accessed=1_000_000, transcendentals=0),
         name="faces",
-    )(place, adjoint_now)
+    )(place, far(adjoint_now))
     faces = swap_faces(*send)
-    now = near(adjoint_now)
-    prev = near(adjoint_prev)
     speed = near(speed_term)
     source = near(adjoint_source)
     forward = near(forward_accel)
+    now = near(adjoint_now)
+    prev = near(adjoint_prev)
     high, low = [near(jnp.asarray(term)) for term in depth_band()]
     part_one, outgoing, at = pl.pallas_call(
         first_kernel,
-        in_specs=[SMEM, SMEM] + [VMEM] * 6,
-        out_specs=[VMEM, VMEM, SMEM],
-        out_shape=[level, begun, jax.ShapeDtypeStruct((SUB,), jnp.int32)],
-        scratch_shapes=[ext, depth, pltpu.VMEM((OWNERS, CAP, 128), F32), pltpu.SMEM((OWNERS,), jnp.int32)],
+        in_specs=[SMEM, SMEM] + [VMEM] * 7,
+        out_specs=[VMEM] * 3,
+        out_shape=[level, begun, jax.ShapeDtypeStruct((1, SUB), jnp.int32)],
+        scratch_shapes=[ext, depth],
         compiler_params=params(12),
         name="level_one",
-    )(footprint.reshape(-1), live_counts.reshape(-1), now, prev, speed, source, high, low)
+    )(
+        place, live_counts.reshape(-1), footprint.reshape(1, SUB), now, prev, source, speed, high, low,
+    )
     whole_one, *send = pl.pallas_call(
         first_edge_kernel,
         in_specs=[SMEM] + [VMEM] * 6,
@@ -435,11 +446,12 @@
         scratch_shapes=[
             pltpu.VMEM((OWNERS * CAP, 8, 128), F32),
             pltpu.VMEM((OWNERS * CAP, 128), F32),
+            pltpu.VMEM((OWNERS * CAP, 1024), BF16),
             pltpu.VMEM((OWNERS, 1024), F32),
         ],
         compiler_params=params(8),
         name="owner_sum",
-    )(near(incoming))
+    )(near(incoming.reshape(OWNERS * SLABS // 2, 8, 128)))
     return (level_one, level_two, gradient)
 
 

time: 82.1 us -> 70.9 us (0.86)
  local copies, waits for them, and re-layouts: 9.2 us -> 0.04 us
  Pallas kernels: 25.3 us -> 22.2 us
  waiting for transfers between devices: 2 us -> 3.86 us
    unnamed x24 -> x16, local copies, waits for them, and re-layouts: 9.2 us -> 0.04 us
    pallas_call x1, Pallas kernels: 10.5 us -> 6.45 us  [per_device(): pl.pallas_call(first_kernel, in_specs=[SMEM, SMEM] + [VMEM] * 7, out_spec...]
    ppermute x2, waiting for transfers between devices: 1.98 us -> 3.84 us  [swap_faces(): lax.ppermute(y1, 'gy', SWAP_B)]
    pallas_call x1, Pallas kernels: 0.81 us -> 2.14 us  [per_device(): pl.pallas_call(face_kernel, in_specs=[SMEM, HBM], out_specs=[VMEM] * 4, o...]
    ppermute x2, starting transfers between devices: 3.79 us -> 2.96 us  [swap_faces(): lax.ppermute(x1, 'gx', SWAP_B)]
  transfers between devices with their start and end apart: 8 -> 8, of which waited for: 1 -> 2; matrix products, arithmetic and copies ran while one was open for 0% -> 0% of each run, Pallas kernels for 20% -> 17%
where the time goes in v3:
time: 70.9 us; the launch traced here: 70.8 us
  blocking collectives  28.2 us (40%)
  Pallas kernels  22.2 us (31%)
  starting transfers between devices  15 us (21%)
  waiting for transfers between devices  3.86 us (5%)
  between operations  1.47 us (2%)
    all_to_all x1, blocking collectives, per_device(): lax.all_to_all(outgoing, ('shot', 'gx', 'gy'), split_axis=0, concat_axis=...  28.2 us
    pallas_call x1, Pallas kernels, per_device(): pl.pallas_call(first_kernel, in_specs=[SMEM, SMEM] + [VMEM] * 7, out_spec...  6.45 us
    ppermute x2, starting transfers between devices, swap_faces(): lax.ppermute(y1, 'gy', SWAP_B)  5.72 us
    pallas_call x1, Pallas kernels, per_device(): pl.pallas_call(second_kernel, in_specs=[VMEM] * 7, out_specs=[HBM, VMEM,...  5.63 us
    ppermute x2, starting transfers between devices, swap_faces(): lax.ppermute(y0, 'gy', SWAP_A)  4.12 us
    pallas_call x1, Pallas kernels, per_device(): pl.pallas_call(owner_kernel, in_specs=[VMEM], out_specs=VMEM, out_shape=j...  4.01 us
    ppermute x2, waiting for transfers between devices, swap_faces(): lax.ppermute(y1, 'gy', SWAP_B)  3.84 us
    ppermute x2, starting transfers between devices, swap_faces(): lax.ppermute(x1, 'gx', SWAP_B)  2.96 us
  transfers between devices with their start and end apart: 8, of which 2 were waited for; matrix products, arithmetic and copies ran while one was open for 0% of the time, Pallas kernels for 17%

profile of v3, /device:TPU:1, one launch (start us, length us, event | category | flops | bytes accessed | tf_op | source)
XLA Modules:
  0.0 70.8 jit_solution(15856458033704870262)
XLA Ops:
  0.6 0.1 pad_add_fusion.where_ref
  0.7 0.0 copy-start.5
  0.7 0.0 copy-start.6
  0.7 0.0 copy-start.7
  0.8 2.1 %faces.1 = (bf16[4,32,512]{2,1,0:T(8,128)(2,1)S(1)}, bf16[4,32,512]{2,1,0:T(8,128)(2,1)S(1)}, bf16[32,4,512]{2,1,0:T(4,128)(2,1)S(1)}, bf16[32,4,512]{2,1,0:T(4,128)(2,1)S(1)}) custom-call(s32[2]{0:T(128)S(1)} %pad_add_fusion.where_ref, f32[1,32,32,512]{3,2,1,0:T(8,128)} %now_ref.3), custom_call_target="tpu_custom_call" | custom-call | flops 10000000000 | bytes 1000000 | tf_op jit(solution)/shard_map/faces/pallas_call | solution.py:381
  2.9 2.1 %collective-permute-start = (bf16[4,32,512]{2,1,0:T(8,128)(2,1)S(1)}, bf16[4,32,512]{2,1,0:T(8,128)(2,1)S(1)}, u32[]{:S(2)}, u32[]{:S(2)}) collective-permute-start(bf16[4,32,512]{2,1,0:T(8,128)(2,1)S(1)} %get-tuple-element.21), channel_id=1, source_target_pairs={{0,8},{8,0},{16,24},{24,16},{32,40},{40,32},{48,56},{56,48},{1,9},... | collective-permute-start | bytes 393224 | tf_op jit(solution)/shard_map/ppermute | solution.py:41
  5.0 2.8 %collective-permute-start.1 = (bf16[4,32,512]{2,1,0:T(8,128)(2,1)S(1)}, bf16[4,32,512]{2,1,0:T(8,128)(2,1)S(1)}, u32[]{:S(2)}, u32[]{:S(2)}) collective-permute-start(bf16[4,32,512]{2,1,0:T(8,128)(2,1)S(1)} %get-tuple-element.22), channel_id=1, source_target_pairs={{0,56},{8,16},{16,8},{24,32},{32,24},{40,48},{48,40},{56,0},{1,57}... | collective-permute-start | bytes 393224 | tf_op jit(solution)/shard_map/ppermute | solution.py:42
  7.9 2.6 %collective-permute-start.2 = (bf16[32,4,512]{2,1,0:T(4,128)(2,1)S(1)}, bf16[32,4,512]{2,1,0:T(4,128)(2,1)S(1)}, u32[]{:S(2)}, u32[]{:S(2)}) collective-permute-start(bf16[32,4,512]{2,1,0:T(4,128)(2,1)S(1)} %get-tuple-element.23), channel_id=1, source_target_pairs={{0,1},{1,0},{2,3},{3,2},{4,5},{5,4},{6,7},{7,6},{8,9},{9,8},{10,11... | collective-permute-start | bytes 393224 | tf_op jit(solution)/shard_map/ppermute | solution.py:43
  10.5 3.8 %collective-permute-start.3 = (bf16[32,4,512]{2,1,0:T(4,128)(2,1)S(1)}, bf16[32,4,512]{2,1,0:T(4,128)(2,1)S(1)}, u32[]{:S(2)}, u32[]{:S(2)}) collective-permute-start(bf16[32,4,512]{2,1,0:T(4,128)(2,1)S(1)} %get-tuple-element.24), channel_id=1, source_target_pairs={{0,7},{1,2},{2,1},{3,4},{4,3},{5,6},{6,5},{7,0},{8,15},{9,10},{10,... | collective-permute-start | bytes 393224 | tf_op jit(solution)/shard_map/ppermute | solution.py:44
  15.0 0.0 copy-done
  15.0 0.0 copy-done.1
  15.0 0.0 copy-done.3
  15.0 0.0 copy-done.4
  15.0 0.0 copy-done.5
  15.0 6.5 %level_one.1 = (f32[1,32,32,512]{3,2,1,0:T(8,128)S(1)}, bf16[1152,4,128]{2,1,0:T(4,128)(2,1)S(1)}, s32[1,512]{1,0:T(1,128)S(1)}) custom-call(s32[2]{0:T(128)S(1)} %pad_add_fusion.where_ref, s32[1]{0:T(128)} %bitcast.5.live_ref, s32[1,512]{1,0:T(1,128)S(1)} %bitcast.7, f32[1,32,32,512]{3,2,1,0:T(8,128)S(1)} %copy-done.3, f32[1,32,32,512]{3,2,1,0:T(8,128)S(1)} %copy-done.4, ...), custom_call_target="tpu_custom_call" | custom-call | tf_op jit(solution)/shard_map/level_one/pallas_call | solution.py:400
  21.5 0.0 collective-permute-done.rx0
  21.5 0.0 collective-permute-done.1.rx1
  21.5 0.0 collective-permute-done.2.ry0
  21.5 2.1 %collective-permute-done.3.ry1 = bf16[32,4,512]{2,1,0:T(4,128)(2,1)S(1)} collective-permute-done((bf16[32,4,512]{2,1,0:T(4,128)(2,1)S(1)}, bf16[32,4,512]{2,1,0:T(4,128)(2,1)S(1)}, u32[]{:S(2)}, u32[]{:S(2)}) %collective-permute-start.3) | collective-permute-done | bytes 131104 | tf_op jit(solution)/shard_map/ppermute | solution.py:44
  23.6 1.3 %level_one_edge.1 = (f32[1,32,32,512]{3,2,1,0:T(8,128)S(1)}, bf16[4,32,512]{2,1,0:T(8,128)(2,1)S(1)}, bf16[4,32,512]{2,1,0:T(8,128)(2,1)S(1)}, bf16[32,4,512]{2,1,0:T(4,128)(2,1)S(1)}, bf16[32,4,512]{2,1,0:T(4,128)(2,1)S(1)}) custom-call(s32[2]{0:T(128)S(1)} %pad_add_fusion.where_ref, ...), custom_call_target="tpu_custom_call", output_to_operand_aliasing={{0}: (1, {})} | custom-call | tf_op jit(solution)/shard_map/level_one_edge/pallas_call | solution.py:411
  24.9 0.1 collective-permute-start.4
  25.0 0.1 collective-permute-start.5
  25.2 1.5 %collective-permute-start.6 = (bf16[32,4,512]{2,1,0:T(4,128)(2,1)S(1)}, bf16[32,4,512]{2,1,0:T(4,128)(2,1)S(1)}, u32[]{:S(2)}, u32[]{:S(2)}) collective-permute-start(bf16[32,4,512]{2,1,0:T(4,128)(2,1)S(1)} %get-tuple-element.33), channel_id=1, source_target_pairs={{0,1},{1,0},{2,3},{3,2},{4,5},{5,4},{6,7},{7,6},{8,9},{9,8},{10,11... | collective-permute-start | bytes 393224 | tf_op jit(solution)/shard_map/ppermute | solution.py:43
  26.7 1.9 %collective-permute-start.7 = (bf16[32,4,512]{2,1,0:T(4,128)(2,1)S(1)}, bf16[32,4,512]{2,1,0:T(4,128)(2,1)S(1)}, u32[]{:S(2)}, u32[]{:S(2)}) collective-permute-start(bf16[32,4,512]{2,1,0:T(4,128)(2,1)S(1)} %get-tuple-element.34), channel_id=1, source_target_pairs={{0,7},{1,2},{2,1},{3,4},{4,3},{5,6},{6,5},{7,0},{8,15},{9,10},{10,... | collective-permute-start | bytes 393224 | tf_op jit(solution)/shard_map/ppermute | solution.py:44
  28.6 5.6 %level_two.1 = (f32[1,32,32,512]{3,2,1,0:T(8,128)}, f32[1,32,32,512]{3,2,1,0:T(8,128)S(1)}, f32[1,32,32,512]{3,2,1,0:T(8,128)S(1)}) custom-call(f32[1,32,32,512]{3,2,1,0:T(8,128)S(1)} %get-tuple-element.25.one_ref, f32[1,32,32,512]{3,2,1,0:T(8,128)S(1)} %copy-done.3, f32[1,32,32,512]{3,2,1,0:T(8,128)S(1)} %copy-done, f32[1,2,32,32,512]{4,3,2,1,0:T(8,128)S(1)} %copy-done.1, ...), custom_call_target="tpu_custom_call" | custom-call | tf_op jit(solution)/shard_map/level_two/pallas_call | solution.py:421
  34.2 0.0 collective-permute-done.4.rx0
  34.2 0.0 collective-permute-done.5.rx1
  34.2 0.0 collective-permute-done.6.ry0
  34.2 1.7 %collective-permute-done.7.ry1 = bf16[32,4,512]{2,1,0:T(4,128)(2,1)S(1)} collective-permute-done((bf16[32,4,512]{2,1,0:T(4,128)(2,1)S(1)}, bf16[32,4,512]{2,1,0:T(4,128)(2,1)S(1)}, u32[]{:S(2)}, u32[]{:S(2)}) %collective-permute-start.7) | collective-permute-done | bytes 131104 | tf_op jit(solution)/shard_map/ppermute | solution.py:44
  36.0 2.7 %level_two_edge.1 = (f32[1,32,32,512]{3,2,1,0:T(8,128)S(1)}, f32[1,32,32,512]{3,2,1,0:T(8,128)S(1)}, bf16[1152,4,128]{2,1,0:T(4,128)(2,1)S(1)}, f32[1,32,32,512]{3,2,1,0:T(8,128)}) custom-call(s32[2]{0:T(128)S(1)} %pad_add_fusion.where_ref, s32[1,512]{1,0:T(1,128)S(1)} %get-tuple-element.27.at_ref, ...), custom_call_target="tpu_custom_call", output_to_operand_aliasing={{0}: (2, {}), {1}: (3, {}), {2}: (4, {})} | custom-call | tf_op jit(solution)/shard_map/level_two_edge/pallas_call | solution.py:430
  38.6 28.2 %all_to_all.5 = bf16[1152,4,128]{2,1,0:T(4,128)(2,1)S(1)} all-to-all(bf16[1152,4,128]{2,1,0:T(4,128)(2,1)S(1)} %get-tuple-element.36), channel_id=1, replica_groups=mesh['shot'=2,'gx'=8,'gy'=8] {'shot','gx','gy'}, dimensions={0} | all-to-all | bytes 2359296 | tf_op jit(solution)/shard_map/all_to_all | solution.py:440
  66.8 4.0 %owner_sum.1 = f32[128,1024]{1,0:T(8,128)} custom-call(bf16[576,8,128]{2,1,0:T(8,128)(2,1)S(1)} %bitcast.6), custom_call_target="tpu_custom_call" | custom-call | tf_op jit(solution)/shard_map/owner_sum/pallas_call | solution.py:441
  (8 shorter events, 0.0 us)
Async XLA Ops:
  0.7 14.2 %copy-start = (f32[1,32,32,512]{3,2,1,0:T(8,128)S(1)}, f32[1,32,32,512]{3,2,1,0:T(8,128)}, u32[]{:S(2)}) copy-start(f32[1,32,32,512]{3,2,1,0:T(8,128)} %speed_ref.7) | copy-start | bytes 6291460
  0.7 14.3 %copy-start.1 = (f32[1,2,32,32,512]{4,3,2,1,0:T(8,128)S(1)}, f32[1,2,32,32,512]{4,3,2,1,0:T(8,128)}, u32[]{:S(2)}) copy-start(f32[1,2,32,32,512]{4,3,2,1,0:T(8,128)} %source_ref.3) | copy-start | bytes 12582916
  0.7 14.3 %copy-start.3 = (f32[1,32,32,512]{3,2,1,0:T(8,128)S(1)}, f32[1,32,32,512]{3,2,1,0:T(8,128)}, u32[]{:S(2)}) copy-start(f32[1,32,32,512]{3,2,1,0:T(8,128)} %now_ref.3) | copy-start | bytes 6291460
  0.7 14.3 %copy-start.4 = (f32[1,32,32,512]{3,2,1,0:T(8,128)S(1)}, f32[1,32,32,512]{3,2,1,0:T(8,128)}, u32[]{:S(2)}) copy-start(f32[1,32,32,512]{3,2,1,0:T(8,128)} %prev_ref.1) | copy-start | bytes 6291460
  0.7 14.3 %copy-start.5 = (bf16[512,512]{1,0:T(8,128)(2,1)S(1)}, bf16[512,512]{1,0:T(8,128)(2,1)}, u32[]{:S(2)}) copy-start(bf16[512,512]{1,0:T(8,128)(2,1)} %constant.12.clone.low_ref) | copy-start | bytes 1572868
  0.7 14.3 %copy-start.6 = (bf16[512,512]{1,0:T(8,128)(2,1)S(1)}, bf16[512,512]{1,0:T(8,128)(2,1)}, u32[]{:S(2)}) copy-start(bf16[512,512]{1,0:T(8,128)(2,1)} %constant.11.clone.high_ref) | copy-start | bytes 1572868
  0.7 14.3 %copy-start.7 = (s32[1,1,1,512]{3,2,1,0:T(1,128)S(1)}, s32[1,1,1,512]{3,2,1,0:T(1,128)}, u32[]{:S(2)}) copy-start(s32[1,1,1,512]{3,2,1,0:T(1,128)} %param.14) | copy-start | bytes 6148
  2.9 18.6 %collective-permute-start = (bf16[4,32,512]{2,1,0:T(8,128)(2,1)S(1)}, bf16[4,32,512]{2,1,0:T(8,128)(2,1)S(1)}, u32[]{:S(2)}, u32[]{:S(2)}) collective-permute-start(bf16[4,32,512]{2,1,0:T(8,128)(2,1)S(1)} %get-tuple-element.21), channel_id=1, source_target_pairs={{0,8},{8,0},{16,24},{24,16},{32,40},{40,32},{48,56},{56,48},{1,9},... | collective-permute-start | bytes 393224 | tf_op jit(solution)/shard_map/ppermute | solution.py:41
  5.0 16.5 %collective-permute-start.1 = (bf16[4,32,512]{2,1,0:T(8,128)(2,1)S(1)}, bf16[4,32,512]{2,1,0:T(8,128)(2,1)S(1)}, u32[]{:S(2)}, u32[]{:S(2)}) collective-permute-start(bf16[4,32,512]{2,1,0:T(8,128)(2,1)S(1)} %get-tuple-element.22), channel_id=1, source_target_pairs={{0,56},{8,16},{16,8},{24,32},{32,24},{40,48},{48,40},{56,0},{1,57}... | collective-permute-start | bytes 393224 | tf_op jit(solution)/shard_map/ppermute | solution.py:42
  7.9 13.6 %collective-permute-start.2 = (bf16[32,4,512]{2,1,0:T(4,128)(2,1)S(1)}, bf16[32,4,512]{2,1,0:T(4,128)(2,1)S(1)}, u32[]{:S(2)}, u32[]{:S(2)}) collective-permute-start(bf16[32,4,512]{2,1,0:T(4,128)(2,1)S(1)} %get-tuple-element.23), channel_id=1, source_target_pairs={{0,1},{1,0},{2,3},{3,2},{4,5},{5,4},{6,7},{7,6},{8,9},{9,8},{10,11... | collective-permute-start | bytes 393224 | tf_op jit(solution)/shard_map/ppermute | solution.py:43
  10.5 13.2 %collective-permute-start.3 = (bf16[32,4,512]{2,1,0:T(4,128)(2,1)S(1)}, bf16[32,4,512]{2,1,0:T(4,128)(2,1)S(1)}, u32[]{:S(2)}, u32[]{:S(2)}) collective-permute-start(bf16[32,4,512]{2,1,0:T(4,128)(2,1)S(1)} %get-tuple-element.24), channel_id=1, source_target_pairs={{0,7},{1,2},{2,1},{3,4},{4,3},{5,6},{6,5},{7,0},{8,15},{9,10},{10,... | collective-permute-start | bytes 393224 | tf_op jit(solution)/shard_map/ppermute | solution.py:44
  23.6 4.9 %copy-start.2 = (f32[1,2,32,32,512]{4,3,2,1,0:T(8,128)S(1)}, f32[1,2,32,32,512]{4,3,2,1,0:T(8,128)}, u32[]{:S(2)}) copy-start(f32[1,2,32,32,512]{4,3,2,1,0:T(8,128)} %forward_ref.3) | copy-start | bytes 12582916
  24.9 9.3 %collective-permute-start.4 = (bf16[4,32,512]{2,1,0:T(8,128)(2,1)S(1)}, bf16[4,32,512]{2,1,0:T(8,128)(2,1)S(1)}, u32[]{:S(2)}, u32[]{:S(2)}) collective-permute-start(bf16[4,32,512]{2,1,0:T(8,128)(2,1)S(1)} %get-tuple-element.31), channel_id=1, source_target_pairs={{0,8},{8,0},{16,24},{24,16},{32,40},{40,32},{48,56},{56,48},{1,9},... | collective-permute-start | bytes 393224 | tf_op jit(solution)/shard_map/ppermute | solution.py:41
  25.0 9.2 %collective-permute-start.5 = (bf16[4,32,512]{2,1,0:T(8,128)(2,1)S(1)}, bf16[4,32,512]{2,1,0:T(8,128)(2,1)S(1)}, u32[]{:S(2)}, u32[]{:S(2)}) collective-permute-start(bf16[4,32,512]{2,1,0:T(8,128)(2,1)S(1)} %get-tuple-element.32), channel_id=1, source_target_pairs={{0,56},{8,16},{16,8},{24,32},{32,24},{40,48},{48,40},{56,0},{1,57}... | collective-permute-start | bytes 393224 | tf_op jit(solution)/shard_map/ppermute | solution.py:42
  25.2 9.1 %collective-permute-start.6 = (bf16[32,4,512]{2,1,0:T(4,128)(2,1)S(1)}, bf16[32,4,512]{2,1,0:T(4,128)(2,1)S(1)}, u32[]{:S(2)}, u32[]{:S(2)}) collective-permute-start(bf16[32,4,512]{2,1,0:T(4,128)(2,1)S(1)} %get-tuple-element.33), channel_id=1, source_target_pairs={{0,1},{1,0},{2,3},{3,2},{4,5},{5,4},{6,7},{7,6},{8,9},{9,8},{10,11... | collective-permute-start | bytes 393224 | tf_op jit(solution)/shard_map/ppermute | solution.py:43
  26.7 9.3 %collective-permute-start.7 = (bf16[32,4,512]{2,1,0:T(4,128)(2,1)S(1)}, bf16[32,4,512]{2,1,0:T(4,128)(2,1)S(1)}, u32[]{:S(2)}, u32[]{:S(2)}) collective-permute-start(bf16[32,4,512]{2,1,0:T(4,128)(2,1)S(1)} %get-tuple-element.34), channel_id=1, source_target_pairs={{0,7},{1,2},{2,1},{3,4},{4,3},{5,6},{6,5},{7,0},{8,15},{9,10},{10,... | collective-permute-start | bytes 393224 | tf_op jit(solution)/shard_map/ppermute | solution.py:44

commit v4 on v3

--- a/solution.py
+++ b/solution.py
@@ -141,10 +141,8 @@
 
 
 def first_kernel(
-    where_ref, live_ref, foot_ref, now_ref, prev_ref, source_ref, speed_ref, high_ref, low_ref,
-    one_ref, out_ref, at_ref, ext, zs,
+    now_ref, prev_ref, source_ref, speed_ref, high_ref, low_ref, one_ref, ext, zs,
 ):
-    place_pieces(foot_ref, live_ref[0], where_ref[1] % 2, at_ref, out_ref)
     clear_edges(ext)
     for i in range(4):
         block = now_ref[0, 8 * i : 8 * i + 8]
@@ -165,11 +163,12 @@
 
 
 def second_kernel(
-    one_ref, now_ref, speed_ref, source_ref, forward_ref, high_ref, low_ref,
-    done_hbm, two_ref, image_ref, ext, zs, sem,
+    where_ref, live_ref, foot_ref, one_ref, now_ref, speed_ref, source_ref, forward_ref, high_ref, low_ref,
+    done_hbm, two_ref, image_ref, out_ref, at_ref, ext, zs, sem,
 ):
     copy = pltpu.make_async_copy(one_ref, done_hbm, sem)
     copy.start()
+    place_pieces(foot_ref, live_ref[0], where_ref[1] % 2, at_ref, out_ref)
     clear_edges(ext)
     for i in range(4):
         block = one_ref[0, 8 * i : 8 * i + 8]
@@ -192,86 +191,86 @@
     copy.wait()
 
 
-def add_halos(rx0, rx1, ry0, ry1, gx, gy, add):
-    row = lax.broadcasted_iota(jnp.int32, (8, CZ), 0)
-
-    def x_side(face, side):
-        def rows_of(ty):
-            at = pl.ds(pl.multiple_of(8 * ty, 8), 8)
-            layers = [face[h, at, :].astype(F32) for h in range(4)]
-            for j in range(4):
-                if side == 0:
-                    term = sum(COEFFS[k - 1] * layers[4 + j - k] for k in range(j + 1, 5))
-                    add(j, at, term)
-                else:
-                    term = sum(COEFFS[k - 1] * layers[k - 1 - j] for k in range(j + 1, 5))
-                    add(CX - 1 - j, at, term)
-
-        for ty in range(4):
-            rows_of(ty)
-
-    def y_side(face, side):
-        def weights(h):
-            total = jnp.zeros((8, CZ), F32)
+def add_halos(rx0, rx1, ry0, ry1, gx, gy, update):
+    def store(changes):
+        for ref, at, value in changes:
+            ref[at] = value
+
+    def x_sides(low, high):
+        inside = [jnp.where(gx > 0, 1.0, 0.0), jnp.where(gx < NDEV - 1, 1.0, 0.0)]
+
+        def strip(ty, carry):
+            rows = pl.ds(pl.multiple_of(8 * ty, 8), 8)
+            for side, face in enumerate((low, high)):
+                layers = [face[h, rows, :].astype(F32) * inside[side] for h in range(4)]
+                changes = []
+                for j in range(4):
+                    near_first = layers[::-1] if side == 0 else layers
+                    term = sum(COEFFS[j + h] * near_first[h] for h in range(4 - j))
+                    changes += update(j if side == 0 else CX - 1 - j, rows, slice(0, CZ), term)
+                store(changes)
+            return carry
+
+        lax.fori_loop(0, 4, strip, 0)
+
+    def y_sides(low, high):
+        inside = [jnp.where(gy > 0, 1.0, 0.0), jnp.where(gy < NDEV - 1, 1.0, 0.0)]
+        row = lax.broadcasted_iota(jnp.int32, (8, 128), 0)
+
+        def column(side, h):
+            total = jnp.zeros((8, 128), F32)
             for j in range(4):
                 k = 4 + j - h if side == 0 else h + 1 + j
-                if 1 <= k <= 4:
-                    at = j if side == 0 else 7 - j
-                    total = jnp.where(row == at, COEFFS[k - 1], total)
+                if k <= 4:
+                    total = jnp.where(row == (j if side == 0 else 7 - j), COEFFS[k - 1] * inside[side], total)
             return total
 
-        columns = [weights(h) for h in range(4)]
-
-        def plane(x, carry):
-            layers = face[x].astype(F32)
-            term = sum(columns[h] * jnp.broadcast_to(layers[h : h + 1], (8, CZ)) for h in range(4))
-            add(x, slice(0, 8) if side == 0 else slice(24, 32), term)
+        columns = [[column(side, h) for h in range(4)] for side in range(2)]
+
+        def planes(i, carry):
+            changes = []
+            for b in range(4):
+                x = 4 * i + b
+                for side, face in enumerate((low, high)):
+                    layers = face[x].astype(F32)
+                    for zv in range(4):
+                        lanes = slice(128 * zv, 128 * zv + 128)
+                        term = sum(
+                            columns[side][h] * jnp.broadcast_to(layers[h : h + 1, lanes], (8, 128)) for h in range(4)
+                        )
+                        changes += update(x, slice(24 * side, 24 * side + 8), lanes, term)
+            store(changes)
             return carry
 
-        lax.fori_loop(0, CX, plane, 0)
-
-    @pl.when((gx > 0) & (gx % 2 == 1))
-    def _():
-        x_side(rx0, 0)
-
-    @pl.when((gx > 0) & (gx % 2 == 0))
-    def _():
-        x_side(rx1, 0)
-
-    @pl.when((gx < NDEV - 1) & (gx % 2 == 1))
-    def _():
-        x_side(rx1, 1)
-
-    @pl.when((gx < NDEV - 1) & (gx % 2 == 0))
-    def _():
-        x_side(rx0, 1)
-
-    @pl.when((gy > 0) & (gy % 2 == 1))
-    def _():
-        y_side(ry0, 0)
-
-    @pl.when((gy > 0) & (gy % 2 == 0))
-    def _():
-        y_side(ry1, 0)
-
-    @pl.when((gy < NDEV - 1) & (gy % 2 == 1))
-    def _():
-        y_side(ry1, 1)
-
-    @pl.when((gy < NDEV - 1) & (gy % 2 == 0))
-    def _():
-        y_side(ry0, 1)
-
-
-def first_edge_kernel(where_ref, part_ref, speed_ref, rx0, rx1, ry0, ry1, one_ref, sx0, sx1, sy0, sy1):
+        lax.fori_loop(0, CX // 4, planes, 0)
+
+    @pl.when(gx % 2 == 1)
+    def _():
+        x_sides(rx0, rx1)
+
+    @pl.when(gx % 2 == 0)
+    def _():
+        x_sides(rx1, rx0)
+
+    @pl.when(gy % 2 == 1)
+    def _():
+        y_sides(ry0, ry1)
+
+    @pl.when(gy % 2 == 0)
+    def _():
+        y_sides(ry1, ry0)
+
+
+def first_edge_kernel(where_ref, part_ref, speed_ref, ry1, ry0, rx1, rx0, one_ref, sx0, sx1, sy0, sy1):
     del part_ref
     gx = where_ref[0]
     gy = where_ref[1]
 
-    def add(x, rows, term):
-        one_ref[0, x, rows, :] = one_ref[0, x, rows, :] + speed_ref[0, x, rows, :] * term
-
-    add_halos(rx0, rx1, ry0, ry1, gx, gy, add)
+    def update(x, rows, lanes, term):
+        at = (0, x, rows, lanes)
+        return [(one_ref, at, one_ref[at] + speed_ref[at] * term)]
+
+    add_halos(rx0, rx1, ry0, ry1, gx, gy, update)
     emit_faces(
         lambda side: one_ref[0, 28 * side : 28 * side + 4],
         lambda side: one_ref[0, :, 28 * side : 28 * side + 4, :],
@@ -294,19 +293,22 @@
 
 
 def second_edge_kernel(
-    where_ref, at_ref, part_ref, image_in, begun_ref, speed_ref, forward_ref, rx0, rx1, ry0, ry1,
+    where_ref, at_ref, part_ref, image_in, begun_ref, speed_ref, forward_ref, ry1, ry0, rx1, rx0,
     two_ref, image_ref, out_ref, done_hbm, sem,
 ):
     del part_ref, image_in, begun_ref
     gx = where_ref[0]
     gy = where_ref[1]
 
-    def add(x, rows, term):
-        change = speed_ref[0, x, rows, :] * term
-        two_ref[0, x, rows, :] = two_ref[0, x, rows, :] + change
-        image_ref[0, x, rows, :] = image_ref[0, x, rows, :] + forward_ref[0, 1, x, rows, :] * change
-
-    add_halos(rx0, rx1, ry0, ry1, gx, gy, add)
+    def update(x, rows, lanes, term):
+        at = (0, x, rows, lanes)
+        change = speed_ref[at] * term
+        return [
+            (two_ref, at, two_ref[at] + change),
+            (image_ref, at, image_ref[at] + forward_ref[0, 1, x, rows, lanes] * change),
+        ]
+
+    add_halos(rx0, rx1, ry0, ry1, gx, gy, update)
     copy = pltpu.make_async_copy(two_ref, done_hbm, sem)
     copy.start()
 
@@ -397,17 +399,15 @@
     now = near(adjoint_now)
     prev = near(adjoint_prev)
     high, low = [near(jnp.asarray(term)) for term in depth_band()]
-    part_one, outgoing, at = pl.pallas_call(
+    part_one = pl.pallas_call(
         first_kernel,
-        in_specs=[SMEM, SMEM] + [VMEM] * 7,
-        out_specs=[VMEM] * 3,
-        out_shape=[level, begun, jax.ShapeDtypeStruct((1, SUB), jnp.int32)],
+        in_specs=[VMEM] * 6,
+        out_specs=VMEM,
+        out_shape=level,
         scratch_shapes=[ext, depth],
         compiler_params=params(12),
         name="level_one",
-    )(
-        place, live_counts.reshape(-1), footprint.reshape(1, SUB), now, prev, source, speed, high, low,
-    )
+    )(now, prev, source, speed, high, low)
     whole_one, *send = pl.pallas_call(
         first_edge_kernel,
         in_specs=[SMEM] + [VMEM] * 6,
@@ -416,17 +416,20 @@
         input_output_aliases={1: 0},
         compiler_params=params(4),
         name="level_one_edge",
-    )(place, part_one, speed, *[near(face) for face in faces])
+    )(place, part_one, speed, *[near(face) for face in faces[::-1]])
     faces = swap_faces(*send)
-    level_one, part_two, image = pl.pallas_call(
+    level_one, part_two, image, outgoing, at = pl.pallas_call(
         second_kernel,
-        in_specs=[VMEM] * 7,
-        out_specs=[HBM, VMEM, VMEM],
-        out_shape=[final, level, level],
+        in_specs=[SMEM, SMEM] + [VMEM] * 8,
+        out_specs=[HBM] + [VMEM] * 4,
+        out_shape=[final, level, level, begun, jax.ShapeDtypeStruct((1, SUB), jnp.int32)],
         scratch_shapes=[ext, depth, pltpu.SemaphoreType.DMA],
         compiler_params=params(12),
         name="level_two",
-    )(whole_one, now, speed, source, forward, high, low)
+    )(
+        place, live_counts.reshape(-1), footprint.reshape(1, SUB),
+        whole_one, now, speed, source, forward, high, low,
+    )
     _, _, outgoing, level_two = pl.pallas_call(
         second_edge_kernel,
         in_specs=[SMEM, SMEM] + [VMEM] * 9,
@@ -436,7 +439,7 @@
         input_output_aliases={2: 0, 3: 1, 4: 2},
         compiler_params=params(4),
         name="level_two_edge",
-    )(place, at, part_two, image, outgoing, speed, forward, *[near(face) for face in faces])
+    )(place, at, part_two, image, outgoing, speed, forward, *[near(face) for face in faces[::-1]])
     incoming = lax.all_to_all(outgoing, ("shot", "gx", "gy"), split_axis=0, concat_axis=0, tiled=True)
     gradient = pl.pallas_call(
         owner_kernel,

time: 70.9 us -> 69.9 us (0.986)
  waiting for transfers between devices: 3.86 us -> 0.02 us
  blocking collectives: 28.2 us -> 29.4 us
  starting transfers between devices: 15 us -> 16.1 us
    ppermute x2, starting transfers between devices: 5.72 us -> 10.8 us  [swap_faces(): lax.ppermute(y1, 'gy', SWAP_B)]
    ppermute x2, starting transfers between devices: 4.12 us -> 0.25 us  [swap_faces(): lax.ppermute(y0, 'gy', SWAP_A)]
    ppermute x2, waiting for transfers between devices: 3.84 us -> 0.01 us  [swap_faces(): lax.ppermute(y1, 'gy', SWAP_B)]
    ppermute x2, starting transfers between devices: 2.21 us -> 0.01 us  [swap_faces(): lax.ppermute(x0, 'gx', SWAP_A)]
    ppermute x2, starting transfers between devices: 2.96 us -> 5.06 us  [swap_faces(): lax.ppermute(x1, 'gx', SWAP_B)]
    all_to_all x1, blocking collectives: 28.2 us -> 29.4 us  [per_device(): lax.all_to_all(outgoing, ('shot', 'gx', 'gy'), split_axis=0, concat_axis=...]
  transfers between devices with their start and end apart: 8 -> 8, of which waited for: 2 -> 0; matrix products, arithmetic and copies ran while one was open for 0% -> 0% of each run, Pallas kernels for 17% -> 17%
where the time goes in v4:
time: 69.9 us; the launch traced here: 69.7 us
  blocking collectives  29.4 us (42%)
  Pallas kernels  22.6 us (32%)
  starting transfers between devices  16.1 us (23%)
  between operations  1.48 us (2%)
    all_to_all x1, blocking collectives, per_device(): lax.all_to_all(outgoing, ('shot', 'gx', 'gy'), split_axis=0, concat_axis=...  29.4 us
    ppermute x2, starting transfers between devices, swap_faces(): lax.ppermute(y1, 'gy', SWAP_B)  10.8 us
    pallas_call x1, Pallas kernels, per_device(): pl.pallas_call(second_kernel, in_specs=[SMEM, SMEM] + [VMEM] * 8, out_spe...  6.76 us
    pallas_call x1, Pallas kernels, per_device(): pl.pallas_call(first_kernel, in_specs=[VMEM] * 6, out_specs=VMEM, out_sha...  5.43 us
    ppermute x2, starting transfers between devices, swap_faces(): lax.ppermute(x1, 'gx', SWAP_B)  5.06 us
    pallas_call x1, Pallas kernels, per_device(): pl.pallas_call(owner_kernel, in_specs=[VMEM], out_specs=VMEM, out_shape=j...  4.01 us
    pallas_call x1, Pallas kernels, per_device(): pl.pallas_call(second_edge_kernel, in_specs=[SMEM, SMEM] + [VMEM] * 9, ou...  2.86 us
    pallas_call x1, Pallas kernels, per_device(): pl.pallas_call(face_kernel, in_specs=[SMEM, HBM], out_specs=[VMEM] * 4, o...  2.14 us
  transfers between devices with their start and end apart: 8, of which 0 were waited for; matrix products, arithmetic and copies ran while one was open for 0% of the time, Pallas kernels for 17%

profile of v4, /device:TPU:1, one launch (start us, length us, event | category | flops | bytes accessed | tf_op | source)
XLA Modules:
  0.0 69.7 jit_solution(16229972853617829423)
XLA Ops:
  0.6 0.1 pad_add_fusion.where_ref
  0.7 0.0 copy-start.5
  0.7 0.0 copy-start.6
  0.7 2.1 %faces.1 = (bf16[4,32,512]{2,1,0:T(8,128)(2,1)S(1)}, bf16[4,32,512]{2,1,0:T(8,128)(2,1)S(1)}, bf16[32,4,512]{2,1,0:T(4,128)(2,1)S(1)}, bf16[32,4,512]{2,1,0:T(4,128)(2,1)S(1)}) custom-call(s32[2]{0:T(128)S(1)} %pad_add_fusion.where_ref, f32[1,32,32,512]{3,2,1,0:T(8,128)} %now_ref.3), custom_call_target="tpu_custom_call" | custom-call | flops 10000000000 | bytes 1000000 | tf_op jit(solution)/shard_map/faces/pallas_call | solution.py:383
  2.9 7.3 %collective-permute-start = (bf16[32,4,512]{2,1,0:T(4,128)(2,1)S(1)}, bf16[32,4,512]{2,1,0:T(4,128)(2,1)S(1)}, u32[]{:S(2)}, u32[]{:S(2)}) collective-permute-start(bf16[32,4,512]{2,1,0:T(4,128)(2,1)S(1)} %get-tuple-element.19), channel_id=1, source_target_pairs={{0,7},{1,2},{2,1},{3,4},{4,3},{5,6},{6,5},{7,0},{8,15},{9,10},{10,... | collective-permute-start | bytes 393224 | tf_op jit(solution)/shard_map/ppermute | solution.py:44
  10.2 0.0 collective-permute-start.1
  10.2 2.6 %collective-permute-start.2 = (bf16[4,32,512]{2,1,0:T(8,128)(2,1)S(1)}, bf16[4,32,512]{2,1,0:T(8,128)(2,1)S(1)}, u32[]{:S(2)}, u32[]{:S(2)}) collective-permute-start(bf16[4,32,512]{2,1,0:T(8,128)(2,1)S(1)} %get-tuple-element.21), channel_id=1, source_target_pairs={{0,56},{8,16},{16,8},{24,32},{32,24},{40,48},{48,40},{56,0},{1,57}... | collective-permute-start | bytes 393224 | tf_op jit(solution)/shard_map/ppermute | solution.py:42
  12.8 0.0 collective-permute-start.3
  12.8 0.0 copy-done
  12.8 0.0 copy-done.1
  12.8 0.0 copy-done.3
  12.8 0.0 copy-done.4
  12.8 5.4 %level_one.1.part_ref = f32[1,32,32,512]{3,2,1,0:T(8,128)S(1)} custom-call(f32[1,32,32,512]{3,2,1,0:T(8,128)S(1)} %copy-done.3, f32[1,32,32,512]{3,2,1,0:T(8,128)S(1)} %copy-done.4, f32[1,2,32,32,512]{4,3,2,1,0:T(8,128)S(1)} %copy-done.1, f32[1,32,32,512]{3,2,1,0:T(8,128)S(1)} %copy-done, bf16[512,512]{1,0:T(8,128)(2,1)S(1)} %copy-done.6, ...), custom_call_target="tpu_custom_call" | custom-call | tf_op jit(solution)/shard_map/level_one/pallas_call | solution.py:402
  18.3 0.0 copy-start.2
  18.3 0.0 copy-start.7
  18.3 0.0 collective-permute-done.ry1
  18.3 0.0 collective-permute-done.1.ry0
  18.3 0.0 collective-permute-done.2.rx1
  18.3 0.0 collective-permute-done.3.rx0
  18.3 1.4 %level_one_edge.1 = (f32[1,32,32,512]{3,2,1,0:T(8,128)S(1)}, bf16[4,32,512]{2,1,0:T(8,128)(2,1)S(1)}, bf16[4,32,512]{2,1,0:T(8,128)(2,1)S(1)}, bf16[32,4,512]{2,1,0:T(4,128)(2,1)S(1)}, bf16[32,4,512]{2,1,0:T(4,128)(2,1)S(1)}) custom-call(s32[2]{0:T(128)S(1)} %pad_add_fusion.where_ref, ...), custom_call_target="tpu_custom_call", output_to_operand_aliasing={{0}: (1, {})} | custom-call | tf_op jit(solution)/shard_map/level_one_edge/pallas_call | solution.py:411
  19.8 3.5 %collective-permute-start.4 = (bf16[32,4,512]{2,1,0:T(4,128)(2,1)S(1)}, bf16[32,4,512]{2,1,0:T(4,128)(2,1)S(1)}, u32[]{:S(2)}, u32[]{:S(2)}) collective-permute-start(bf16[32,4,512]{2,1,0:T(4,128)(2,1)S(1)} %get-tuple-element.29), channel_id=1, source_target_pairs={{0,7},{1,2},{2,1},{3,4},{4,3},{5,6},{6,5},{7,0},{8,15},{9,10},{10,... | collective-permute-start | bytes 393224 | tf_op jit(solution)/shard_map/ppermute | solution.py:44
  23.3 0.3 collective-permute-start.5
  23.5 2.5 %collective-permute-start.6 = (bf16[4,32,512]{2,1,0:T(8,128)(2,1)S(1)}, bf16[4,32,512]{2,1,0:T(8,128)(2,1)S(1)}, u32[]{:S(2)}, u32[]{:S(2)}) collective-permute-start(bf16[4,32,512]{2,1,0:T(8,128)(2,1)S(1)} %get-tuple-element.31), channel_id=1, source_target_pairs={{0,56},{8,16},{16,8},{24,32},{32,24},{40,48},{48,40},{56,0},{1,57}... | collective-permute-start | bytes 393224 | tf_op jit(solution)/shard_map/ppermute | solution.py:42
  26.0 0.0 collective-permute-start.7
  26.7 6.8 %level_two.1 = (f32[1,32,32,512]{3,2,1,0:T(8,128)}, f32[1,32,32,512]{3,2,1,0:T(8,128)S(1)}, f32[1,32,32,512]{3,2,1,0:T(8,128)S(1)}, bf16[1152,4,128]{2,1,0:T(4,128)(2,1)S(1)}, s32[1,512]{1,0:T(1,128)S(1)}) custom-call(s32[2]{0:T(128)S(1)} %pad_add_fusion.where_ref, s32[1]{0:T(128)} %bitcast.5.live_ref, s32[1,512]{1,0:T(1,128)S(1)} %bitcast.7, ...), custom_call_target="tpu_custom_call" | custom-call | tf_op jit(solution)/shard_map/level_two/pallas_call | solution.py:421
  33.4 0.0 collective-permute-done.4.ry1
  33.4 0.0 collective-permute-done.5.ry0
  33.4 0.0 collective-permute-done.6.rx1
  33.5 0.0 collective-permute-done.7.rx0
  33.5 2.9 %level_two_edge.1 = (f32[1,32,32,512]{3,2,1,0:T(8,128)S(1)}, f32[1,32,32,512]{3,2,1,0:T(8,128)S(1)}, bf16[1152,4,128]{2,1,0:T(4,128)(2,1)S(1)}, f32[1,32,32,512]{3,2,1,0:T(8,128)}) custom-call(s32[2]{0:T(128)S(1)} %pad_add_fusion.where_ref, s32[1,512]{1,0:T(1,128)S(1)} %get-tuple-element.25.at_ref, ...), custom_call_target="tpu_custom_call", output_to_operand_aliasing={{0}: (2, {}), {1}: (3, {}), {2}: (4, {})} | custom-call | tf_op jit(solution)/shard_map/level_two_edge/pallas_call | solution.py:433
  36.3 29.4 %all_to_all.5 = bf16[1152,4,128]{2,1,0:T(4,128)(2,1)S(1)} all-to-all(bf16[1152,4,128]{2,1,0:T(4,128)(2,1)S(1)} %get-tuple-element.34), channel_id=1, replica_groups=mesh['shot'=2,'gx'=8,'gy'=8] {'shot','gx','gy'}, dimensions={0} | all-to-all | bytes 2359296 | tf_op jit(solution)/shard_map/all_to_all | solution.py:443
  65.7 4.0 %owner_sum.1 = f32[128,1024]{1,0:T(8,128)} custom-call(bf16[576,8,128]{2,1,0:T(8,128)(2,1)S(1)} %bitcast.6), custom_call_target="tpu_custom_call" | custom-call | tf_op jit(solution)/shard_map/owner_sum/pallas_call | solution.py:444
  (8 shorter events, 0.0 us)
Async XLA Ops:
  0.7 12.1 %copy-start = (f32[1,32,32,512]{3,2,1,0:T(8,128)S(1)}, f32[1,32,32,512]{3,2,1,0:T(8,128)}, u32[]{:S(2)}) copy-start(f32[1,32,32,512]{3,2,1,0:T(8,128)} %speed_ref.7) | copy-start | bytes 6291460
  0.7 12.1 %copy-start.1 = (f32[1,2,32,32,512]{4,3,2,1,0:T(8,128)S(1)}, f32[1,2,32,32,512]{4,3,2,1,0:T(8,128)}, u32[]{:S(2)}) copy-start(f32[1,2,32,32,512]{4,3,2,1,0:T(8,128)} %source_ref.3) | copy-start | bytes 12582916
  0.7 12.1 %copy-start.3 = (f32[1,32,32,512]{3,2,1,0:T(8,128)S(1)}, f32[1,32,32,512]{3,2,1,0:T(8,128)}, u32[]{:S(2)}) copy-start(f32[1,32,32,512]{3,2,1,0:T(8,128)} %now_ref.3) | copy-start | bytes 6291460
  0.7 12.1 %copy-start.4 = (f32[1,32,32,512]{3,2,1,0:T(8,128)S(1)}, f32[1,32,32,512]{3,2,1,0:T(8,128)}, u32[]{:S(2)}) copy-start(f32[1,32,32,512]{3,2,1,0:T(8,128)} %prev_ref.1) | copy-start | bytes 6291460
  0.7 12.1 %copy-start.5 = (bf16[512,512]{1,0:T(8,128)(2,1)S(1)}, bf16[512,512]{1,0:T(8,128)(2,1)}, u32[]{:S(2)}) copy-start(bf16[512,512]{1,0:T(8,128)(2,1)} %constant.12.clone.low_ref) | copy-start | bytes 1572868
  0.7 12.1 %copy-start.6 = (bf16[512,512]{1,0:T(8,128)(2,1)S(1)}, bf16[512,512]{1,0:T(8,128)(2,1)}, u32[]{:S(2)}) copy-start(bf16[512,512]{1,0:T(8,128)(2,1)} %constant.11.clone.high_ref) | copy-start | bytes 1572868
  2.9 15.4 %collective-permute-start = (bf16[32,4,512]{2,1,0:T(4,128)(2,1)S(1)}, bf16[32,4,512]{2,1,0:T(4,128)(2,1)S(1)}, u32[]{:S(2)}, u32[]{:S(2)}) collective-permute-start(bf16[32,4,512]{2,1,0:T(4,128)(2,1)S(1)} %get-tuple-element.19), channel_id=1, source_target_pairs={{0,7},{1,2},{2,1},{3,4},{4,3},{5,6},{6,5},{7,0},{8,15},{9,10},{10,... | collective-permute-start | bytes 393224 | tf_op jit(solution)/shard_map/ppermute | solution.py:44
  10.2 8.1 %collective-permute-start.1 = (bf16[32,4,512]{2,1,0:T(4,128)(2,1)S(1)}, bf16[32,4,512]{2,1,0:T(4,128)(2,1)S(1)}, u32[]{:S(2)}, u32[]{:S(2)}) collective-permute-start(bf16[32,4,512]{2,1,0:T(4,128)(2,1)S(1)} %get-tuple-element.20), channel_id=1, source_target_pairs={{0,1},{1,0},{2,3},{3,2},{4,5},{5,4},{6,7},{7,6},{8,9},{9,8},{10,11... | collective-permute-start | bytes 393224 | tf_op jit(solution)/shard_map/ppermute | solution.py:43
  10.2 8.1 %collective-permute-start.2 = (bf16[4,32,512]{2,1,0:T(8,128)(2,1)S(1)}, bf16[4,32,512]{2,1,0:T(8,128)(2,1)S(1)}, u32[]{:S(2)}, u32[]{:S(2)}) collective-permute-start(bf16[4,32,512]{2,1,0:T(8,128)(2,1)S(1)} %get-tuple-element.21), channel_id=1, source_target_pairs={{0,56},{8,16},{16,8},{24,32},{32,24},{40,48},{48,40},{56,0},{1,57}... | collective-permute-start | bytes 393224 | tf_op jit(solution)/shard_map/ppermute | solution.py:42
  12.8 5.5 %collective-permute-start.3 = (bf16[4,32,512]{2,1,0:T(8,128)(2,1)S(1)}, bf16[4,32,512]{2,1,0:T(8,128)(2,1)S(1)}, u32[]{:S(2)}, u32[]{:S(2)}) collective-permute-start(bf16[4,32,512]{2,1,0:T(8,128)(2,1)S(1)} %get-tuple-element.22), channel_id=1, source_target_pairs={{0,8},{8,0},{16,24},{24,16},{32,40},{40,32},{48,56},{56,48},{1,9},... | collective-permute-start | bytes 393224 | tf_op jit(solution)/shard_map/ppermute | solution.py:41
  18.3 8.4 %copy-start.2 = (f32[1,2,32,32,512]{4,3,2,1,0:T(8,128)S(1)}, f32[1,2,32,32,512]{4,3,2,1,0:T(8,128)}, u32[]{:S(2)}) copy-start(f32[1,2,32,32,512]{4,3,2,1,0:T(8,128)} %forward_ref.3) | copy-start | bytes 12582916
  18.3 8.4 %copy-start.7 = (s32[1,1,1,512]{3,2,1,0:T(1,128)S(1)}, s32[1,1,1,512]{3,2,1,0:T(1,128)}, u32[]{:S(2)}) copy-start(s32[1,1,1,512]{3,2,1,0:T(1,128)} %param.14) | copy-start | bytes 6148
  19.8 13.7 %collective-permute-start.4 = (bf16[32,4,512]{2,1,0:T(4,128)(2,1)S(1)}, bf16[32,4,512]{2,1,0:T(4,128)(2,1)S(1)}, u32[]{:S(2)}, u32[]{:S(2)}) collective-permute-start(bf16[32,4,512]{2,1,0:T(4,128)(2,1)S(1)} %get-tuple-element.29), channel_id=1, source_target_pairs={{0,7},{1,2},{2,1},{3,4},{4,3},{5,6},{6,5},{7,0},{8,15},{9,10},{10,... | collective-permute-start | bytes 393224 | tf_op jit(solution)/shard_map/ppermute | solution.py:44
  23.3 10.2 %collective-permute-start.5 = (bf16[32,4,512]{2,1,0:T(4,128)(2,1)S(1)}, bf16[32,4,512]{2,1,0:T(4,128)(2,1)S(1)}, u32[]{:S(2)}, u32[]{:S(2)}) collective-permute-start(bf16[32,4,512]{2,1,0:T(4,128)(2,1)S(1)} %get-tuple-element.30), channel_id=1, source_target_pairs={{0,1},{1,0},{2,3},{3,2},{4,5},{5,4},{6,7},{7,6},{8,9},{9,8},{10,11... | collective-permute-start | bytes 393224 | tf_op jit(solution)/shard_map/ppermute | solution.py:43
  23.5 9.9 %collective-permute-start.6 = (bf16[4,32,512]{2,1,0:T(8,128)(2,1)S(1)}, bf16[4,32,512]{2,1,0:T(8,128)(2,1)S(1)}, u32[]{:S(2)}, u32[]{:S(2)}) collective-permute-start(bf16[4,32,512]{2,1,0:T(8,128)(2,1)S(1)} %get-tuple-element.31), channel_id=1, source_target_pairs={{0,56},{8,16},{16,8},{24,32},{32,24},{40,48},{48,40},{56,0},{1,57}... | collective-permute-start | bytes 393224 | tf_op jit(solution)/shard_map/ppermute | solution.py:42
  26.0 7.5 %collective-permute-start.7 = (bf16[4,32,512]{2,1,0:T(8,128)(2,1)S(1)}, bf16[4,32,512]{2,1,0:T(8,128)(2,1)S(1)}, u32[]{:S(2)}, u32[]{:S(2)}) collective-permute-start(bf16[4,32,512]{2,1,0:T(8,128)(2,1)S(1)} %get-tuple-element.32), channel_id=1, source_target_pairs={{0,8},{8,0},{16,24},{24,16},{32,40},{40,32},{48,56},{56,48},{1,9},... | collective-permute-start | bytes 393224 | tf_op jit(solution)/shard_map/ppermute | solution.py:41

commit v5 on v4

--- a/solution.py
+++ b/solution.py
@@ -27,10 +27,11 @@
 SWAP_B = [(i, (i + 1) % NDEV if i % 2 else (i - 1) % NDEV) for i in range(NDEV)]
 
 
-def depth_band():
-    band = np.zeros((CZ, CZ), np.float64)
+def banded(size, block):
+    band = np.zeros((block, block), np.float64)
     for k, weight in enumerate(COEFFS, 1):
-        band += weight * (np.eye(CZ, k=k) + np.eye(CZ, k=-k))
+        band += weight * (np.eye(block, k=k) + np.eye(block, k=-k))
+    band = np.kron(np.eye(size // block), band)
     high = band.astype(jnp.bfloat16)
     low = (band - high.astype(np.float64)).astype(jnp.bfloat16)
     return high, low
@@ -85,36 +86,35 @@
     )
 
 
-def depth_term(block, high_ref, low_ref):
+def plane_terms(block, bands):
+    high, low, row_high, row_low = bands
     block = block.reshape(8 * CY, CZ)
     big = block.astype(BF16)
     small = (block - big.astype(F32)).astype(BF16)
-    term = jnp.dot(big, high_ref[...], preferred_element_type=F32)
-    term = term + jnp.dot(big, low_ref[...], preferred_element_type=F32)
-    term = term + jnp.dot(small, high_ref[...], preferred_element_type=F32)
+    term = jnp.dot(big, high[...], preferred_element_type=F32)
+    term = term + jnp.dot(big, low[...], preferred_element_type=F32)
+    term = term + jnp.dot(small, high[...], preferred_element_type=F32)
+    term = term + jnp.dot(row_high[...], big, preferred_element_type=F32)
+    term = term + jnp.dot(row_low[...], big, preferred_element_type=F32)
+    term = term + jnp.dot(row_high[...], small, preferred_element_type=F32)
     return term.reshape(8, CY, CZ)
 
 
-def clear_edges(ext):
-    ext[0:4, 8:40, :] = jnp.zeros((4, CY, CZ), F32)
-    ext[36:40, 8:40, :] = jnp.zeros((4, CY, CZ), F32)
-
-    def clear(x, carry):
-        ext[x + 4, 0:8, :] = jnp.zeros((8, CZ), F32)
-        ext[x + 4, 40:48, :] = jnp.zeros((8, CZ), F32)
-        return carry
-
-    lax.fori_loop(0, CX, clear, 0)
+def prepare(values, ext, zs, bands):
+    ext[0:4] = jnp.zeros((4, CY, CZ), F32)
+    ext[36:40] = jnp.zeros((4, CY, CZ), F32)
+    for i in range(4):
+        block = values[0, 8 * i : 8 * i + 8]
+        ext[8 * i + 4 : 8 * i + 12] = block
+        zs[8 * i : 8 * i + 8] = plane_terms(block, bands)
 
 
 def laplace_rows(ext, zs, x, ty):
-    rows = ext[x + 4, 8 * ty : 8 * ty + 24, :]
-    middle = rows[8:16]
-    summed = (3.0 * CENTER) * middle + zs[x, 8 * ty : 8 * ty + 8, :]
+    rows = slice(8 * ty, 8 * ty + 8)
+    middle = ext[x + 4, rows, :]
+    summed = (3.0 * CENTER) * middle + zs[x, rows, :]
     for k, weight in enumerate(COEFFS, 1):
-        nearby = ext[x + 4 + k, 8 * ty + 8 : 8 * ty + 16, :] + ext[x + 4 - k, 8 * ty + 8 : 8 * ty + 16, :]
-        nearby = nearby + rows[8 + k : 16 + k] + rows[8 - k : 16 - k]
-        summed = summed + weight * nearby
+        summed = summed + weight * (ext[x + 4 + k, rows, :] + ext[x + 4 - k, rows, :])
     return summed, middle
 
 
@@ -141,13 +141,10 @@
 
 
 def first_kernel(
-    now_ref, prev_ref, source_ref, speed_ref, high_ref, low_ref, one_ref, ext, zs,
+    now_ref, prev_ref, source_ref, speed_ref, high, low, row_high, row_low, one_ref, ext, zs,
 ):
-    clear_edges(ext)
-    for i in range(4):
-        block = now_ref[0, 8 * i : 8 * i + 8]
-        ext[8 * i + 4 : 8 * i + 12, 8:40, :] = block
-        zs[8 * i : 8 * i + 8] = depth_term(block, high_ref, low_ref)
+    bands = (high, low, row_high, row_low)
+    prepare(now_ref, ext, zs, bands)
 
     def plane(x, carry):
         for ty in range(4):
@@ -163,17 +160,14 @@
 
 
 def second_kernel(
-    where_ref, live_ref, foot_ref, one_ref, now_ref, speed_ref, source_ref, forward_ref, high_ref, low_ref,
+    where_ref, foot_ref, one_ref, now_ref, speed_ref, source_ref, forward_ref, high, low, row_high, row_low,
     done_hbm, two_ref, image_ref, out_ref, at_ref, ext, zs, sem,
 ):
+    bands = (high, low, row_high, row_low)
     copy = pltpu.make_async_copy(one_ref, done_hbm, sem)
     copy.start()
-    place_pieces(foot_ref, live_ref[0], where_ref[1] % 2, at_ref, out_ref)
-    clear_edges(ext)
-    for i in range(4):
-        block = one_ref[0, 8 * i : 8 * i + 8]
-        ext[8 * i + 4 : 8 * i + 12, 8:40, :] = block
-        zs[8 * i : 8 * i + 8] = depth_term(block, high_ref, low_ref)
+    place_pieces(foot_ref, where_ref[2], where_ref[1] % 2, at_ref, out_ref)
+    prepare(one_ref, ext, zs, bands)
 
     def plane(x, carry):
         for ty in range(4):
@@ -332,18 +326,24 @@
     copy.wait()
 
 
-def owner_kernel(in_ref, grad_ref, rows, ids, flat, spread):
+def owner_kernel(in_ref, grad_ref, ids, flat, spread):
     def unpack(j, carry):
-        for k in range(2 * CAP):
-            rows[8 * j + k] = in_ref[SLABS * j + k + k // CAP].astype(F32)
-        ids[pl.ds(pl.multiple_of(8 * j, 8), 8), :] = in_ref[SLABS * j + CAP].astype(F32)
+        lines = []
+        slots = []
+        for b in range(2):
+            base = SLABS * (2 * j + b)
+            pieces = [in_ref[base + k + k // CAP].astype(F32) for k in range(2 * CAP)]
+            lines.append(jnp.swapaxes(jnp.stack(pieces), 0, 1))
+            slots.append(in_ref[base + CAP].astype(F32))
+        at = pl.ds(pl.multiple_of(16 * j, 16), 16)
+        for y in range(8):
+            flat[at, 128 * y : 128 * y + 128] = jnp.concatenate([lines[0][y], lines[1][y]], axis=0).astype(BF16)
+        ids[at, :] = jnp.concatenate(slots, axis=0)
         return carry
 
-    lax.fori_loop(0, OWNERS // 2, unpack, 0, unroll=4)
+    lax.fori_loop(0, OWNERS // 4, unpack, 0, unroll=4)
     slot = lax.broadcasted_iota(jnp.int32, (OWNERS * CAP, 128), 1).astype(F32)
     onehot = jnp.where(ids[...] == slot, 1.0, 0.0).astype(BF16)
-    for y in range(8):
-        flat[:, 128 * y : 128 * y + 128] = rows[:, y, :].astype(BF16)
     spread[...] = lax.dot_general(onehot, flat[...], (((0,), (0,)), ((), ())), preferred_element_type=F32)
     for t in range(16):
         at = slice(8 * t, 8 * t + 8)
@@ -372,12 +372,12 @@
 def per_device(
     adjoint_prev, adjoint_now, speed_term, adjoint_source, forward_accel, footprint, live_counts
 ):
-    place = jnp.stack([lax.axis_index("gx"), lax.axis_index("gy")]).astype(jnp.int32)
+    place = jnp.stack([lax.axis_index("gx"), lax.axis_index("gy"), live_counts[0, 0, 0]]).astype(jnp.int32)
     faces_out = [pltpu.VMEM((4, CY, CZ), BF16)] * 2 + [pltpu.VMEM((CX, 4, CZ), BF16)] * 2
     level = pltpu.VMEM((1, CX, CY, CZ), F32)
     final = jax.ShapeDtypeStruct((1, CX, CY, CZ), F32)
     begun = pltpu.VMEM((OWNERS * SLABS, 4, 128), BF16)
-    ext = pltpu.VMEM((CX + 8, CY + 16, CZ), F32)
+    ext = pltpu.VMEM((CX + 8, CY, CZ), F32)
     depth = pltpu.VMEM((CX, CY, CZ), F32)
 
     send = pl.pallas_call(
@@ -398,16 +398,16 @@
     forward = near(forward_accel)
     now = near(adjoint_now)
     prev = near(adjoint_prev)
-    high, low = [near(jnp.asarray(term)) for term in depth_band()]
+    high, low, row_high, row_low = [near(jnp.asarray(term)) for term in banded(CZ, CZ) + banded(8 * CY, CY)]
     part_one = pl.pallas_call(
         first_kernel,
-        in_specs=[VMEM] * 6,
+        in_specs=[VMEM] * 8,
         out_specs=VMEM,
         out_shape=level,
         scratch_shapes=[ext, depth],
         compiler_params=params(12),
         name="level_one",
-    )(now, prev, source, speed, high, low)
+    )(now, prev, source, speed, high, low, row_high, row_low)
     whole_one, *send = pl.pallas_call(
         first_edge_kernel,
         in_specs=[SMEM] + [VMEM] * 6,
@@ -420,15 +420,14 @@
     faces = swap_faces(*send)
     level_one, part_two, image, outgoing, at = pl.pallas_call(
         second_kernel,
-        in_specs=[SMEM, SMEM] + [VMEM] * 8,
+        in_specs=[SMEM] + [VMEM] * 10,
         out_specs=[HBM] + [VMEM] * 4,
         out_shape=[final, level, level, begun, jax.ShapeDtypeStruct((1, SUB), jnp.int32)],
         scratch_shapes=[ext, depth, pltpu.SemaphoreType.DMA],
         compiler_params=params(12),
         name="level_two",
     )(
-        place, live_counts.reshape(-1), footprint.reshape(1, SUB),
-        whole_one, now, speed, source, forward, high, low,
+        place, footprint.reshape(1, SUB), whole_one, now, speed, source, forward, high, low, row_high, row_low,
     )
     _, _, outgoing, level_two = pl.pallas_call(
         second_edge_kernel,
@@ -447,7 +446,6 @@
         out_specs=VMEM,
         out_shape=jax.ShapeDtypeStruct((OWNERS, 1024), F32),
         scratch_shapes=[
-            pltpu.VMEM((OWNERS * CAP, 8, 128), F32),
             pltpu.VMEM((OWNERS * CAP, 128), F32),
             pltpu.VMEM((OWNERS * CAP, 1024), BF16),
             pltpu.VMEM((OWNERS, 1024), F32),

time: 69.9 us -> 66.9 us (0.957)
  Pallas kernels: 22.6 us -> 18.5 us
  waiting for transfers between devices: 0.02 us -> 0.83 us
    pallas_call x2, Pallas kernels: 12.2 us -> 9.97 us  [the longest x1 5.71 us: per_device(): pl.pallas_call(second_kernel, in_specs=[SMEM] + [VMEM] * 10, out_specs=[H...]
    pallas_call x1, Pallas kernels: 4.01 us -> 2.13 us  [per_device(): pl.pallas_call(owner_kernel, in_specs=[VMEM], out_specs=VMEM, out_shape=j...]
    ppermute x2, waiting for transfers between devices: 0.01 us -> 0.81 us  [swap_faces(): lax.ppermute(y0, 'gy', SWAP_A)]
  transfers between devices with their start and end apart: 8 -> 8, of which waited for: 0 -> 1; matrix products, arithmetic and copies ran while one was open for 0% -> 0% of each run, Pallas kernels for 17% -> 15%
where the time goes in v5:
time: 66.9 us; the launch traced here: 66.8 us
  blocking collectives  29.4 us (44%)
  Pallas kernels  18.5 us (28%)
  starting transfers between devices  16.5 us (25%)
  between operations  1.48 us (2%)
  waiting for transfers between devices  0.83 us (1%)
    all_to_all x1, blocking collectives, per_device(): lax.all_to_all(outgoing, ('shot', 'gx', 'gy'), split_axis=0, concat_axis=...  29.4 us
    ppermute x2, starting transfers between devices, swap_faces(): lax.ppermute(y1, 'gy', SWAP_B)  10.9 us
    pallas_call x1, Pallas kernels, per_device(): pl.pallas_call(second_kernel, in_specs=[SMEM] + [VMEM] * 10, out_specs=[H...  5.71 us
    ppermute x2, starting transfers between devices, swap_faces(): lax.ppermute(x1, 'gx', SWAP_B)  5.29 us
    pallas_call x1, Pallas kernels, per_device(): pl.pallas_call(first_kernel, in_specs=[VMEM] * 8, out_specs=VMEM, out_sha...  4.26 us
    pallas_call x1, Pallas kernels, per_device(): pl.pallas_call(second_edge_kernel, in_specs=[SMEM, SMEM] + [VMEM] * 9, ou...  2.87 us
    pallas_call x1, Pallas kernels, per_device(): pl.pallas_call(face_kernel, in_specs=[SMEM, HBM], out_specs=[VMEM] * 4, o...  2.15 us
    pallas_call x1, Pallas kernels, per_device(): pl.pallas_call(owner_kernel, in_specs=[VMEM], out_specs=VMEM, out_shape=j...  2.13 us
  transfers between devices with their start and end apart: 8, of which 1 were waited for; matrix products, arithmetic and copies ran while one was open for 0% of the time, Pallas kernels for 15%

profile of v5, /device:TPU:1, one launch (start us, length us, event | category | flops | bytes accessed | tf_op | source)
XLA Modules:
  0.0 66.8 jit_solution(9575909191363685330)
XLA Ops:
  1.3 0.1 pad_add_fusion.where_ref
  1.4 0.0 copy-start.5
  1.4 0.0 copy-start.6
  1.4 0.0 copy-start.7
  1.4 0.0 copy-start.8
  1.4 2.1 %faces.1 = (bf16[4,32,512]{2,1,0:T(8,128)(2,1)S(1)}, bf16[4,32,512]{2,1,0:T(8,128)(2,1)S(1)}, bf16[32,4,512]{2,1,0:T(4,128)(2,1)S(1)}, bf16[32,4,512]{2,1,0:T(4,128)(2,1)S(1)}) custom-call(s32[3]{0:T(128)S(1)} %pad_add_fusion.where_ref, f32[1,32,32,512]{3,2,1,0:T(8,128)} %now_ref.3), custom_call_target="tpu_custom_call" | custom-call | flops 10000000000 | bytes 1000000 | tf_op jit(solution)/shard_map/faces/pallas_call | solution.py:383
  3.6 7.3 %collective-permute-start = (bf16[32,4,512]{2,1,0:T(4,128)(2,1)S(1)}, bf16[32,4,512]{2,1,0:T(4,128)(2,1)S(1)}, u32[]{:S(2)}, u32[]{:S(2)}) collective-permute-start(bf16[32,4,512]{2,1,0:T(4,128)(2,1)S(1)} %get-tuple-element.19), channel_id=1, source_target_pairs={{0,7},{1,2},{2,1},{3,4},{4,3},{5,6},{6,5},{7,0},{8,15},{9,10},{10,... | collective-permute-start | bytes 393224 | tf_op jit(solution)/shard_map/ppermute | solution.py:45
  10.9 0.0 collective-permute-start.1
  10.9 2.6 %collective-permute-start.2 = (bf16[4,32,512]{2,1,0:T(8,128)(2,1)S(1)}, bf16[4,32,512]{2,1,0:T(8,128)(2,1)S(1)}, u32[]{:S(2)}, u32[]{:S(2)}) collective-permute-start(bf16[4,32,512]{2,1,0:T(8,128)(2,1)S(1)} %get-tuple-element.21), channel_id=1, source_target_pairs={{0,56},{8,16},{16,8},{24,32},{32,24},{40,48},{48,40},{56,0},{1,57}... | collective-permute-start | bytes 393224 | tf_op jit(solution)/shard_map/ppermute | solution.py:43
  13.5 0.0 collective-permute-start.3
  13.5 0.0 copy-done
  13.5 0.0 copy-done.1
  13.5 4.3 %level_one.1.part_ref = f32[1,32,32,512]{3,2,1,0:T(8,128)S(1)} custom-call(f32[1,32,32,512]{3,2,1,0:T(8,128)S(1)} %copy-done.3, f32[1,32,32,512]{3,2,1,0:T(8,128)S(1)} %copy-done.4, f32[1,2,32,32,512]{4,3,2,1,0:T(8,128)S(1)} %copy-done.1, f32[1,32,32,512]{3,2,1,0:T(8,128)S(1)} %copy-done, bf16[512,512]{1,0:T(8,128)(2,1)S(1)} %copy-done.6, ...), custom_call_target="tpu_custom_call" | custom-call | tf_op jit(solution)/shard_map/level_one/pallas_call | solution.py:402
  17.8 0.0 copy-start.2
  17.8 0.0 copy-start.9
  17.8 0.0 collective-permute-done.ry1
  17.8 0.8 %collective-permute-done.1.ry0 = bf16[32,4,512]{2,1,0:T(4,128)(2,1)S(1)} collective-permute-done((bf16[32,4,512]{2,1,0:T(4,128)(2,1)S(1)}, bf16[32,4,512]{2,1,0:T(4,128)(2,1)S(1)}, u32[]{:S(2)}, u32[]{:S(2)}) %collective-permute-start.1) | collective-permute-done | bytes 131104 | tf_op jit(solution)/shard_map/ppermute | solution.py:44
  18.7 0.0 collective-permute-done.2.rx1
  18.7 0.0 collective-permute-done.3.rx0
  18.7 1.4 %level_one_edge.1 = (f32[1,32,32,512]{3,2,1,0:T(8,128)S(1)}, bf16[4,32,512]{2,1,0:T(8,128)(2,1)S(1)}, bf16[4,32,512]{2,1,0:T(8,128)(2,1)S(1)}, bf16[32,4,512]{2,1,0:T(4,128)(2,1)S(1)}, bf16[32,4,512]{2,1,0:T(4,128)(2,1)S(1)}) custom-call(s32[3]{0:T(128)S(1)} %pad_add_fusion.where_ref, ...), custom_call_target="tpu_custom_call", output_to_operand_aliasing={{0}: (1, {})} | custom-call | tf_op jit(solution)/shard_map/level_one_edge/pallas_call | solution.py:411
  20.1 3.6 %collective-permute-start.4 = (bf16[32,4,512]{2,1,0:T(4,128)(2,1)S(1)}, bf16[32,4,512]{2,1,0:T(4,128)(2,1)S(1)}, u32[]{:S(2)}, u32[]{:S(2)}) collective-permute-start(bf16[32,4,512]{2,1,0:T(4,128)(2,1)S(1)} %get-tuple-element.29), channel_id=1, source_target_pairs={{0,7},{1,2},{2,1},{3,4},{4,3},{5,6},{6,5},{7,0},{8,15},{9,10},{10,... | collective-permute-start | bytes 393224 | tf_op jit(solution)/shard_map/ppermute | solution.py:45
  23.7 0.3 collective-permute-start.5
  24.0 2.7 %collective-permute-start.6 = (bf16[4,32,512]{2,1,0:T(8,128)(2,1)S(1)}, bf16[4,32,512]{2,1,0:T(8,128)(2,1)S(1)}, u32[]{:S(2)}, u32[]{:S(2)}) collective-permute-start(bf16[4,32,512]{2,1,0:T(8,128)(2,1)S(1)} %get-tuple-element.31), channel_id=1, source_target_pairs={{0,56},{8,16},{16,8},{24,32},{32,24},{40,48},{48,40},{56,0},{1,57}... | collective-permute-start | bytes 393224 | tf_op jit(solution)/shard_map/ppermute | solution.py:43
  26.7 0.0 collective-permute-start.7
  26.7 5.7 %level_two.1 = (f32[1,32,32,512]{3,2,1,0:T(8,128)}, f32[1,32,32,512]{3,2,1,0:T(8,128)S(1)}, f32[1,32,32,512]{3,2,1,0:T(8,128)S(1)}, bf16[1152,4,128]{2,1,0:T(4,128)(2,1)S(1)}, s32[1,512]{1,0:T(1,128)S(1)}) custom-call(s32[3]{0:T(128)S(1)} %pad_add_fusion.where_ref, s32[1,512]{1,0:T(1,128)S(1)} %bitcast.7, f32[1,32,32,512]{3,2,1,0:T(8,128)S(1)} %get-tuple-element.23.one_ref, ...), custom_call_target="tpu_custom_call" | custom-call | tf_op jit(solution)/shard_map/level_two/pallas_call | solution.py:421
  32.4 0.0 collective-permute-done.4.ry1
  32.4 0.0 collective-permute-done.5.ry0
  32.4 0.0 collective-permute-done.6.rx1
  32.4 0.0 collective-permute-done.7.rx0
  32.4 2.9 %level_two_edge.1 = (f32[1,32,32,512]{3,2,1,0:T(8,128)S(1)}, f32[1,32,32,512]{3,2,1,0:T(8,128)S(1)}, bf16[1152,4,128]{2,1,0:T(4,128)(2,1)S(1)}, f32[1,32,32,512]{3,2,1,0:T(8,128)}) custom-call(s32[3]{0:T(128)S(1)} %pad_add_fusion.where_ref, s32[1,512]{1,0:T(1,128)S(1)} %get-tuple-element.25.at_ref, ...), custom_call_target="tpu_custom_call", output_to_operand_aliasing={{0}: (2, {}), {1}: (3, {}), {2}: (4, {})} | custom-call | tf_op jit(solution)/shard_map/level_two_edge/pallas_call | solution.py:432
  35.3 29.4 %all_to_all.5 = bf16[1152,4,128]{2,1,0:T(4,128)(2,1)S(1)} all-to-all(bf16[1152,4,128]{2,1,0:T(4,128)(2,1)S(1)} %get-tuple-element.34), channel_id=1, replica_groups=mesh['shot'=2,'gx'=8,'gy'=8] {'shot','gx','gy'}, dimensions={0} | all-to-all | bytes 2359296 | tf_op jit(solution)/shard_map/all_to_all | solution.py:442
  64.7 2.1 %owner_sum.1 = f32[128,1024]{1,0:T(8,128)} custom-call(bf16[576,8,128]{2,1,0:T(8,128)(2,1)S(1)} %bitcast.6), custom_call_target="tpu_custom_call" | custom-call | tf_op jit(solution)/shard_map/owner_sum/pallas_call | solution.py:443
  (12 shorter events, 0.0 us)
Async XLA Ops:
  1.4 12.1 %copy-start = (f32[1,32,32,512]{3,2,1,0:T(8,128)S(1)}, f32[1,32,32,512]{3,2,1,0:T(8,128)}, u32[]{:S(2)}) copy-start(f32[1,32,32,512]{3,2,1,0:T(8,128)} %speed_ref.7) | copy-start | bytes 6291460
  1.4 12.1 %copy-start.1 = (f32[1,2,32,32,512]{4,3,2,1,0:T(8,128)S(1)}, f32[1,2,32,32,512]{4,3,2,1,0:T(8,128)}, u32[]{:S(2)}) copy-start(f32[1,2,32,32,512]{4,3,2,1,0:T(8,128)} %source_ref.3) | copy-start | bytes 12582916
  1.4 12.1 %copy-start.3 = (f32[1,32,32,512]{3,2,1,0:T(8,128)S(1)}, f32[1,32,32,512]{3,2,1,0:T(8,128)}, u32[]{:S(2)}) copy-start(f32[1,32,32,512]{3,2,1,0:T(8,128)} %now_ref.3) | copy-start | bytes 6291460
  1.4 12.1 %copy-start.4 = (f32[1,32,32,512]{3,2,1,0:T(8,128)S(1)}, f32[1,32,32,512]{3,2,1,0:T(8,128)}, u32[]{:S(2)}) copy-start(f32[1,32,32,512]{3,2,1,0:T(8,128)} %prev_ref.1) | copy-start | bytes 6291460
  1.4 12.1 %copy-start.5 = (bf16[512,512]{1,0:T(8,128)(2,1)S(1)}, bf16[512,512]{1,0:T(8,128)(2,1)}, u32[]{:S(2)}) copy-start(bf16[512,512]{1,0:T(8,128)(2,1)} %constant.16.clone.low) | copy-start | bytes 1572868
  1.4 12.1 %copy-start.6 = (bf16[512,512]{1,0:T(8,128)(2,1)S(1)}, bf16[512,512]{1,0:T(8,128)(2,1)}, u32[]{:S(2)}) copy-start(bf16[512,512]{1,0:T(8,128)(2,1)} %constant.15.clone.high) | copy-start | bytes 1572868
  1.4 12.1 %copy-start.7 = (bf16[256,256]{1,0:T(8,128)(2,1)S(1)}, bf16[256,256]{1,0:T(8,128)(2,1)}, u32[]{:S(2)}) copy-start(bf16[256,256]{1,0:T(8,128)(2,1)} %constant.18.clone.row_low) | copy-start | bytes 393220
  1.4 12.1 %copy-start.8 = (bf16[256,256]{1,0:T(8,128)(2,1)S(1)}, bf16[256,256]{1,0:T(8,128)(2,1)}, u32[]{:S(2)}) copy-start(bf16[256,256]{1,0:T(8,128)(2,1)} %constant.17.clone.row_high) | copy-start | bytes 393220
  3.6 14.3 %collective-permute-start = (bf16[32,4,512]{2,1,0:T(4,128)(2,1)S(1)}, bf16[32,4,512]{2,1,0:T(4,128)(2,1)S(1)}, u32[]{:S(2)}, u32[]{:S(2)}) collective-permute-start(bf16[32,4,512]{2,1,0:T(4,128)(2,1)S(1)} %get-tuple-element.19), channel_id=1, source_target_pairs={{0,7},{1,2},{2,1},{3,4},{4,3},{5,6},{6,5},{7,0},{8,15},{9,10},{10,... | collective-permute-start | bytes 393224 | tf_op jit(solution)/shard_map/ppermute | solution.py:45
  10.9 7.8 %collective-permute-start.1 = (bf16[32,4,512]{2,1,0:T(4,128)(2,1)S(1)}, bf16[32,4,512]{2,1,0:T(4,128)(2,1)S(1)}, u32[]{:S(2)}, u32[]{:S(2)}) collective-permute-start(bf16[32,4,512]{2,1,0:T(4,128)(2,1)S(1)} %get-tuple-element.20), channel_id=1, source_target_pairs={{0,1},{1,0},{2,3},{3,2},{4,5},{5,4},{6,7},{7,6},{8,9},{9,8},{10,11... | collective-permute-start | bytes 393224 | tf_op jit(solution)/shard_map/ppermute | solution.py:44
  10.9 7.8 %collective-permute-start.2 = (bf16[4,32,512]{2,1,0:T(8,128)(2,1)S(1)}, bf16[4,32,512]{2,1,0:T(8,128)(2,1)S(1)}, u32[]{:S(2)}, u32[]{:S(2)}) collective-permute-start(bf16[4,32,512]{2,1,0:T(8,128)(2,1)S(1)} %get-tuple-element.21), channel_id=1, source_target_pairs={{0,56},{8,16},{16,8},{24,32},{32,24},{40,48},{48,40},{56,0},{1,57}... | collective-permute-start | bytes 393224 | tf_op jit(solution)/shard_map/ppermute | solution.py:43
  13.5 5.2 %collective-permute-start.3 = (bf16[4,32,512]{2,1,0:T(8,128)(2,1)S(1)}, bf16[4,32,512]{2,1,0:T(8,128)(2,1)S(1)}, u32[]{:S(2)}, u32[]{:S(2)}) collective-permute-start(bf16[4,32,512]{2,1,0:T(8,128)(2,1)S(1)} %get-tuple-element.22), channel_id=1, source_target_pairs={{0,8},{8,0},{16,24},{24,16},{32,40},{40,32},{48,56},{56,48},{1,9},... | collective-permute-start | bytes 393224 | tf_op jit(solution)/shard_map/ppermute | solution.py:42
  17.8 8.9 %copy-start.2 = (f32[1,2,32,32,512]{4,3,2,1,0:T(8,128)S(1)}, f32[1,2,32,32,512]{4,3,2,1,0:T(8,128)}, u32[]{:S(2)}) copy-start(f32[1,2,32,32,512]{4,3,2,1,0:T(8,128)} %forward_ref.3) | copy-start | bytes 12582916
  17.8 8.9 %copy-start.9 = (s32[1,1,1,512]{3,2,1,0:T(1,128)S(1)}, s32[1,1,1,512]{3,2,1,0:T(1,128)}, u32[]{:S(2)}) copy-start(s32[1,1,1,512]{3,2,1,0:T(1,128)} %param.16) | copy-start | bytes 6148
  20.1 12.3 %collective-permute-start.4 = (bf16[32,4,512]{2,1,0:T(4,128)(2,1)S(1)}, bf16[32,4,512]{2,1,0:T(4,128)(2,1)S(1)}, u32[]{:S(2)}, u32[]{:S(2)}) collective-permute-start(bf16[32,4,512]{2,1,0:T(4,128)(2,1)S(1)} %get-tuple-element.29), channel_id=1, source_target_pairs={{0,7},{1,2},{2,1},{3,4},{4,3},{5,6},{6,5},{7,0},{8,15},{9,10},{10,... | collective-permute-start | bytes 393224 | tf_op jit(solution)/shard_map/ppermute | solution.py:45
  23.7 8.7 %collective-permute-start.5 = (bf16[32,4,512]{2,1,0:T(4,128)(2,1)S(1)}, bf16[32,4,512]{2,1,0:T(4,128)(2,1)S(1)}, u32[]{:S(2)}, u32[]{:S(2)}) collective-permute-start(bf16[32,4,512]{2,1,0:T(4,128)(2,1)S(1)} %get-tuple-element.30), channel_id=1, source_target_pairs={{0,1},{1,0},{2,3},{3,2},{4,5},{5,4},{6,7},{7,6},{8,9},{9,8},{10,11... | collective-permute-start | bytes 393224 | tf_op jit(solution)/shard_map/ppermute | solution.py:44
  24.0 8.5 %collective-permute-start.6 = (bf16[4,32,512]{2,1,0:T(8,128)(2,1)S(1)}, bf16[4,32,512]{2,1,0:T(8,128)(2,1)S(1)}, u32[]{:S(2)}, u32[]{:S(2)}) collective-permute-start(bf16[4,32,512]{2,1,0:T(8,128)(2,1)S(1)} %get-tuple-element.31), channel_id=1, source_target_pairs={{0,56},{8,16},{16,8},{24,32},{32,24},{40,48},{48,40},{56,0},{1,57}... | collective-permute-start | bytes 393224 | tf_op jit(solution)/shard_map/ppermute | solution.py:43
  26.7 5.8 %collective-permute-start.7 = (bf16[4,32,512]{2,1,0:T(8,128)(2,1)S(1)}, bf16[4,32,512]{2,1,0:T(8,128)(2,1)S(1)}, u32[]{:S(2)}, u32[]{:S(2)}) collective-permute-start(bf16[4,32,512]{2,1,0:T(8,128)(2,1)S(1)} %get-tuple-element.32), channel_id=1, source_target_pairs={{0,8},{8,0},{16,24},{24,16},{32,40},{40,32},{48,56},{56,48},{1,9},... | collective-permute-start | bytes 393224 | tf_op jit(solution)/shard_map/ppermute | solution.py:42

commit v6 on v5

--- a/solution.py
+++ b/solution.py
@@ -13,6 +13,7 @@
 CY = 32
 CZ = 512
 OWNERS = 128
+TILES_DEV = 128
 CAP = 4
 SUB = 512
 SLABS = 9
@@ -68,9 +69,9 @@
         sy1[...] = get_y(0).astype(BF16)
 
 
-def face_kernel(where_ref, now_hbm, sx0, sx1, sy0, sy1, xs, ys, sems):
-    gx = where_ref[0]
-    gy = where_ref[1]
+def face_kernel(now_hbm, sx0, sx1, sy0, sy1, xs, ys, sems):
+    gx = lax.axis_index("gx")
+    gy = lax.axis_index("gy")
     copies = [
         pltpu.make_async_copy(now_hbm.at[0, 0:4], xs.at[0], sems.at[0]),
         pltpu.make_async_copy(now_hbm.at[0, 28:32], xs.at[1], sems.at[1]),
@@ -118,11 +119,10 @@
     return summed, middle
 
 
-def place_pieces(foot_ref, live, odd, at_ref, out_ref):
+def place_pieces(foot_ref, odd, at_ref, out_ref):
     listed = foot_ref[...]
-    owner = listed // OWNERS
-    piece = lax.broadcasted_iota(jnp.int32, (1, SUB), 1)
-    slot = jnp.where(piece < live, listed % OWNERS, -1)
+    owner = listed // TILES_DEV % OWNERS
+    slot = jnp.where(listed < OWNERS * TILES_DEV, listed % TILES_DEV, -1)
     match = owner == lax.broadcasted_iota(jnp.int32, (OWNERS, SUB), 0)
     earlier = lax.broadcasted_iota(jnp.int32, (SUB, SUB), 0) < lax.broadcasted_iota(jnp.int32, (SUB, SUB), 1)
     ahead = jnp.dot(
@@ -160,13 +160,15 @@
 
 
 def second_kernel(
-    where_ref, foot_ref, one_ref, now_ref, speed_ref, source_ref, forward_ref, high, low, row_high, row_low,
-    done_hbm, two_ref, image_ref, out_ref, at_ref, ext, zs, sem,
+    foot_ref, one_ref, now_ref, speed_ref, source_ref, forward_ref, high, low, row_high, row_low,
+    done_hbm, two_ref, image_ref, out_ref, at_smem, ext, zs, at_ref, sem, at_sem,
 ):
     bands = (high, low, row_high, row_low)
     copy = pltpu.make_async_copy(one_ref, done_hbm, sem)
     copy.start()
-    place_pieces(foot_ref, where_ref[2], where_ref[1] % 2, at_ref, out_ref)
+    place_pieces(foot_ref, lax.axis_index("gy") % 2, at_ref, out_ref)
+    at_copy = pltpu.make_async_copy(at_ref, at_smem, at_sem)
+    at_copy.start()
     prepare(one_ref, ext, zs, bands)
 
     def plane(x, carry):
@@ -182,6 +184,7 @@
         return carry
 
     lax.fori_loop(0, CX, plane, 0)
+    at_copy.wait()
     copy.wait()
 
 
@@ -255,10 +258,10 @@
         y_sides(ry1, ry0)
 
 
-def first_edge_kernel(where_ref, part_ref, speed_ref, ry1, ry0, rx1, rx0, one_ref, sx0, sx1, sy0, sy1):
+def first_edge_kernel(part_ref, speed_ref, ry0, ry1, rx0, rx1, one_ref, sx0, sx1, sy0, sy1):
     del part_ref
-    gx = where_ref[0]
-    gy = where_ref[1]
+    gx = lax.axis_index("gx")
+    gy = lax.axis_index("gy")
 
     def update(x, rows, lanes, term):
         at = (0, x, rows, lanes)
@@ -287,12 +290,12 @@
 
 
 def second_edge_kernel(
-    where_ref, at_ref, part_ref, image_in, begun_ref, speed_ref, forward_ref, ry1, ry0, rx1, rx0,
+    at_ref, part_ref, image_in, begun_ref, speed_ref, forward_ref, ry0, ry1, rx0, rx1,
     two_ref, image_ref, out_ref, done_hbm, sem,
 ):
     del part_ref, image_in, begun_ref
-    gx = where_ref[0]
-    gy = where_ref[1]
+    gx = lax.axis_index("gx")
+    gy = lax.axis_index("gy")
 
     def update(x, rows, lanes, term):
         at = (0, x, rows, lanes)
@@ -372,7 +375,9 @@
 def per_device(
     adjoint_prev, adjoint_now, speed_term, adjoint_source, forward_accel, footprint, live_counts
 ):
-    place = jnp.stack([lax.axis_index("gx"), lax.axis_index("gy"), live_counts[0, 0, 0]]).astype(jnp.int32)
+    piece = lax.broadcasted_iota(jnp.int32, footprint.shape, 3)
+    marked = jnp.where(piece < live_counts[..., None], footprint, footprint + OWNERS * TILES_DEV)
+    marked = near(marked.reshape(1, SUB))
     faces_out = [pltpu.VMEM((4, CY, CZ), BF16)] * 2 + [pltpu.VMEM((CX, 4, CZ), BF16)] * 2
     level = pltpu.VMEM((1, CX, CY, CZ), F32)
     final = jax.ShapeDtypeStruct((1, CX, CY, CZ), F32)
@@ -382,7 +387,7 @@
 
     send = pl.pallas_call(
         face_kernel,
-        in_specs=[SMEM, HBM],
+        in_specs=[HBM],
         out_specs=[VMEM] * 4,
         out_shape=faces_out,
         scratch_shapes=[
@@ -391,7 +396,7 @@
         compiler_params=params(8),
         cost_estimate=pl.CostEstimate(flops=FACES_FLOPS, bytes_accessed=1_000_000, transcendentals=0),
         name="faces",
-    )(place, far(adjoint_now))
+    )(far(adjoint_now))
     faces = swap_faces(*send)
     speed = near(speed_term)
     source = near(adjoint_source)
@@ -410,35 +415,37 @@
     )(now, prev, source, speed, high, low, row_high, row_low)
     whole_one, *send = pl.pallas_call(
         first_edge_kernel,
-        in_specs=[SMEM] + [VMEM] * 6,
+        in_specs=[VMEM] * 6,
         out_specs=[VMEM] * 5,
         out_shape=[level] + faces_out,
-        input_output_aliases={1: 0},
+        input_output_aliases={0: 0},
         compiler_params=params(4),
         name="level_one_edge",
-    )(place, part_one, speed, *[near(face) for face in faces[::-1]])
+    )(part_one, speed, *[near(faces[i]) for i in (2, 3, 0, 1)])
     faces = swap_faces(*send)
     level_one, part_two, image, outgoing, at = pl.pallas_call(
         second_kernel,
-        in_specs=[SMEM] + [VMEM] * 10,
-        out_specs=[HBM] + [VMEM] * 4,
-        out_shape=[final, level, level, begun, jax.ShapeDtypeStruct((1, SUB), jnp.int32)],
-        scratch_shapes=[ext, depth, pltpu.SemaphoreType.DMA],
+        in_specs=[VMEM] * 10,
+        out_specs=[HBM, VMEM, VMEM, VMEM, SMEM],
+        out_shape=[final, level, level, begun, pltpu.SMEM((1, SUB), jnp.int32)],
+        scratch_shapes=[
+            ext, depth, pltpu.VMEM((1, SUB), jnp.int32), pltpu.SemaphoreType.DMA, pltpu.SemaphoreType.DMA,
+        ],
         compiler_params=params(12),
         name="level_two",
     )(
-        place, footprint.reshape(1, SUB), whole_one, now, speed, source, forward, high, low, row_high, row_low,
+        marked, whole_one, now, speed, source, forward, high, low, row_high, row_low,
     )
     _, _, outgoing, level_two = pl.pallas_call(
         second_edge_kernel,
-        in_specs=[SMEM, SMEM] + [VMEM] * 9,
+        in_specs=[SMEM] + [VMEM] * 9,
         out_specs=[VMEM, VMEM, VMEM, HBM],
         out_shape=[level, level, begun, final],
         scratch_shapes=[pltpu.SemaphoreType.DMA],
-        input_output_aliases={2: 0, 3: 1, 4: 2},
+        input_output_aliases={1: 0, 2: 1, 3: 2},
         compiler_params=params(4),
         name="level_two_edge",
-    )(place, at, part_two, image, outgoing, speed, forward, *[near(face) for face in faces[::-1]])
+    )(at, part_two, image, outgoing, speed, forward, *[near(faces[i]) for i in (2, 3, 0, 1)])
     incoming = lax.all_to_all(outgoing, ("shot", "gx", "gy"), split_axis=0, concat_axis=0, tiled=True)
     gradient = pl.pallas_call(
         owner_kernel,

time: 66.9 us -> 63.1 us (0.943)
  Pallas kernels: 18.5 us -> 16.9 us
  starting transfers between devices: 16.5 us -> 15.2 us
  waiting for transfers between devices: 0.83 us -> 0.02 us
    ppermute x2, starting transfers between devices: 10.9 us -> 5.88 us  [swap_faces(): lax.ppermute(y1, 'gy', SWAP_B)]
    ppermute x2, starting transfers between devices: 0.26 us -> 4.4 us  [swap_faces(): lax.ppermute(y0, 'gy', SWAP_A)]
    pallas_call x4, Pallas kernels: 12.1 us -> 10.2 us  [the longest x1 5.52 us: per_device(): pl.pallas_call(second_kernel, in_specs=[VMEM] * 10, out_specs=[HBM, VMEM,...]
    ppermute x2, starting transfers between devices: 5.29 us -> 3.71 us  [swap_faces(): lax.ppermute(x1, 'gx', SWAP_B)]
    ppermute x2, starting transfers between devices: 0.01 us -> 1.22 us  [swap_faces(): lax.ppermute(x0, 'gx', SWAP_A)]
    ppermute x2, waiting for transfers between devices: 0.81 us -> 0.01 us  [swap_faces(): lax.ppermute(y0, 'gy', SWAP_A)]
  transfers between devices with their start and end apart: 8 -> 8, of which waited for: 1 -> 0; matrix products, arithmetic and copies ran while one was open for 0% -> 0% of each run, Pallas kernels for 15% -> 16%
where the time goes in v6:
time: 63.1 us; the launch traced here: 63 us
  blocking collectives  29.3 us (46%)
  Pallas kernels  16.9 us (27%)
  starting transfers between devices  15.2 us (24%)
  between operations  1.54 us (2%)
    all_to_all x1, blocking collectives, per_device(): lax.all_to_all(outgoing, ('shot', 'gx', 'gy'), split_axis=0, concat_axis=...  29.3 us
    ppermute x2, starting transfers between devices, swap_faces(): lax.ppermute(y1, 'gy', SWAP_B)  5.88 us
    pallas_call x1, Pallas kernels, per_device(): pl.pallas_call(second_kernel, in_specs=[VMEM] * 10, out_specs=[HBM, VMEM,...  5.52 us
    pallas_call x1, Pallas kernels, per_device(): pl.pallas_call(first_kernel, in_specs=[VMEM] * 8, out_specs=VMEM, out_sha...  4.59 us
    ppermute x2, starting transfers between devices, swap_faces(): lax.ppermute(y0, 'gy', SWAP_A)  4.4 us
    ppermute x2, starting transfers between devices, swap_faces(): lax.ppermute(x1, 'gx', SWAP_B)  3.71 us
    pallas_call x1, Pallas kernels, per_device(): pl.pallas_call(second_edge_kernel, in_specs=[SMEM] + [VMEM] * 9, out_spec...  2.28 us
    pallas_call x1, Pallas kernels, per_device(): pl.pallas_call(owner_kernel, in_specs=[VMEM], out_specs=VMEM, out_shape=j...  2.13 us
  transfers between devices with their start and end apart: 8, of which 0 were waited for; matrix products, arithmetic and copies ran while one was open for 0% of the time, Pallas kernels for 16%

profile of v6, /device:TPU:1, one launch (start us, length us, event | category | flops | bytes accessed | tf_op | source)
XLA Modules:
  0.0 63.0 jit_solution(949684073176419698)
XLA Ops:
  0.6 0.0 copy-start.5
  0.6 0.0 copy-start.6
  0.7 0.0 copy-start.7
  0.7 0.0 copy-start.8
  0.7 0.0 copy-start.3
  0.7 0.0 copy-start
  0.7 0.0 copy-start.4
  0.7 1.5 %faces.1 = (bf16[4,32,512]{2,1,0:T(8,128)(2,1)S(1)}, bf16[4,32,512]{2,1,0:T(8,128)(2,1)S(1)}, bf16[32,4,512]{2,1,0:T(4,128)(2,1)S(1)}, bf16[32,4,512]{2,1,0:T(4,128)(2,1)S(1)}) custom-call(f32[1,32,32,512]{3,2,1,0:T(8,128)} %now_ref.3), custom_call_target="tpu_custom_call" | custom-call | flops 10000000000 | bytes 1000000 | tf_op jit(solution)/shard_map/faces/pallas_call | solution.py:388
  2.2 3.8 %collective-permute-start = (bf16[32,4,512]{2,1,0:T(4,128)(2,1)S(1)}, bf16[32,4,512]{2,1,0:T(4,128)(2,1)S(1)}, u32[]{:S(2)}, u32[]{:S(2)}) collective-permute-start(bf16[32,4,512]{2,1,0:T(4,128)(2,1)S(1)} %get-tuple-element.19), channel_id=1, source_target_pairs={{0,1},{1,0},{2,3},{3,2},{4,5},{5,4},{6,7},{7,6},{8,9},{9,8},{10,11... | collective-permute-start | bytes 393224 | tf_op jit(solution)/shard_map/ppermute | solution.py:45
  6.0 3.6 %collective-permute-start.1 = (bf16[32,4,512]{2,1,0:T(4,128)(2,1)S(1)}, bf16[32,4,512]{2,1,0:T(4,128)(2,1)S(1)}, u32[]{:S(2)}, u32[]{:S(2)}) collective-permute-start(bf16[32,4,512]{2,1,0:T(4,128)(2,1)S(1)} %get-tuple-element.20), channel_id=1, source_target_pairs={{0,7},{1,2},{2,1},{3,4},{4,3},{5,6},{6,5},{7,0},{8,15},{9,10},{10,... | collective-permute-start | bytes 393224 | tf_op jit(solution)/shard_map/ppermute | solution.py:46
  9.6 1.2 %collective-permute-start.2 = (bf16[4,32,512]{2,1,0:T(8,128)(2,1)S(1)}, bf16[4,32,512]{2,1,0:T(8,128)(2,1)S(1)}, u32[]{:S(2)}, u32[]{:S(2)}) collective-permute-start(bf16[4,32,512]{2,1,0:T(8,128)(2,1)S(1)} %get-tuple-element.21), channel_id=1, source_target_pairs={{0,8},{8,0},{16,24},{24,16},{32,40},{40,32},{48,56},{56,48},{1,9},... | collective-permute-start | bytes 393224 | tf_op jit(solution)/shard_map/ppermute | solution.py:43
  10.8 2.8 %collective-permute-start.3 = (bf16[4,32,512]{2,1,0:T(8,128)(2,1)S(1)}, bf16[4,32,512]{2,1,0:T(8,128)(2,1)S(1)}, u32[]{:S(2)}, u32[]{:S(2)}) collective-permute-start(bf16[4,32,512]{2,1,0:T(8,128)(2,1)S(1)} %get-tuple-element.22), channel_id=1, source_target_pairs={{0,56},{8,16},{16,8},{24,32},{32,24},{40,48},{48,40},{56,0},{1,57}... | collective-permute-start | bytes 393224 | tf_op jit(solution)/shard_map/ppermute | solution.py:44
  14.3 4.6 %level_one.1.part_ref = f32[1,32,32,512]{3,2,1,0:T(8,128)S(1)} custom-call(f32[1,32,32,512]{3,2,1,0:T(8,128)S(1)} %copy-done.3, f32[1,32,32,512]{3,2,1,0:T(8,128)S(1)} %copy-done.4, f32[1,2,32,32,512]{4,3,2,1,0:T(8,128)S(1)} %copy-done.2, f32[1,32,32,512]{3,2,1,0:T(8,128)S(1)} %copy-done, bf16[512,512]{1,0:T(8,128)(2,1)S(1)} %copy-done.6, ...), custom_call_target="tpu_custom_call" | custom-call | tf_op jit(solution)/shard_map/level_one/pallas_call | solution.py:407
  18.9 0.0 copy-start.9
  18.9 0.0 copy-start.1
  18.9 0.0 collective-permute-done.ry0
  19.0 0.0 collective-permute-done.1.ry1
  19.0 0.0 collective-permute-done.2.rx0
  19.0 0.0 collective-permute-done.3.rx1
  19.0 0.9 %level_one_edge.1 = (f32[1,32,32,512]{3,2,1,0:T(8,128)S(1)}, bf16[4,32,512]{2,1,0:T(8,128)(2,1)S(1)}, bf16[4,32,512]{2,1,0:T(8,128)(2,1)S(1)}, bf16[32,4,512]{2,1,0:T(4,128)(2,1)S(1)}, bf16[32,4,512]{2,1,0:T(4,128)(2,1)S(1)}) custom-call(f32[1,32,32,512]{3,2,1,0:T(8,128)S(1)} %level_one.1.part_ref, ...), custom_call_target="tpu_custom_call", output_to_operand_aliasing={{0}: (0, {})} | custom-call | tf_op jit(solution)/shard_map/level_one_edge/pallas_call | solution.py:416
  19.9 0.6 collective-permute-start.4
  20.5 2.3 %collective-permute-start.5 = (bf16[32,4,512]{2,1,0:T(4,128)(2,1)S(1)}, bf16[32,4,512]{2,1,0:T(4,128)(2,1)S(1)}, u32[]{:S(2)}, u32[]{:S(2)}) collective-permute-start(bf16[32,4,512]{2,1,0:T(4,128)(2,1)S(1)} %get-tuple-element.30), channel_id=1, source_target_pairs={{0,7},{1,2},{2,1},{3,4},{4,3},{5,6},{6,5},{7,0},{8,15},{9,10},{10,... | collective-permute-start | bytes 393224 | tf_op jit(solution)/shard_map/ppermute | solution.py:46
  22.8 0.0 collective-permute-start.6
  22.8 0.9 %collective-permute-start.7 = (bf16[4,32,512]{2,1,0:T(8,128)(2,1)S(1)}, bf16[4,32,512]{2,1,0:T(8,128)(2,1)S(1)}, u32[]{:S(2)}, u32[]{:S(2)}) collective-permute-start(bf16[4,32,512]{2,1,0:T(8,128)(2,1)S(1)} %get-tuple-element.32), channel_id=1, source_target_pairs={{0,56},{8,16},{16,8},{24,32},{32,24},{40,48},{48,40},{56,0},{1,57}... | collective-permute-start | bytes 393224 | tf_op jit(solution)/shard_map/ppermute | solution.py:44
  23.7 5.5 %level_two.1 = (f32[1,32,32,512]{3,2,1,0:T(8,128)}, f32[1,32,32,512]{3,2,1,0:T(8,128)S(1)}, f32[1,32,32,512]{3,2,1,0:T(8,128)S(1)}, bf16[1152,4,128]{2,1,0:T(4,128)(2,1)S(1)}, s32[1,512]{1,0:T(1,128)S(4)}) custom-call(s32[1,512]{1,0:T(1,128)S(1)} %fusion.foot_ref, f32[1,32,32,512]{3,2,1,0:T(8,128)S(1)} %get-tuple-element.23.one_ref, ...), custom_call_target="tpu_custom_call" | custom-call | tf_op jit(solution)/shard_map/level_two/pallas_call | solution.py:426
  29.3 0.0 collective-permute-done.4.ry0
  29.3 0.0 collective-permute-done.5.ry1
  29.3 0.0 collective-permute-done.6.rx0
  29.3 0.0 collective-permute-done.7.rx1
  29.3 2.3 %level_two_edge.1 = (f32[1,32,32,512]{3,2,1,0:T(8,128)S(1)}, f32[1,32,32,512]{3,2,1,0:T(8,128)S(1)}, bf16[1152,4,128]{2,1,0:T(4,128)(2,1)S(1)}, f32[1,32,32,512]{3,2,1,0:T(8,128)}) custom-call(s32[1,512]{1,0:T(1,128)S(4)} %get-tuple-element.25.at_ref, ...), custom_call_target="tpu_custom_call", output_to_operand_aliasing={{0}: (1, {}), {1}: (2, {}), {2}: (3, {})} | custom-call | tf_op jit(solution)/shard_map/level_two_edge/pallas_call | solution.py:439
  31.6 29.3 %all_to_all.5 = bf16[1152,4,128]{2,1,0:T(4,128)(2,1)S(1)} all-to-all(bf16[1152,4,128]{2,1,0:T(4,128)(2,1)S(1)} %get-tuple-element.34), channel_id=1, replica_groups=mesh['shot'=2,'gx'=8,'gy'=8] {'shot','gx','gy'}, dimensions={0} | all-to-all | bytes 2359296 | tf_op jit(solution)/shard_map/all_to_all | solution.py:449
  60.8 2.1 %owner_sum.1 = f32[128,1024]{1,0:T(8,128)} custom-call(bf16[576,8,128]{2,1,0:T(8,128)(2,1)S(1)} %bitcast.5), custom_call_target="tpu_custom_call" | custom-call | tf_op jit(solution)/shard_map/owner_sum/pallas_call | solution.py:450
  (12 shorter events, 0.0 us)
Async XLA Ops:
  0.6 13.6 %copy-start.5 = (bf16[512,512]{1,0:T(8,128)(2,1)S(1)}, bf16[512,512]{1,0:T(8,128)(2,1)}, u32[]{:S(2)}) copy-start(bf16[512,512]{1,0:T(8,128)(2,1)} %constant.11.clone.low) | copy-start | bytes 1572868
  0.6 13.6 %copy-start.6 = (bf16[512,512]{1,0:T(8,128)(2,1)S(1)}, bf16[512,512]{1,0:T(8,128)(2,1)}, u32[]{:S(2)}) copy-start(bf16[512,512]{1,0:T(8,128)(2,1)} %constant.10.clone.high) | copy-start | bytes 1572868
  0.7 13.6 %copy-start.7 = (bf16[256,256]{1,0:T(8,128)(2,1)S(1)}, bf16[256,256]{1,0:T(8,128)(2,1)}, u32[]{:S(2)}) copy-start(bf16[256,256]{1,0:T(8,128)(2,1)} %constant.13.clone.row_low) | copy-start | bytes 393220
  0.7 13.6 %copy-start.8 = (bf16[256,256]{1,0:T(8,128)(2,1)S(1)}, bf16[256,256]{1,0:T(8,128)(2,1)}, u32[]{:S(2)}) copy-start(bf16[256,256]{1,0:T(8,128)(2,1)} %constant.12.clone.row_high) | copy-start | bytes 393220
  0.7 13.6 %copy-start.3 = (f32[1,32,32,512]{3,2,1,0:T(8,128)S(1)}, f32[1,32,32,512]{3,2,1,0:T(8,128)}, u32[]{:S(2)}) copy-start(f32[1,32,32,512]{3,2,1,0:T(8,128)} %now_ref.3) | copy-start | bytes 6291460
  0.7 13.6 %copy-start = (f32[1,32,32,512]{3,2,1,0:T(8,128)S(1)}, f32[1,32,32,512]{3,2,1,0:T(8,128)}, u32[]{:S(2)}) copy-start(f32[1,32,32,512]{3,2,1,0:T(8,128)} %speed_ref.7) | copy-start | bytes 6291460
  0.7 13.6 %copy-start.4 = (f32[1,32,32,512]{3,2,1,0:T(8,128)S(1)}, f32[1,32,32,512]{3,2,1,0:T(8,128)}, u32[]{:S(2)}) copy-start(f32[1,32,32,512]{3,2,1,0:T(8,128)} %prev_ref.1) | copy-start | bytes 6291460
  0.7 13.6 %copy-start.2 = (f32[1,2,32,32,512]{4,3,2,1,0:T(8,128)S(1)}, f32[1,2,32,32,512]{4,3,2,1,0:T(8,128)}, u32[]{:S(2)}) copy-start(f32[1,2,32,32,512]{4,3,2,1,0:T(8,128)} %source_ref.3) | copy-start | bytes 12582916
  2.2 16.7 %collective-permute-start = (bf16[32,4,512]{2,1,0:T(4,128)(2,1)S(1)}, bf16[32,4,512]{2,1,0:T(4,128)(2,1)S(1)}, u32[]{:S(2)}, u32[]{:S(2)}) collective-permute-start(bf16[32,4,512]{2,1,0:T(4,128)(2,1)S(1)} %get-tuple-element.19), channel_id=1, source_target_pairs={{0,1},{1,0},{2,3},{3,2},{4,5},{5,4},{6,7},{7,6},{8,9},{9,8},{10,11... | collective-permute-start | bytes 393224 | tf_op jit(solution)/shard_map/ppermute | solution.py:45
  6.0 12.9 %collective-permute-start.1 = (bf16[32,4,512]{2,1,0:T(4,128)(2,1)S(1)}, bf16[32,4,512]{2,1,0:T(4,128)(2,1)S(1)}, u32[]{:S(2)}, u32[]{:S(2)}) collective-permute-start(bf16[32,4,512]{2,1,0:T(4,128)(2,1)S(1)} %get-tuple-element.20), channel_id=1, source_target_pairs={{0,7},{1,2},{2,1},{3,4},{4,3},{5,6},{6,5},{7,0},{8,15},{9,10},{10,... | collective-permute-start | bytes 393224 | tf_op jit(solution)/shard_map/ppermute | solution.py:46
  9.6 9.4 %collective-permute-start.2 = (bf16[4,32,512]{2,1,0:T(8,128)(2,1)S(1)}, bf16[4,32,512]{2,1,0:T(8,128)(2,1)S(1)}, u32[]{:S(2)}, u32[]{:S(2)}) collective-permute-start(bf16[4,32,512]{2,1,0:T(8,128)(2,1)S(1)} %get-tuple-element.21), channel_id=1, source_target_pairs={{0,8},{8,0},{16,24},{24,16},{32,40},{40,32},{48,56},{56,48},{1,9},... | collective-permute-start | bytes 393224 | tf_op jit(solution)/shard_map/ppermute | solution.py:43
  10.8 8.2 %collective-permute-start.3 = (bf16[4,32,512]{2,1,0:T(8,128)(2,1)S(1)}, bf16[4,32,512]{2,1,0:T(8,128)(2,1)S(1)}, u32[]{:S(2)}, u32[]{:S(2)}) collective-permute-start(bf16[4,32,512]{2,1,0:T(8,128)(2,1)S(1)} %get-tuple-element.22), channel_id=1, source_target_pairs={{0,56},{8,16},{16,8},{24,32},{32,24},{40,48},{48,40},{56,0},{1,57}... | collective-permute-start | bytes 393224 | tf_op jit(solution)/shard_map/ppermute | solution.py:44
  18.9 4.8 %copy-start.9 = (s32[1,1,1,512]{3,2,1,0:T(1,128)S(1)}, s32[1,1,1,512]{3,2,1,0:T(1,128)}, u32[]{:S(2)}) copy-start(s32[1,1,1,512]{3,2,1,0:T(1,128)} %param.16) | copy-start | bytes 6148
  18.9 4.8 %copy-start.1 = (f32[1,2,32,32,512]{4,3,2,1,0:T(8,128)S(1)}, f32[1,2,32,32,512]{4,3,2,1,0:T(8,128)}, u32[]{:S(2)}) copy-start(f32[1,2,32,32,512]{4,3,2,1,0:T(8,128)} %forward_ref.3) | copy-start | bytes 12582916
  19.9 9.4 %collective-permute-start.4 = (bf16[32,4,512]{2,1,0:T(4,128)(2,1)S(1)}, bf16[32,4,512]{2,1,0:T(4,128)(2,1)S(1)}, u32[]{:S(2)}, u32[]{:S(2)}) collective-permute-start(bf16[32,4,512]{2,1,0:T(4,128)(2,1)S(1)} %get-tuple-element.29), channel_id=1, source_target_pairs={{0,1},{1,0},{2,3},{3,2},{4,5},{5,4},{6,7},{7,6},{8,9},{9,8},{10,11... | collective-permute-start | bytes 393224 | tf_op jit(solution)/shard_map/ppermute | solution.py:45
  20.5 8.8 %collective-permute-start.5 = (bf16[32,4,512]{2,1,0:T(4,128)(2,1)S(1)}, bf16[32,4,512]{2,1,0:T(4,128)(2,1)S(1)}, u32[]{:S(2)}, u32[]{:S(2)}) collective-permute-start(bf16[32,4,512]{2,1,0:T(4,128)(2,1)S(1)} %get-tuple-element.30), channel_id=1, source_target_pairs={{0,7},{1,2},{2,1},{3,4},{4,3},{5,6},{6,5},{7,0},{8,15},{9,10},{10,... | collective-permute-start | bytes 393224 | tf_op jit(solution)/shard_map/ppermute | solution.py:46
  22.8 6.5 %collective-permute-start.6 = (bf16[4,32,512]{2,1,0:T(8,128)(2,1)S(1)}, bf16[4,32,512]{2,1,0:T(8,128)(2,1)S(1)}, u32[]{:S(2)}, u32[]{:S(2)}) collective-permute-start(bf16[4,32,512]{2,1,0:T(8,128)(2,1)S(1)} %get-tuple-element.31), channel_id=1, source_target_pairs={{0,8},{8,0},{16,24},{24,16},{32,40},{40,32},{48,56},{56,48},{1,9},... | collective-permute-start | bytes 393224 | tf_op jit(solution)/shard_map/ppermute | solution.py:43
  22.8 6.5 %collective-permute-start.7 = (bf16[4,32,512]{2,1,0:T(8,128)(2,1)S(1)}, bf16[4,32,512]{2,1,0:T(8,128)(2,1)S(1)}, u32[]{:S(2)}, u32[]{:S(2)}) collective-permute-start(bf16[4,32,512]{2,1,0:T(8,128)(2,1)S(1)} %get-tuple-element.32), channel_id=1, source_target_pairs={{0,56},{8,16},{16,8},{24,32},{32,24},{40,48},{48,40},{56,0},{1,57}... | collective-permute-start | bytes 393224 | tf_op jit(solution)/shard_map/ppermute | solution.py:44

commit v7 on v6

--- a/solution.py
+++ b/solution.py
@@ -258,7 +258,7 @@
         y_sides(ry1, ry0)
 
 
-def first_edge_kernel(part_ref, speed_ref, ry0, ry1, rx0, rx1, one_ref, sx0, sx1, sy0, sy1):
+def first_edge_kernel(part_ref, speed_ref, ry0, ry1, rx1, rx0, one_ref, sx0, sx1, sy0, sy1):
     del part_ref
     gx = lax.axis_index("gx")
     gy = lax.axis_index("gy")
@@ -290,7 +290,7 @@
 
 
 def second_edge_kernel(
-    at_ref, part_ref, image_in, begun_ref, speed_ref, forward_ref, ry0, ry1, rx0, rx1,
+    at_ref, part_ref, image_in, begun_ref, speed_ref, forward_ref, ry0, ry1, rx1, rx0,
     two_ref, image_ref, out_ref, done_hbm, sem,
 ):
     del part_ref, image_in, begun_ref
@@ -421,7 +421,7 @@
         input_output_aliases={0: 0},
         compiler_params=params(4),
         name="level_one_edge",
-    )(part_one, speed, *[near(faces[i]) for i in (2, 3, 0, 1)])
+    )(part_one, speed, *[near(faces[i]) for i in (2, 3, 1, 0)])
     faces = swap_faces(*send)
     level_one, part_two, image, outgoing, at = pl.pallas_call(
         second_kernel,
@@ -445,7 +445,7 @@
         input_output_aliases={1: 0, 2: 1, 3: 2},
         compiler_params=params(4),
         name="level_two_edge",
-    )(at, part_two, image, outgoing, speed, forward, *[near(faces[i]) for i in (2, 3, 0, 1)])
+    )(at, part_two, image, outgoing, speed, forward, *[near(faces[i]) for i in (2, 3, 1, 0)])
     incoming = lax.all_to_all(outgoing, ("shot", "gx", "gy"), split_axis=0, concat_axis=0, tiled=True)
     gradient = pl.pallas_call(
         owner_kernel,

time: 63.1 us -> 64.5 us (1.022)
  blocking collectives: 29.3 us -> 30.6 us
    ppermute x2, starting transfers between devices: 3.71 us -> 5.03 us  [swap_faces(): lax.ppermute(x1, 'gx', SWAP_B)]
    all_to_all x1, blocking collectives: 29.3 us -> 30.6 us  [per_device(): lax.all_to_all(outgoing, ('shot', 'gx', 'gy'), split_axis=0, concat_axis=...]
    ppermute x2, starting transfers between devices: 1.22 us -> 0.01 us  [swap_faces(): lax.ppermute(x0, 'gx', SWAP_A)]
where the time goes in v7:
time: 64.5 us; the launch traced here: 64.4 us
  blocking collectives  30.6 us (47%)
  Pallas kernels  16.9 us (26%)
  starting transfers between devices  15.3 us (24%)
  between operations  1.54 us (2%)
    all_to_all x1, blocking collectives, per_device(): lax.all_to_all(outgoing, ('shot', 'gx', 'gy'), split_axis=0, concat_axis=...  30.6 us
    ppermute x2, starting transfers between devices, swap_faces(): lax.ppermute(y1, 'gy', SWAP_B)  5.88 us
    pallas_call x1, Pallas kernels, per_device(): pl.pallas_call(second_kernel, in_specs=[VMEM] * 10, out_specs=[HBM, VMEM,...  5.52 us
    ppermute x2, starting transfers between devices, swap_faces(): lax.ppermute(x1, 'gx', SWAP_B)  5.03 us
    pallas_call x1, Pallas kernels, per_device(): pl.pallas_call(first_kernel, in_specs=[VMEM] * 8, out_specs=VMEM, out_sha...  4.59 us
    ppermute x2, starting transfers between devices, swap_faces(): lax.ppermute(y0, 'gy', SWAP_A)  4.4 us
    pallas_call x1, Pallas kernels, per_device(): pl.pallas_call(second_edge_kernel, in_specs=[SMEM] + [VMEM] * 9, out_spec...  2.28 us
    pallas_call x1, Pallas kernels, per_device(): pl.pallas_call(owner_kernel, in_specs=[VMEM], out_specs=VMEM, out_shape=j...  2.12 us
  transfers between devices with their start and end apart: 8, of which 0 were waited for; matrix products, arithmetic and copies ran while one was open for 0% of the time, Pallas kernels for 16%

profile of v7, /device:TPU:1, one launch (start us, length us, event | category | flops | bytes accessed | tf_op | source)
XLA Modules:
  0.0 64.4 jit_solution(13435925568462952647)
XLA Ops:
  0.6 0.0 copy-start.5
  0.6 0.0 copy-start.6
  0.7 0.0 copy-start.7
  0.7 0.0 copy-start.8
  0.7 0.0 copy-start.3
  0.7 0.0 copy-start
  0.7 0.0 copy-start.4
  0.7 1.5 %faces.1 = (bf16[4,32,512]{2,1,0:T(8,128)(2,1)S(1)}, bf16[4,32,512]{2,1,0:T(8,128)(2,1)S(1)}, bf16[32,4,512]{2,1,0:T(4,128)(2,1)S(1)}, bf16[32,4,512]{2,1,0:T(4,128)(2,1)S(1)}) custom-call(f32[1,32,32,512]{3,2,1,0:T(8,128)} %now_ref.3), custom_call_target="tpu_custom_call" | custom-call | flops 10000000000 | bytes 1000000 | tf_op jit(solution)/shard_map/faces/pallas_call | solution.py:388
  2.2 3.8 %collective-permute-start = (bf16[32,4,512]{2,1,0:T(4,128)(2,1)S(1)}, bf16[32,4,512]{2,1,0:T(4,128)(2,1)S(1)}, u32[]{:S(2)}, u32[]{:S(2)}) collective-permute-start(bf16[32,4,512]{2,1,0:T(4,128)(2,1)S(1)} %get-tuple-element.19), channel_id=1, source_target_pairs={{0,1},{1,0},{2,3},{3,2},{4,5},{5,4},{6,7},{7,6},{8,9},{9,8},{10,11... | collective-permute-start | bytes 393224 | tf_op jit(solution)/shard_map/ppermute | solution.py:45
  6.0 3.6 %collective-permute-start.1 = (bf16[32,4,512]{2,1,0:T(4,128)(2,1)S(1)}, bf16[32,4,512]{2,1,0:T(4,128)(2,1)S(1)}, u32[]{:S(2)}, u32[]{:S(2)}) collective-permute-start(bf16[32,4,512]{2,1,0:T(4,128)(2,1)S(1)} %get-tuple-element.20), channel_id=1, source_target_pairs={{0,7},{1,2},{2,1},{3,4},{4,3},{5,6},{6,5},{7,0},{8,15},{9,10},{10,... | collective-permute-start | bytes 393224 | tf_op jit(solution)/shard_map/ppermute | solution.py:46
  9.6 3.5 %collective-permute-start.2 = (bf16[4,32,512]{2,1,0:T(8,128)(2,1)S(1)}, bf16[4,32,512]{2,1,0:T(8,128)(2,1)S(1)}, u32[]{:S(2)}, u32[]{:S(2)}) collective-permute-start(bf16[4,32,512]{2,1,0:T(8,128)(2,1)S(1)} %get-tuple-element.21), channel_id=1, source_target_pairs={{0,56},{8,16},{16,8},{24,32},{32,24},{40,48},{48,40},{56,0},{1,57}... | collective-permute-start | bytes 393224 | tf_op jit(solution)/shard_map/ppermute | solution.py:44
  13.1 0.0 collective-permute-start.3
  13.8 4.6 %level_one.1.part_ref = f32[1,32,32,512]{3,2,1,0:T(8,128)S(1)} custom-call(f32[1,32,32,512]{3,2,1,0:T(8,128)S(1)} %copy-done.3, f32[1,32,32,512]{3,2,1,0:T(8,128)S(1)} %copy-done.4, f32[1,2,32,32,512]{4,3,2,1,0:T(8,128)S(1)} %copy-done.2, f32[1,32,32,512]{3,2,1,0:T(8,128)S(1)} %copy-done, bf16[512,512]{1,0:T(8,128)(2,1)S(1)} %copy-done.6, ...), custom_call_target="tpu_custom_call" | custom-call | tf_op jit(solution)/shard_map/level_one/pallas_call | solution.py:407
  18.4 0.0 copy-start.9
  18.4 0.0 copy-start.1
  18.4 0.0 collective-permute-done.ry0
  18.4 0.0 collective-permute-done.1.ry1
  18.4 0.0 collective-permute-done.2.rx1
  18.4 0.0 collective-permute-done.3.rx0
  18.5 0.9 %level_one_edge.1 = (f32[1,32,32,512]{3,2,1,0:T(8,128)S(1)}, bf16[4,32,512]{2,1,0:T(8,128)(2,1)S(1)}, bf16[4,32,512]{2,1,0:T(8,128)(2,1)S(1)}, bf16[32,4,512]{2,1,0:T(4,128)(2,1)S(1)}, bf16[32,4,512]{2,1,0:T(4,128)(2,1)S(1)}) custom-call(f32[1,32,32,512]{3,2,1,0:T(8,128)S(1)} %level_one.1.part_ref, ...), custom_call_target="tpu_custom_call", output_to_operand_aliasing={{0}: (0, {})} | custom-call | tf_op jit(solution)/shard_map/level_one_edge/pallas_call | solution.py:416
  19.3 0.6 collective-permute-start.4
  19.9 2.3 %collective-permute-start.5 = (bf16[32,4,512]{2,1,0:T(4,128)(2,1)S(1)}, bf16[32,4,512]{2,1,0:T(4,128)(2,1)S(1)}, u32[]{:S(2)}, u32[]{:S(2)}) collective-permute-start(bf16[32,4,512]{2,1,0:T(4,128)(2,1)S(1)} %get-tuple-element.30), channel_id=1, source_target_pairs={{0,7},{1,2},{2,1},{3,4},{4,3},{5,6},{6,5},{7,0},{8,15},{9,10},{10,... | collective-permute-start | bytes 393224 | tf_op jit(solution)/shard_map/ppermute | solution.py:46
  22.2 1.6 %collective-permute-start.6 = (bf16[4,32,512]{2,1,0:T(8,128)(2,1)S(1)}, bf16[4,32,512]{2,1,0:T(8,128)(2,1)S(1)}, u32[]{:S(2)}, u32[]{:S(2)}) collective-permute-start(bf16[4,32,512]{2,1,0:T(8,128)(2,1)S(1)} %get-tuple-element.31), channel_id=1, source_target_pairs={{0,56},{8,16},{16,8},{24,32},{32,24},{40,48},{48,40},{56,0},{1,57}... | collective-permute-start | bytes 393224 | tf_op jit(solution)/shard_map/ppermute | solution.py:44
  23.8 0.0 collective-permute-start.7
  23.8 5.5 %level_two.1 = (f32[1,32,32,512]{3,2,1,0:T(8,128)}, f32[1,32,32,512]{3,2,1,0:T(8,128)S(1)}, f32[1,32,32,512]{3,2,1,0:T(8,128)S(1)}, bf16[1152,4,128]{2,1,0:T(4,128)(2,1)S(1)}, s32[1,512]{1,0:T(1,128)S(4)}) custom-call(s32[1,512]{1,0:T(1,128)S(1)} %fusion.foot_ref, f32[1,32,32,512]{3,2,1,0:T(8,128)S(1)} %get-tuple-element.23.one_ref, ...), custom_call_target="tpu_custom_call" | custom-call | tf_op jit(solution)/shard_map/level_two/pallas_call | solution.py:426
  29.4 0.0 collective-permute-done.4.ry0
  29.4 0.0 collective-permute-done.5.ry1
  29.4 0.0 collective-permute-done.6.rx1
  29.4 0.0 collective-permute-done.7.rx0
  29.4 2.3 %level_two_edge.1 = (f32[1,32,32,512]{3,2,1,0:T(8,128)S(1)}, f32[1,32,32,512]{3,2,1,0:T(8,128)S(1)}, bf16[1152,4,128]{2,1,0:T(4,128)(2,1)S(1)}, f32[1,32,32,512]{3,2,1,0:T(8,128)}) custom-call(s32[1,512]{1,0:T(1,128)S(4)} %get-tuple-element.25.at_ref, ...), custom_call_target="tpu_custom_call", output_to_operand_aliasing={{0}: (1, {}), {1}: (2, {}), {2}: (3, {})} | custom-call | tf_op jit(solution)/shard_map/level_two_edge/pallas_call | solution.py:439
  31.7 30.6 %all_to_all.5 = bf16[1152,4,128]{2,1,0:T(4,128)(2,1)S(1)} all-to-all(bf16[1152,4,128]{2,1,0:T(4,128)(2,1)S(1)} %get-tuple-element.34), channel_id=1, replica_groups=mesh['shot'=2,'gx'=8,'gy'=8] {'shot','gx','gy'}, dimensions={0} | all-to-all | bytes 2359296 | tf_op jit(solution)/shard_map/all_to_all | solution.py:449
  62.3 2.1 %owner_sum.1 = f32[128,1024]{1,0:T(8,128)} custom-call(bf16[576,8,128]{2,1,0:T(8,128)(2,1)S(1)} %bitcast.5), custom_call_target="tpu_custom_call" | custom-call | tf_op jit(solution)/shard_map/owner_sum/pallas_call | solution.py:450
  (12 shorter events, 0.0 us)
Async XLA Ops:
  0.6 13.1 %copy-start.5 = (bf16[512,512]{1,0:T(8,128)(2,1)S(1)}, bf16[512,512]{1,0:T(8,128)(2,1)}, u32[]{:S(2)}) copy-start(bf16[512,512]{1,0:T(8,128)(2,1)} %constant.11.clone.low) | copy-start | bytes 1572868
  0.6 13.1 %copy-start.6 = (bf16[512,512]{1,0:T(8,128)(2,1)S(1)}, bf16[512,512]{1,0:T(8,128)(2,1)}, u32[]{:S(2)}) copy-start(bf16[512,512]{1,0:T(8,128)(2,1)} %constant.10.clone.high) | copy-start | bytes 1572868
  0.7 13.1 %copy-start.7 = (bf16[256,256]{1,0:T(8,128)(2,1)S(1)}, bf16[256,256]{1,0:T(8,128)(2,1)}, u32[]{:S(2)}) copy-start(bf16[256,256]{1,0:T(8,128)(2,1)} %constant.13.clone.row_low) | copy-start | bytes 393220
  0.7 13.1 %copy-start.8 = (bf16[256,256]{1,0:T(8,128)(2,1)S(1)}, bf16[256,256]{1,0:T(8,128)(2,1)}, u32[]{:S(2)}) copy-start(bf16[256,256]{1,0:T(8,128)(2,1)} %constant.12.clone.row_high) | copy-start | bytes 393220
  0.7 13.1 %copy-start.3 = (f32[1,32,32,512]{3,2,1,0:T(8,128)S(1)}, f32[1,32,32,512]{3,2,1,0:T(8,128)}, u32[]{:S(2)}) copy-start(f32[1,32,32,512]{3,2,1,0:T(8,128)} %now_ref.3) | copy-start | bytes 6291460
  0.7 13.1 %copy-start = (f32[1,32,32,512]{3,2,1,0:T(8,128)S(1)}, f32[1,32,32,512]{3,2,1,0:T(8,128)}, u32[]{:S(2)}) copy-start(f32[1,32,32,512]{3,2,1,0:T(8,128)} %speed_ref.7) | copy-start | bytes 6291460
  0.7 13.1 %copy-start.4 = (f32[1,32,32,512]{3,2,1,0:T(8,128)S(1)}, f32[1,32,32,512]{3,2,1,0:T(8,128)}, u32[]{:S(2)}) copy-start(f32[1,32,32,512]{3,2,1,0:T(8,128)} %prev_ref.1) | copy-start | bytes 6291460
  0.7 13.1 %copy-start.2 = (f32[1,2,32,32,512]{4,3,2,1,0:T(8,128)S(1)}, f32[1,2,32,32,512]{4,3,2,1,0:T(8,128)}, u32[]{:S(2)}) copy-start(f32[1,2,32,32,512]{4,3,2,1,0:T(8,128)} %source_ref.3) | copy-start | bytes 12582916
  2.2 16.2 %collective-permute-start = (bf16[32,4,512]{2,1,0:T(4,128)(2,1)S(1)}, bf16[32,4,512]{2,1,0:T(4,128)(2,1)S(1)}, u32[]{:S(2)}, u32[]{:S(2)}) collective-permute-start(bf16[32,4,512]{2,1,0:T(4,128)(2,1)S(1)} %get-tuple-element.19), channel_id=1, source_target_pairs={{0,1},{1,0},{2,3},{3,2},{4,5},{5,4},{6,7},{7,6},{8,9},{9,8},{10,11... | collective-permute-start | bytes 393224 | tf_op jit(solution)/shard_map/ppermute | solution.py:45
  6.0 12.4 %collective-permute-start.1 = (bf16[32,4,512]{2,1,0:T(4,128)(2,1)S(1)}, bf16[32,4,512]{2,1,0:T(4,128)(2,1)S(1)}, u32[]{:S(2)}, u32[]{:S(2)}) collective-permute-start(bf16[32,4,512]{2,1,0:T(4,128)(2,1)S(1)} %get-tuple-element.20), channel_id=1, source_target_pairs={{0,7},{1,2},{2,1},{3,4},{4,3},{5,6},{6,5},{7,0},{8,15},{9,10},{10,... | collective-permute-start | bytes 393224 | tf_op jit(solution)/shard_map/ppermute | solution.py:46
  9.6 8.8 %collective-permute-start.2 = (bf16[4,32,512]{2,1,0:T(8,128)(2,1)S(1)}, bf16[4,32,512]{2,1,0:T(8,128)(2,1)S(1)}, u32[]{:S(2)}, u32[]{:S(2)}) collective-permute-start(bf16[4,32,512]{2,1,0:T(8,128)(2,1)S(1)} %get-tuple-element.21), channel_id=1, source_target_pairs={{0,56},{8,16},{16,8},{24,32},{32,24},{40,48},{48,40},{56,0},{1,57}... | collective-permute-start | bytes 393224 | tf_op jit(solution)/shard_map/ppermute | solution.py:44
  13.1 5.4 %collective-permute-start.3 = (bf16[4,32,512]{2,1,0:T(8,128)(2,1)S(1)}, bf16[4,32,512]{2,1,0:T(8,128)(2,1)S(1)}, u32[]{:S(2)}, u32[]{:S(2)}) collective-permute-start(bf16[4,32,512]{2,1,0:T(8,128)(2,1)S(1)} %get-tuple-element.22), channel_id=1, source_target_pairs={{0,8},{8,0},{16,24},{24,16},{32,40},{40,32},{48,56},{56,48},{1,9},... | collective-permute-start | bytes 393224 | tf_op jit(solution)/shard_map/ppermute | solution.py:43
  18.4 5.4 %copy-start.9 = (s32[1,1,1,512]{3,2,1,0:T(1,128)S(1)}, s32[1,1,1,512]{3,2,1,0:T(1,128)}, u32[]{:S(2)}) copy-start(s32[1,1,1,512]{3,2,1,0:T(1,128)} %param.16) | copy-start | bytes 6148
  18.4 5.4 %copy-start.1 = (f32[1,2,32,32,512]{4,3,2,1,0:T(8,128)S(1)}, f32[1,2,32,32,512]{4,3,2,1,0:T(8,128)}, u32[]{:S(2)}) copy-start(f32[1,2,32,32,512]{4,3,2,1,0:T(8,128)} %forward_ref.3) | copy-start | bytes 12582916
  19.3 10.0 %collective-permute-start.4 = (bf16[32,4,512]{2,1,0:T(4,128)(2,1)S(1)}, bf16[32,4,512]{2,1,0:T(4,128)(2,1)S(1)}, u32[]{:S(2)}, u32[]{:S(2)}) collective-permute-start(bf16[32,4,512]{2,1,0:T(4,128)(2,1)S(1)} %get-tuple-element.29), channel_id=1, source_target_pairs={{0,1},{1,0},{2,3},{3,2},{4,5},{5,4},{6,7},{7,6},{8,9},{9,8},{10,11... | collective-permute-start | bytes 393224 | tf_op jit(solution)/shard_map/ppermute | solution.py:45
  19.9 9.5 %collective-permute-start.5 = (bf16[32,4,512]{2,1,0:T(4,128)(2,1)S(1)}, bf16[32,4,512]{2,1,0:T(4,128)(2,1)S(1)}, u32[]{:S(2)}, u32[]{:S(2)}) collective-permute-start(bf16[32,4,512]{2,1,0:T(4,128)(2,1)S(1)} %get-tuple-element.30), channel_id=1, source_target_pairs={{0,7},{1,2},{2,1},{3,4},{4,3},{5,6},{6,5},{7,0},{8,15},{9,10},{10,... | collective-permute-start | bytes 393224 | tf_op jit(solution)/shard_map/ppermute | solution.py:46
  22.2 7.2 %collective-permute-start.6 = (bf16[4,32,512]{2,1,0:T(8,128)(2,1)S(1)}, bf16[4,32,512]{2,1,0:T(8,128)(2,1)S(1)}, u32[]{:S(2)}, u32[]{:S(2)}) collective-permute-start(bf16[4,32,512]{2,1,0:T(8,128)(2,1)S(1)} %get-tuple-element.31), channel_id=1, source_target_pairs={{0,56},{8,16},{16,8},{24,32},{32,24},{40,48},{48,40},{56,0},{1,57}... | collective-permute-start | bytes 393224 | tf_op jit(solution)/shard_map/ppermute | solution.py:44
  23.8 5.6 %collective-permute-start.7 = (bf16[4,32,512]{2,1,0:T(8,128)(2,1)S(1)}, bf16[4,32,512]{2,1,0:T(8,128)(2,1)S(1)}, u32[]{:S(2)}, u32[]{:S(2)}) collective-permute-start(bf16[4,32,512]{2,1,0:T(8,128)(2,1)S(1)} %get-tuple-element.32), channel_id=1, source_target_pairs={{0,8},{8,0},{16,24},{24,16},{32,40},{40,32},{48,56},{56,48},{1,9},... | collective-permute-start | bytes 393224 | tf_op jit(solution)/shard_map/ppermute | solution.py:43
